TPU v7x, 128 devices: a whole 4x4x4 slice. The times are simulated.
128 devices in a mesh: ctx: 32 (over x, y_hi, z), head: 4 (over y_lo, core).
Axes of the slice: x: 4, y: 4 (y_hi: 2, y_lo: 2; y = y_hi * 2 + y_lo), z: 4, core: 2. Of those that a mesh axis runs over, the one named last changes fastest.
Arguments:
- queries: bfloat16 [4096, 4096], P('ctx', 'head'), may hold values from -6 to 6
- keys_new: bfloat16 [4096, 1024], P('ctx', 'head'), may hold values from -6 to 6
- values_new: bfloat16 [4096, 1024], P('ctx', 'head'), may hold values from -6 to 6
- cache_keys: bfloat16 [32768, 1024], P('ctx', 'head'), may hold values from -6 to 6
- cache_values: bfloat16 [32768, 1024], P('ctx', 'head'), may hold values from -6 to 6
- block_list: int32 [8, 32, 64], P('head', 'ctx'), may hold values from -1 to 255, as said below
- block_count: int32 [8, 32], P('head', 'ctx'), may hold values from 0 to 64
- out_weight: bfloat16 [4096, 4096], P('head'), may hold values from -0.21875 to 0.21875
Outputs:
- mixed: bfloat16 [4096, 4096], P(('ctx', 'head'))
Inputs may be any that keep to these rules, and one draw needn't show every extreme that they name: `block_list`: row (h, q) holds distinct cache block numbers in increasing order in its first block_count[h, q] entries and -1 after them. For each KV head, the query blocks of one aligned run of 1 query block together list at most 2 blocks of each aligned run of 8 cache blocks and at least one; for every KV head some run lists exactly 2 of every run of cache blocks.
All inputs are finite; a program needn't handle non-finite values.
Results may differ from a plain program's by a relative error of at most 0.015.
Values may be sent and summed in bfloat16 or wider, within the bound.
No kernel may reach another device: no remote copies, remote signals or barrier semaphores. Data moves between devices by JAX's collectives and lax.ppermute only.
A program may use at most 192 MiB of HBM per device.

v0:
```python
import jax
import jax.numpy as jnp
from jax import lax
from jax.sharding import PartitionSpec as P

HD = 128
BLOCK = 128
CAP = 2
CB_DEV = 8


def passed_along(shard, axis, by):
    devices = lax.axis_size(axis)
    pairs = [(i, i + by) for i in range(devices) if 0 <= i + by < devices]
    return lax.ppermute(shard, axis, pairs)


def wanted(block_rows, counts, block_ids):
    in_use = jnp.arange(block_rows.shape[2])[None, None, :] < counts[:, :, None]
    matches = (block_rows[:, :, :, None] == block_ids[None, None, None, :]) & in_use[:, :, :, None]
    return jnp.any(matches, axis=2)


def slot_table(union_mask):
    position = jnp.cumsum(union_mask.astype(jnp.int32), axis=-1) - 1
    return union_mask[:, :, None, :] & (
        position[:, :, None, :] == jnp.arange(CAP)[None, None, :, None]
    )


def shards(
    queries, keys_new, values_new, cache_keys, cache_values, block_list, block_count, out_weight
):
    n_ctx = lax.axis_size("ctx")
    my_index = lax.axis_index("ctx")
    kv_local = keys_new.shape[1] // HD
    group_size = queries.shape[1] // keys_new.shape[1]
    row_count = queries.shape[0]
    qb_dev = row_count // BLOCK
    nblocks = n_ctx * CB_DEV
    slot_count = n_ctx * CAP
    per_query = wanted(block_list, block_count, jnp.arange(nblocks, dtype=jnp.int32))
    union_mask = jnp.any(per_query, axis=1).reshape(kv_local, n_ctx, CB_DEV)
    picker = slot_table(union_mask)
    per_owner = per_query.reshape(kv_local, qb_dev, n_ctx, CB_DEV)
    listed = jnp.any(picker[:, None] & per_owner[:, :, :, None, :], axis=-1).reshape(
        kv_local, qb_dev, slot_count
    )
    same_owner = jnp.arange(n_ctx)[:, None] == jnp.arange(n_ctx)[None, :]
    pick_global = (
        (picker[:, :, :, None, :] & same_owner[None, :, None, :, None])
        .reshape(kv_local, slot_count, nblocks)
        .astype(jnp.bfloat16)
    )
    pieces = (
        lax.all_gather(cache_keys, "ctx", axis=0, tiled=True),
        lax.all_gather(cache_values, "ctx", axis=0, tiled=True),
    )
    piece_blocks = pieces[0].shape[0] // BLOCK
    piece_keys = pieces[0].reshape(piece_blocks, BLOCK, kv_local, HD)
    piece_values = pieces[1].reshape(piece_blocks, BLOCK, kv_local, HD)
    keys_part = jnp.einsum(
        "hsb,bthd->hstd", pick_global, piece_keys, preferred_element_type=jnp.float32
    ).astype(jnp.bfloat16)
    values_part = jnp.einsum(
        "hsb,bthd->hstd", pick_global, piece_values, preferred_element_type=jnp.float32
    ).astype(jnp.bfloat16)
    prev_keys, prev_values = passed_along((keys_new, values_new), "ctx", 1)
    stretch_keys = jnp.concatenate([prev_keys, keys_new], axis=0)
    stretch_values = jnp.concatenate([prev_values, values_new], axis=0)
    row_ids = jnp.arange(row_count)[:, None]
    key_ids = jnp.arange(BLOCK + row_count)[None, :] - BLOCK
    stretch_ok = (
        (key_ids <= row_ids)
        & (key_ids >= (row_ids // BLOCK - 1) * BLOCK)
        & ((my_index > 0) | (key_ids >= 0))
    )
    score_scale = HD ** (-0.5)
    head_outputs = []
    for kv_head in range(kv_local):
        cache_keyhead = keys_part[kv_head].reshape(slot_count * BLOCK, HD)
        cache_valuehead = values_part[kv_head].reshape(slot_count * BLOCK, HD)
        stretch_keyhead = stretch_keys[:, kv_head * HD : (kv_head + 1) * HD]
        stretch_valuehead = stretch_values[:, kv_head * HD : (kv_head + 1) * HD]
        block_ok = listed[kv_head]
        for member in range(group_size):
            column = (kv_head * group_size + member) * HD
            query_head = queries[:, column : column + HD]
            cache_scores = (
                jnp.einsum(
                    "rd,kd->rk", query_head, cache_keyhead, preferred_element_type=jnp.float32
                )
                * score_scale
            )
            cache_scores = jnp.where(
                block_ok[:, None, :, None],
                cache_scores.reshape(qb_dev, BLOCK, slot_count, BLOCK),
                -jnp.inf,
            ).reshape(row_count, slot_count * BLOCK)
            stretch_scores = (
                jnp.einsum(
                    "rd,kd->rk", query_head, stretch_keyhead, preferred_element_type=jnp.float32
                )
                * score_scale
            )
            stretch_scores = jnp.where(stretch_ok, stretch_scores, -jnp.inf)
            row_max = jnp.maximum(jnp.max(cache_scores, axis=1), jnp.max(stretch_scores, axis=1))[
                :, None
            ]
            cache_weights = jnp.exp(cache_scores - row_max)
            stretch_weights = jnp.exp(stretch_scores - row_max)
            weight_sum = jnp.sum(cache_weights, axis=1) + jnp.sum(stretch_weights, axis=1)
            mixture = jnp.dot(
                cache_weights.astype(jnp.bfloat16),
                cache_valuehead,
                preferred_element_type=jnp.float32,
            )
            mixture = mixture + jnp.dot(
                stretch_weights.astype(jnp.bfloat16),
                stretch_valuehead,
                preferred_element_type=jnp.float32,
            )
            head_outputs.append((mixture / weight_sum[:, None]).astype(jnp.bfloat16))
    attention = jnp.concatenate(head_outputs, axis=1)
    mixed = lax.psum_scatter(
        jnp.dot(attention, out_weight, preferred_element_type=jnp.float32).astype(jnp.bfloat16),
        "head",
        scatter_dimension=0,
        tiled=True,
    )
    return mixed


def solution(mesh):
    return jax.shard_map(
        shards,
        mesh=mesh,
        in_specs=(
            P("ctx", "head"),
            P("ctx", "head"),
            P("ctx", "head"),
            P("ctx", "head"),
            P("ctx", "head"),
            P("head", "ctx", None),
            P("head", "ctx"),
            P("head", None),
        ),
        out_specs=P(("ctx", "head"), None),
        check_vma=False,
    )
```

profile of v0, /device:TPU:16, one launch (start us, length us, event | category | flops | bytes accessed | tf_op | source)
XLA Modules:
  0.0 435.8 jit_solution(14608742840540978373)
XLA Ops:
  8.1 3.8 collective-permute-start
  11.9 3.8 collective-permute-start.1
  18.1 1.3 and.111
  26.0 139.5 %all-gather.3.cloned.1.call-done = bf16[32768,256]{1,0:T(8,128)(2,1)} async-done(((bf16[1024,256]{1,0:T(8,128)(2,1)}), bf16[32768,256]{1,0:T(8,128)(2,1)}) %all-gather.3.cloned.1.call-update) | async-done | bytes 16777232 | tf_op jit(solution)/shard_map/all_gather | solution.py:56
  165.4 24.1 %reshape.304 = bf16[256,128,2,128]{3,2,1,0:T(2,128)(2,1)} reshape(bf16[32768,256]{1,0:T(8,128)(2,1)} %all-gather.3.cloned.1.call-done) | data formatting | bytes 33554432 | tf_op jit(solution)/shard_map/reshape | solution.py:60
  189.5 25.0 %fusion.28 = bf16[2,64,128,128]{3,1,2,0:T(8,128)(2,1)S(1)} fusion(bf16[256,128,2,128]{3,2,1,0:T(2,128)(2,1)} %reshape.304, pred[2,64,256]{2,1,0:T(32,128)(4,1)S(1)} %and.111, pred[64,256]{1,0:T(8,128)(4,1)S(1)} %and.113), kind=kOutput, calls=%fused_computation.45 | convolution fusion | flops 1075871744 | bytes 21020672 | tf_op jit(solution)/shard_map/hsb,bthd->hstd/dot_general | solution.py:62
  214.5 2.3 fusion.177
  216.8 1.4 copy.22
  218.1 5.6 %fusion.180 = (f32[128]{0:T(128)S(1)}, f32[8192,128]{1,0:T(8,128)}) fusion(bf16[8192,128]{1,0:T(8,128)(2,1)S(1)} %bitcast.71, bf16[128,1024]{1,0:T(8,128)(2,1)S(1)} %copy-done.3, pred[8192]{0:T(1024)(128)(4,1)S(1)} %broadcast_bitcast_fusion.1), kind=kOutput, calls=%fused_computation.220 | convolution fusion | flops 271581056 | bytes 6332928 | tf_op jit(solution)/shard_map/rd,kd->rk/dot_general | solution.py:90
  223.7 5.6 %fusion.182 = (f32[128]{0:T(128)S(1)}, f32[8192,128]{1,0:T(8,128)}) fusion(bf16[8192,128]{1,0:T(8,128)(2,1)S(1)} %bitcast.72, bf16[128,1024]{1,0:T(8,128)(2,1)S(1)} %copy-done.3, pred[8192]{0:T(1024)(128)(4,1)S(1)} %broadcast_bitcast_fusion.1), kind=kOutput, calls=%fused_computation.222 | convolution fusion | flops 271581056 | bytes 6332928 | tf_op jit(solution)/shard_map/rd,kd->rk/dot_general | solution.py:90
  229.3 92.2 %all-gather.5.cloned.1.call-done = bf16[32768,256]{1,0:T(8,128)(2,1)} async-done(((bf16[1024,256]{1,0:T(8,128)(2,1)}), bf16[32768,256]{1,0:T(8,128)(2,1)}) %all-gather.5.cloned.1.call-update) | async-done | bytes 16777232 | tf_op jit(solution)/shard_map/all_gather | solution.py:57
  321.5 24.1 %reshape.305 = bf16[256,128,2,128]{3,2,1,0:T(2,128)(2,1)} reshape(bf16[32768,256]{1,0:T(8,128)(2,1)} %all-gather.5.cloned.1.call-done) | data formatting | bytes 33554432 | tf_op jit(solution)/shard_map/reshape | solution.py:61
  345.6 24.8 %fusion.31 = bf16[2,64,128,128]{3,1,2,0:T(8,128)(2,1)S(1)} fusion(bf16[256,128,2,128]{3,2,1,0:T(2,128)(2,1)} %reshape.305, pred[2,64,256]{2,1,0:T(32,128)(4,1)S(1)} %and.111, pred[64,256]{1,0:T(8,128)(4,1)S(1)} %and.113), kind=kOutput, calls=%fused_computation.46 | convolution fusion | flops 1075871744 | bytes 21020672 | tf_op jit(solution)/shard_map/hsb,bthd->hstd/dot_general | solution.py:65
  371.4 1.4 copy.25
  376.8 1.4 fusion.46
  386.4 1.4 copy.27
  387.7 1.3 fusion.188
  389.0 1.7 fusion.190
  390.7 1.4 copy.28
  396.6 1.3 fusion.192
  400.2 1.3 fusion.194
  401.5 1.3 fusion.34
  406.4 2.3 convolution_convert_fusion
  408.7 20.4 %reduce-scatter.2.cloned.1.call-done = bf16[32,4096]{1,0:T(8,128)(2,1)} async-done(((bf16[128,4096]{1,0:T(8,128)(2,1)}), bf16[32,4096]{1,0:T(8,128)(2,1)}) %reduce-scatter.2.cloned.1.call-update) | async-done | bytes 262160 | tf_op jit(solution)/shard_map/reduce_scatter | solution.py:125
  (110 shorter events, 33.9 us)
Async XLA Ops:
  6.5 18.2 %copy-start.3 = (bf16[128,1024]{1,0:T(8,128)(2,1)S(1)}, bf16[128,1024]{1,0:T(8,128)(2,1)}, u32[]{:S(2)}) copy-start(bf16[128,1024]{1,0:T(8,128)(2,1)} %param.8) | copy-start | bytes 786436
  6.5 158.9 %all-gather.3.cloned.1.call-start = ((), (), s32[]{:S(2)}) async-start(), calls=%async_computation.1 | async-start | bytes 17301504 | tf_op jit(solution)/shard_map/all_gather | solution.py:56
  7.3 314.2 %all-gather.5.cloned.1.call-start = ((), (), s32[]{:S(2)}) async-start(), calls=%async_computation.2 | async-start | bytes 17301504 | tf_op jit(solution)/shard_map/all_gather | solution.py:57
  8.0 421.1 %reduce-scatter.2.cloned.1.call-start = ((), (), s32[]{:S(2)}) async-start(), calls=%async_computation.3 | async-start | bytes 1310720 | tf_op jit(solution)/shard_map/reduce_scatter | solution.py:125
  8.1 12.9 %collective-permute-start = (bf16[128,256]{1,0:T(8,128)(2,1)}, bf16[128,256]{1,0:T(8,128)(2,1)S(1)}, u32[]{:S(2)}, u32[]{:S(2)}) collective-permute-start(bf16[128,256]{1,0:T(8,128)(2,1)} %param.9), channel_id=1, source_target_pairs={{0,4},{4,8},{8,12},{12,16},{16,20},{20,24},{24,28},{28,32},{32,36}... | collective-permute-start | bytes 196616 | tf_op jit(solution)/shard_map/ppermute | solution.py:15
  11.9 10.0 %collective-permute-start.1 = (bf16[128,256]{1,0:T(8,128)(2,1)}, bf16[128,256]{1,0:T(8,128)(2,1)S(1)}, u32[]{:S(2)}, u32[]{:S(2)}) collective-permute-start(bf16[128,256]{1,0:T(8,128)(2,1)} %param.10), channel_id=1, source_target_pairs={{0,4},{4,8},{8,12},{12,16},{16,20},{20,24},{24,28},{28,32},{32,36}... | collective-permute-start | bytes 196616 | tf_op jit(solution)/shard_map/ppermute | solution.py:15
  22.7 166.8 %copy-start.4 = (bf16[256,256]{1,0:T(8,128)(2,1)}, bf16[256,256]{1,0:T(8,128)(2,1)S(1)}, u32[]{:S(2)}) copy-start(bf16[256,256]{1,0:T(8,128)(2,1)S(1)} %constant_dynamic-update-slice_fusion.2) | copy-start | bytes 393220
  371.3 2.2 copy-start.1
  374.6 2.2 copy-start
  384.1 2.3 copy-start.2
  400.2 6.2 %slice-start = ((s8[8388608]{0:T(1024)(128)(4,1)}), s8[4194304]{0:T(1024)(128)(4,1)S(1)}, s32[]{:S(2)}) async-start(s8[8388608]{0:T(1024)(128)(4,1)} %bitcast.87), calls=%async_computation.4 | async-start | bytes 8388608
  401.5 5.0 %slice-start.1 = ((s8[8388608]{0:T(1024)(128)(4,1)}), s8[4194304]{0:T(1024)(128)(4,1)S(1)}, s32[]{:S(2)}) async-start(s8[8388608]{0:T(1024)(128)(4,1)} %bitcast.87), calls=%async_computation.5 | async-start | bytes 8388608
  402.8 1.7 copy-start.5
Sparse Core Ops, SparseCore 0:
  10.5 154.8 all-gather.2
  168.6 152.8 all-gather.4
  408.9 20.2 reduce-scatter.1
where the time goes:
time: 443 us; the launch traced here: 436 us
  waiting for transfers between devices  254 us (57%)
  matrix products  86 us (19%)
  local copies, waits for them, and re-layouts  63.5 us (14%)
  between operations  13.7 us (3%)
  other arithmetic  11.3 us (3%)
  starting transfers between devices  7.73 us (2%)
    all_gather x1, waiting for transfers between devices, shards(): lax.all_gather(cache_keys, 'ctx', axis=0, tiled=True)  139 us
    all_gather x1, waiting for transfers between devices, shards(): lax.all_gather(cache_values, 'ctx', axis=0, tiled=True)  92.2 us
    dot_general x1, matrix products, shards(): jnp.einsum('hsb,bthd->hstd', pick_global, piece_keys, preferred_element_t...  25 us
    dot_general x1, matrix products, shards(): jnp.einsum('hsb,bthd->hstd', pick_global, piece_values, preferred_element...  24.8 us
    reshape x1, local copies, waits for them, and re-layouts, shards(): piece_keys = pieces[0].reshape(piece_blocks, BLOCK, kv_local, HD)  24.1 us
    reshape x1, local copies, waits for them, and re-layouts, shards(): piece_values = pieces[1].reshape(piece_blocks, BLOCK, kv_local, HD)  24.1 us
    reduce_scatter x1, waiting for transfers between devices, shards(): lax.psum_scatter(jnp.dot(attention, out_weight, preferred_element_type=jn...  20.4 us
    dot_general x8, matrix products, shards(): jnp.einsum('rd,kd->rk', query_head, cache_keyhead, preferred_element_type...  19.2 us
  transfers between devices with their start and end apart: 5, of which 4 were waited for; matrix products, arithmetic and copies ran while one was open for 17% of the time, Pallas kernels for 0%

commit v1 on v0

v1 whole, which is shorter than its diff:
```python
import functools

import jax
import jax.numpy as jnp
from jax import lax
from jax.experimental import pallas as pl
from jax.experimental.pallas import tpu as pltpu
from jax.sharding import PartitionSpec as P

HD = 128
BLOCK = 128
CB_DEV = 8
KVL = 2
GROUP = 4
NX, NY, NZ = 4, 2, 4
HALVES, CORES = 2, 2
COLS = GROUP * BLOCK
ROWS = HD + 8
STEPS = (1, -1, 2)
LOG2E = 1.4426950408889634
CEXP = LOG2E * HD**-0.5
NEG = -1e30
AXES = ("ctx", "head")
BF = jnp.bfloat16
F32 = jnp.float32


def flat(x, y, z, yl, c):
    return ((x * NY + y) * NZ + z) * (HALVES * CORES) + yl * CORES + c


def everyone():
    for x in range(NX):
        for y in range(NY):
            for z in range(NZ):
                for yl in range(HALVES):
                    for c in range(CORES):
                        yield x, y, z, yl, c


def moved(x, y, z, yl, c, by, keys):
    if (c == 0) == keys:
        return flat(x, y, (z + by) % NZ, yl, c)
    return flat((x + by) % NX, y, z, yl, c)


def pairs_along(by, keys):
    return [(flat(*d), moved(*d, by, keys)) for d in everyone()]


PAIRS_Y = [(flat(x, y, z, l, c), flat(x, 1 - y, z, l, c)) for x, y, z, l, c in everyone()]
PAIRS_CORE = [(flat(x, y, z, l, c), flat(x, y, z, l, 1 - c)) for x, y, z, l, c in everyone()]
PAIRS_LO = [(flat(x, y, z, l, c), flat(x, y, z, 1 - l, c)) for x, y, z, l, c in everyone()]
PAIRS_PREV = [
    (i * HALVES * CORES + h, (i + 1) * HALVES * CORES + h)
    for i in range(NX * NY * NZ - 1)
    for h in range(HALVES * CORES)
]


def send(array, pairs):
    return lax.ppermute(array, AXES, pairs)


def nt(a, b):
    return lax.dot_general(a, b, (((1,), (1,)), ((), ())), preferred_element_type=F32)


def nn(a, b):
    return lax.dot_general(a, b, (((1,), (0,)), ((), ())), preferred_element_type=F32)


def turned(block):
    return block.astype(F32).T.astype(BF)


def packed_sum(level):
    hi = level.astype(BF)
    rest = level - hi.astype(F32)
    mid = rest.astype(BF)
    low = (rest - mid.astype(F32)).astype(BF)
    return jnp.concatenate([hi.astype(F32), mid.astype(F32), low.astype(F32), jnp.zeros((5, COLS), F32)], axis=0).astype(BF)


def pack_kernel(k_ref, v_ref, o_ref):
    for h in range(KVL):
        for b in range(CB_DEV):
            rows, cols = slice(b * BLOCK, (b + 1) * BLOCK), slice(h * HD, (h + 1) * HD)
            o_ref[h, b, 0] = k_ref[rows, cols]
            o_ref[h, b, 1] = turned(v_ref[rows, cols])


def query_rows(q):
    return jnp.concatenate([q[:, m * HD : (m + 1) * HD] for m in range(GROUP)], axis=0)


def attend_kernel(tab_ref, q_ref, *refs):
    kvs, o_ref = refs[:-1], refs[-1]
    for y in range(NY):
        for h in range(KVL):
            q = query_rows(q_ref[y, 0:BLOCK, h * COLS : (h + 1) * COLS])
            scores, offs, values = [], [], []
            for s, kv in enumerate(kvs):
                first, second = tab_ref[y, h, s, 0], tab_ref[y, h, s, 1]
                for j, b in enumerate((first, second)):
                    scores.append(nt(kv[h, b, 0], q))
                    values.append(kv[h, b, 1])
                    offs.append(None if j == 0 else jnp.where(second == first, NEG, 0.0).astype(F32))
            tops = [
                jnp.max(t, axis=0, keepdims=True) if o is None else jnp.max(t, axis=0, keepdims=True) + o
                for t, o in zip(scores, offs)
            ]
            top = functools.reduce(jnp.maximum, tops) * CEXP
            total = jnp.zeros((1, COLS), F32)
            weights = []
            for t, o in zip(scores, offs):
                w = jnp.exp2(t * CEXP - (top if o is None else top - o))
                total = total + jnp.sum(w, axis=0, keepdims=True)
                weights.append(w.astype(BF))
            mixture = nn(jnp.concatenate(values, axis=1), jnp.concatenate(weights, axis=0))
            o_ref[y, h, 0:HD, :] = (mixture * (1.0 / total)).astype(BF)
            o_ref[y, h, HD:ROWS, :] = packed_sum(top + jnp.log(total) * LOG2E)


def stretch_kernel(first_ref, q_ref, k_ref, v_ref, prev_ref, o_ref, l_ref):
    off = jnp.where(first_ref[0] == 0, NEG, 0.0).astype(F32)
    key = lax.broadcasted_iota(jnp.int32, (BLOCK, COLS), 0)
    row = lax.broadcasted_iota(jnp.int32, (BLOCK, COLS), 1) % BLOCK
    for h in range(KVL):
        q = query_rows(q_ref[:, h * COLS : (h + 1) * COLS])
        cols = slice(h * HD, (h + 1) * HD)
        vcols = slice((KVL + h) * HD, (KVL + h + 1) * HD)
        own = jnp.where(key <= row, nt(k_ref[:, cols], q), NEG)
        before = nt(prev_ref[:, cols], q)
        top = jnp.maximum(
            jnp.max(own, axis=0, keepdims=True), jnp.max(before, axis=0, keepdims=True) + off
        ) * CEXP
        w_own = jnp.exp2(own * CEXP - top)
        w_before = jnp.exp2(before * CEXP - (top - off))
        total = jnp.sum(w_own, axis=0, keepdims=True) + jnp.sum(w_before, axis=0, keepdims=True)
        mixture = nn(turned(v_ref[:, cols]), w_own.astype(BF)) + nn(
            turned(prev_ref[:, vcols]), w_before.astype(BF)
        )
        o_ref[h] = mixture * (1.0 / total)
        l_ref[h] = jnp.broadcast_to(top + jnp.log(total) * LOG2E, (8, COLS))


def level_of(rows):
    r = rows.astype(F32)
    return r[0:1] + r[1:2] + r[2:3]


def joined(mixtures, levels):
    top = functools.reduce(jnp.maximum, levels)
    shares = [jnp.exp2(v - top) for v in levels]
    total = functools.reduce(jnp.add, shares)
    inverse = 1.0 / total
    mixture = functools.reduce(jnp.add, [m * (s * inverse) for m, s in zip(mixtures, shares)])
    return mixture, top + jnp.log(total) * LOG2E


def join_kernel(which, *refs):
    parts, o_ref = refs[:-1], refs[-1]
    for h in range(KVL):
        mixture, level = joined(
            [p[which, h, 0:HD, :].astype(F32) for p in parts], [level_of(p[which, h, HD:ROWS, :]) for p in parts]
        )
        o_ref[h, 0:HD, :] = mixture.astype(BF)
        o_ref[h, HD:ROWS, :] = packed_sum(level)


def last_kernel(a_ref, b_ref, c_ref, d_ref, e_ref, s_ref, l_ref, o_ref):
    parts = (a_ref, b_ref, c_ref, d_ref)
    for h in range(KVL):
        mixtures = [p[0, h, 0:HD, :].astype(F32) for p in parts] + [e_ref[h, 0:HD, :].astype(F32), s_ref[h]]
        levels = [level_of(p[0, h, HD:ROWS, :]) for p in parts] + [level_of(e_ref[h, HD:ROWS, :]), l_ref[h, 0:1, :]]
        mixture, _ = joined(mixtures, levels)
        for m in range(GROUP):
            c = (h * GROUP + m) * HD
            o_ref[:, c : c + HD] = mixture[:, m * BLOCK : (m + 1) * BLOCK].T.astype(BF)


def call(kernel, out_shape, smem=0, n=0, name=None):
    vm = pl.BlockSpec(memory_space=pltpu.VMEM)
    sm = pl.BlockSpec(memory_space=pltpu.SMEM)
    return pl.pallas_call(
        kernel,
        out_shape=out_shape,
        in_specs=[sm] * smem + [vm] * n,
        out_specs=jax.tree.map(lambda _: vm, out_shape),
        compiler_params=pltpu.CompilerParams(vmem_limit_bytes=48 << 20),
        name=name,
    )


def shards(queries, keys_new, values_new, cache_keys, cache_values, block_list, block_count, out_weight):
    ctx, head = lax.axis_index("ctx"), lax.axis_index("head")
    x, z = ctx // (NY * NZ), ctx % NZ
    core, half = head % CORES, head // CORES

    in_use = jnp.arange(block_list.shape[2])[None, :] < block_count
    listed = jnp.where(in_use, block_list[:, 0, :], -1).astype(BF).reshape(1, -1)
    listed = jnp.pad(listed, ((0, 7), (0, queries.shape[1] - listed.shape[1])))
    asked = jnp.concatenate([queries, listed], axis=0)
    asked_pair = jnp.stack([asked, send(asked, PAIRS_Y)])

    kv = call(pack_kernel, jax.ShapeDtypeStruct((KVL, CB_DEV, 2, BLOCK, HD), BF), n=2, name="pack")(
        cache_keys, cache_values
    )
    kvs = [kv] + [send(kv, pairs_along(-d, True)) for d in STEPS]
    asked_all = [asked_pair] + [send(asked_pair, pairs_along(-d, False)) for d in STEPS]

    prev = send(jnp.concatenate([keys_new, values_new], axis=1), PAIRS_PREV)
    local, local_level = call(
        stretch_kernel,
        (
            jax.ShapeDtypeStruct((KVL, HD, COLS), F32),
            jax.ShapeDtypeStruct((KVL, 8, COLS), F32),
        ),
        smem=1,
        n=4,
        name="stretch",
    )(jnp.minimum(ctx, 1).reshape(1), queries, keys_new, values_new, prev)

    steps = jnp.array((0,) + STEPS, jnp.int32)
    owners = jnp.where(core == 0, ctx - z + (z + steps) % NZ, ctx + ((x + steps) % NX - x) * NY * NZ)
    lists = jnp.stack([a[:, BLOCK, : KVL * block_list.shape[2]] for a in asked_all]).astype(jnp.int32)
    lists = lists.reshape(len(asked_all), NY, KVL, 1, block_list.shape[2])
    inside = lists // CB_DEV == owners[:, None]
    slot = lists % CB_DEV
    table = jnp.stack(
        [jnp.min(jnp.where(inside, slot, CB_DEV), axis=-1), jnp.max(jnp.where(inside, slot, -1), axis=-1)], axis=-1
    )
    table = jnp.clip(table, 0, CB_DEV - 1)

    attend = call(
        attend_kernel, jax.ShapeDtypeStruct((NY, KVL, ROWS, COLS), BF), smem=1, n=1 + len(kvs), name="attend"
    )
    parts = []
    for i in (3, 1, 2, 0):
        part = attend(table[i], asked_all[i], *kvs)
        parts.append(part if i == 0 else send(part, pairs_along(((0,) + STEPS)[i], False)))
    other = call(
        functools.partial(join_kernel, 1), jax.ShapeDtypeStruct((KVL, ROWS, COLS), BF), n=4, name="join"
    )(*parts)
    other = send(other, PAIRS_Y)
    attention = call(last_kernel, jax.ShapeDtypeStruct((BLOCK, KVL * COLS), BF), n=7, name="last")(
        *parts, other, local, local_level
    )

    width = out_weight.shape[1]
    product = jnp.dot(attention, out_weight, preferred_element_type=F32)
    product = product.reshape(HALVES, CORES, BLOCK // (HALVES * CORES), width)
    theirs = lax.dynamic_index_in_dim(product, 1 - core, 1, keepdims=False).astype(BF)
    mine = lax.dynamic_index_in_dim(product, core, 1, keepdims=False)
    chip = mine + send(theirs, PAIRS_CORE).astype(F32)
    theirs = lax.dynamic_index_in_dim(chip, 1 - half, 0, keepdims=False).astype(BF)
    mine = lax.dynamic_index_in_dim(chip, half, 0, keepdims=False)
    return (mine + send(theirs, PAIRS_LO).astype(F32)).astype(BF)


def solution(mesh):
    return jax.shard_map(
        shards,
        mesh=mesh,
        in_specs=(
            P("ctx", "head"),
            P("ctx", "head"),
            P("ctx", "head"),
            P("ctx", "head"),
            P("ctx", "head"),
            P("head", "ctx", None),
            P("head", "ctx"),
            P("head", None),
        ),
        out_specs=P(("ctx", "head"), None),
        check_vma=False,
    )
```

time: 443 us -> 127 us (0.29); the launches traced: 436 us -> 124 us
  waiting for transfers between devices: 254 us -> 51.3 us
  matrix products: 86 us -> 4.64 us
  local copies, waits for them, and re-layouts: 63.5 us -> 8.87 us
  Pallas kernels: 0 us -> 27.4 us
  starting transfers between devices: 7.73 us -> 24 us
  between operations: 13.7 us -> 0.18 us
    all_gather x2 -> x0, waiting for transfers between devices: 232 us -> none  [the longest x1 139 us: shards(): lax.all_gather(cache_keys, 'ctx', axis=0, tiled=True)]
    dot_general x35 -> x1, matrix products: 86 us -> 4.64 us  [shards(): product = jnp.dot(attention, out_weight, preferred_element_type=F32)]
    ppermute x2 -> x14, waiting for transfers between devices: 0.1 us -> 51.3 us  [send(): return lax.ppermute(array, AXES, pairs)]
    reshape x2 -> x0, local copies, waits for them, and re-layouts: 48.1 us -> none  [the longest x1 24.1 us: shards(): piece_keys = pieces[0].reshape(piece_blocks, BLOCK, kv_local, HD)]
    pallas_call x0 -> x8, Pallas kernels: none -> 27.4 us  [the longest x4 22.8 us: shards(): part = attend(table[i], asked_all[i], *kvs)]
    reduce_scatter x1 -> x0, waiting for transfers between devices: 20.4 us -> none  [shards(): lax.psum_scatter(jnp.dot(attention, out_weight, preferred_element_type=jn...]
    ppermute x2 -> x14, starting transfers between devices: 7.66 us -> 24 us  [send(): return lax.ppermute(array, AXES, pairs)]
    reduce_sum x16 -> x0, other arithmetic: 9.29 us -> none  [the longest x8 8.83 us: shards(): jnp.sum(cache_weights, axis=1) + jnp.sum(stretch_weights, axis=1)]
  transfers between devices with their start and end apart: 5 -> 14, of which waited for: 4 -> 8; matrix products, arithmetic and copies ran while one was open for 17% -> 5% of each run, Pallas kernels for 0% -> 14%
where the time goes in v1:
time: 127 us; the launch traced here: 124 us
  waiting for transfers between devices  51.3 us (40%)
  Pallas kernels  27.4 us (22%)
  starting transfers between devices  24 us (19%)
  local copies, waits for them, and re-layouts  8.87 us (7%)
  other arithmetic  8.04 us (6%)
  matrix products  4.64 us (4%)
    ppermute x14, waiting for transfers between devices, send(): return lax.ppermute(array, AXES, pairs)  51.3 us
    ppermute x14, starting transfers between devices, send(): return lax.ppermute(array, AXES, pairs)  24 us
    pallas_call x4, Pallas kernels, shards(): part = attend(table[i], asked_all[i], *kvs)  22.8 us
    dot_general x1, matrix products, shards(): product = jnp.dot(attention, out_weight, preferred_element_type=F32)  4.64 us
    unnamed x17, local copies, waits for them, and re-layouts  4.46 us
  transfers between devices with their start and end apart: 14, of which 8 were waited for; matrix products, arithmetic and copies ran while one was open for 5% of the time, Pallas kernels for 14%

profile of v1, /device:TPU:16, one launch (start us, length us, event | category | flops | bytes accessed | tf_op | source)
XLA Modules:
  0.0 124.5 jit_solution(12950819335911136985)
XLA Ops:
  0.5 1.3 %reduce.11 = s32[2,64]{1,0:T(2,128)S(1)} reduce(s32[2,1,64]{2,1,0:T(1,128)} %param.14, s32[]{:T(128)} %broadcast.130), dimensions={1}, to_apply=%param.14.reduce_sub_computation.3 | reduce | bytes 1028 | tf_op args[5]
  4.1 9.6 %collective-permute-done = bf16[136,1024]{1,0:T(8,128)(2,1)S(1)} collective-permute-done((bf16[136,1024]{1,0:T(8,128)(2,1)S(1)}, bf16[136,1024]{1,0:T(8,128)(2,1)S(1)}, u32[]{:S(2)}, u32[]{:S(2)}) %collective-permute-start) | collective-permute-done | bytes 278560 | tf_op jit(solution)/shard_map/ppermute | solution.py:62
  14.7 2.8 %collective-permute-start.1 = (bf16[2,136,1024]{2,1,0:T(8,128)(2,1)}, bf16[2,136,1024]{2,1,0:T(8,128)(2,1)}, u32[]{:S(2)}, u32[]{:S(2)}) collective-permute-start(bf16[2,136,1024]{2,1,0:T(8,128)(2,1)} %pad_maximum_fusion.q_ref), channel_id=1, source_target_pairs={{0,96},{1,13},{2,98},{3,15},{4,100},{5,1},{6,102},{7,3},{8,104},{9... | collective-permute-start | bytes 1671176 | tf_op jit(solution)/shard_map/ppermute | solution.py:62
  17.5 2.3 %collective-permute-start.3 = (bf16[2,136,1024]{2,1,0:T(8,128)(2,1)}, bf16[2,136,1024]{2,1,0:T(8,128)(2,1)}, u32[]{:S(2)}, u32[]{:S(2)}) collective-permute-start(bf16[2,136,1024]{2,1,0:T(8,128)(2,1)} %pad_maximum_fusion.q_ref), channel_id=1, source_target_pairs={{0,64},{1,9},{2,66},{3,11},{4,68},{5,13},{6,70},{7,15},{8,72},{9,1... | collective-permute-start | bytes 1671176 | tf_op jit(solution)/shard_map/ppermute | solution.py:62
  22.1 4.1 %collective-permute-start.4 = (bf16[2,8,2,128,128]{4,3,2,1,0:T(8,128)(2,1)S(1)}, bf16[2,8,2,128,128]{4,3,2,1,0:T(8,128)(2,1)S(1)}, u32[]{:S(2)}, u32[]{:S(2)}) collective-permute-start(bf16[2,8,2,128,128]{4,3,2,1,0:T(8,128)(2,1)S(1)} %pack.1.refs_0_), channel_id=1, source_target_pairs={{0,12},{1,97},{2,14},{3,99},{4,0},{5,101},{6,2},{7,103},{8,4},{9,1... | collective-permute-start | bytes 3145736 | tf_op jit(solution)/shard_map/ppermute | solution.py:62
  27.6 4.5 %collective-permute-start.6 = (bf16[2,8,2,128,128]{4,3,2,1,0:T(8,128)(2,1)S(1)}, bf16[2,8,2,128,128]{4,3,2,1,0:T(8,128)(2,1)}, u32[]{:S(2)}, u32[]{:S(2)}) collective-permute-start(bf16[2,8,2,128,128]{4,3,2,1,0:T(8,128)(2,1)S(1)} %pack.1.refs_0_), channel_id=1, source_target_pairs={{0,8},{1,65},{2,10},{3,67},{4,12},{5,69},{6,14},{7,71},{8,0},{9,73... | collective-permute-start | bytes 3145736 | tf_op jit(solution)/shard_map/ppermute | solution.py:62
  33.7 6.8 %collective-permute-done.3.q_ref = bf16[2,136,1024]{2,1,0:T(8,128)(2,1)} collective-permute-done((bf16[2,136,1024]{2,1,0:T(8,128)(2,1)}, bf16[2,136,1024]{2,1,0:T(8,128)(2,1)}, u32[]{:S(2)}, u32[]{:S(2)}) %collective-permute-start.3) | collective-permute-done | bytes 557088 | tf_op jit(solution)/shard_map/ppermute | solution.py:62
  43.0 9.5 %collective-permute-done.4.refs_1_ = bf16[2,8,2,128,128]{4,3,2,1,0:T(8,128)(2,1)S(1)} collective-permute-done((bf16[2,8,2,128,128]{4,3,2,1,0:T(8,128)(2,1)S(1)}, bf16[2,8,2,128,128]{4,3,2,1,0:T(8,128)(2,1)S(1)}, u32[]{:S(2)}, u32[]{:S(2)}) %collective-permute-start.4) | collective-permute-done | bytes 1048608 | tf_op jit(solution)/shard_map/ppermute | solution.py:62
  52.4 3.4 %collective-permute-done.5.refs_2_ = bf16[2,8,2,128,128]{4,3,2,1,0:T(8,128)(2,1)S(1)} collective-permute-done((bf16[2,8,2,128,128]{4,3,2,1,0:T(8,128)(2,1)S(1)}, bf16[2,8,2,128,128]{4,3,2,1,0:T(8,128)(2,1)S(1)}, u32[]{:S(2)}, u32[]{:S(2)}) %collective-permute-start.5) | collective-permute-done | bytes 1048608 | tf_op jit(solution)/shard_map/ppermute | solution.py:62
  55.8 5.9 %attend.6 = bf16[2,2,136,512]{3,2,1,0:T(8,128)(2,1)} custom-call(s32[2,2,4,2]{3,2,1,0:T(4,128)S(1)} %copy.33.tab_ref, bf16[2,136,1024]{2,1,0:T(8,128)(2,1)} %collective-permute-done.2.q_ref, bf16[2,8,2,128,128]{4,3,2,1,0:T(8,128)(2,1)S(1)} %pack.1.refs_0_, bf16[2,8,2,128,128]{4,3,2,1,0:T(8,128)(2,1)S(1)} %collective-permute-done.4.refs_1_, ...), custom_call_target="tpu_custom_call" | custom-call | tf_op jit(solution)/shard_map/attend/pallas_call | solution.py:241
  61.7 2.8 %collective-permute-start.9 = (bf16[2,2,136,512]{3,2,1,0:T(8,128)(2,1)}, bf16[2,2,136,512]{3,2,1,0:T(8,128)(2,1)}, u32[]{:S(2)}, u32[]{:S(2)}) collective-permute-start(bf16[2,2,136,512]{3,2,1,0:T(8,128)(2,1)} %attend.6), channel_id=1, source_target_pairs={{0,96},{1,13},{2,98},{3,15},{4,100},{5,1},{6,102},{7,3},{8,104},{9... | collective-permute-start | bytes 1671176 | tf_op jit(solution)/shard_map/ppermute | solution.py:62
  64.6 5.9 %attend.5 = bf16[2,2,136,512]{3,2,1,0:T(8,128)(2,1)} custom-call(s32[2,2,4,2]{3,2,1,0:T(4,128)S(1)} %copy.31.tab_ref, bf16[2,136,1024]{2,1,0:T(8,128)(2,1)} %collective-permute-done.1.q_ref, bf16[2,8,2,128,128]{4,3,2,1,0:T(8,128)(2,1)S(1)} %pack.1.refs_0_, bf16[2,8,2,128,128]{4,3,2,1,0:T(8,128)(2,1)S(1)} %collective-permute-done.4.refs_1_, ...), custom_call_target="tpu_custom_call" | custom-call | tf_op jit(solution)/shard_map/attend/pallas_call | solution.py:241
  70.5 5.9 %attend.4 = bf16[2,2,136,512]{3,2,1,0:T(8,128)(2,1)} custom-call(s32[2,2,4,2]{3,2,1,0:T(4,128)S(1)} %copy.29.tab_ref, bf16[2,136,1024]{2,1,0:T(8,128)(2,1)} %collective-permute-done.3.q_ref, bf16[2,8,2,128,128]{4,3,2,1,0:T(8,128)(2,1)S(1)} %pack.1.refs_0_, bf16[2,8,2,128,128]{4,3,2,1,0:T(8,128)(2,1)S(1)} %collective-permute-done.4.refs_1_, ...), custom_call_target="tpu_custom_call" | custom-call | tf_op jit(solution)/shard_map/attend/pallas_call | solution.py:241
  76.4 2.3 %collective-permute-start.7 = (bf16[2,2,136,512]{3,2,1,0:T(8,128)(2,1)}, bf16[2,2,136,512]{3,2,1,0:T(8,128)(2,1)}, u32[]{:S(2)}, u32[]{:S(2)}) collective-permute-start(bf16[2,2,136,512]{3,2,1,0:T(8,128)(2,1)} %attend.4), channel_id=1, source_target_pairs={{0,64},{1,9},{2,66},{3,11},{4,68},{5,13},{6,70},{7,15},{8,72},{9,1... | collective-permute-start | bytes 1671176 | tf_op jit(solution)/shard_map/ppermute | solution.py:62
  79.5 5.1 %attend.7.refs_3_.d_ref = bf16[2,2,136,512]{3,2,1,0:T(8,128)(2,1)S(1)} custom-call(s32[2,2,4,2]{3,2,1,0:T(4,128)S(1)} %copy.35.tab_ref, bf16[2,136,1024]{2,1,0:T(8,128)(2,1)} %pad_maximum_fusion.q_ref, bf16[2,8,2,128,128]{4,3,2,1,0:T(8,128)(2,1)S(1)} %pack.1.refs_0_, bf16[2,8,2,128,128]{4,3,2,1,0:T(8,128)(2,1)S(1)} %collective-permute-done.4.refs_1_, ...), custom_call_target="tpu_custom_call" | custom-call | tf_op jit(solution)/shard_map/attend/pallas_call | solution.py:241
  84.6 3.2 %collective-permute-done.7.refs_0_.a_ref = bf16[2,2,136,512]{3,2,1,0:T(8,128)(2,1)} collective-permute-done((bf16[2,2,136,512]{3,2,1,0:T(8,128)(2,1)}, bf16[2,2,136,512]{3,2,1,0:T(8,128)(2,1)}, u32[]{:S(2)}, u32[]{:S(2)}) %collective-permute-start.7) | collective-permute-done | bytes 557088 | tf_op jit(solution)/shard_map/ppermute | solution.py:62
  87.7 1.7 %join.1 = bf16[2,136,512]{2,1,0:T(8,128)(2,1)S(1)} custom-call(bf16[2,2,136,512]{3,2,1,0:T(8,128)(2,1)} %collective-permute-done.7.refs_0_.a_ref, bf16[2,2,136,512]{3,2,1,0:T(8,128)(2,1)} %collective-permute-done.8.refs_1_.b_ref, bf16[2,2,136,512]{3,2,1,0:T(8,128)(2,1)} %collective-permute-done.9.refs_2_.c_ref, bf16[2,2,136,512]{3,2,1,0:T(8,128)(2,1)S(1)} %attend.7.refs_3_.d_ref), custom_call_target="tpu_custom_call" | custom-call | tf_op jit(solution)/shard_map/join/pallas_call | solution.py:243
  90.6 1.9 %collective-permute-start.11 = (bf16[128,512]{1,0:T(8,128)(2,1)S(1)}, bf16[128,512]{1,0:T(8,128)(2,1)S(1)}, u32[]{:S(2)}, u32[]{:S(2)}) collective-permute-start(bf16[128,512]{1,0:T(8,128)(2,1)S(1)} %pad_maximum_fusion.1), channel_id=1, source_target_pairs={{0,4},{1,5},{2,6},{3,7},{4,8},{5,9},{6,10},{7,11},{8,12},{9,13},{1... | collective-permute-start | bytes 393224 | tf_op jit(solution)/shard_map/ppermute | solution.py:62
  92.5 10.0 %collective-permute-done.11.prev_ref = bf16[128,512]{1,0:T(8,128)(2,1)S(1)} collective-permute-done((bf16[128,512]{1,0:T(8,128)(2,1)S(1)}, bf16[128,512]{1,0:T(8,128)(2,1)S(1)}, u32[]{:S(2)}, u32[]{:S(2)}) %collective-permute-start.11) | collective-permute-done | bytes 131104 | tf_op jit(solution)/shard_map/ppermute | solution.py:62
  104.5 1.8 %last.1 = bf16[128,1024]{1,0:T(8,128)(2,1)S(1)} custom-call(bf16[2,2,136,512]{3,2,1,0:T(8,128)(2,1)} %collective-permute-done.7.refs_0_.a_ref, bf16[2,2,136,512]{3,2,1,0:T(8,128)(2,1)} %collective-permute-done.8.refs_1_.b_ref, bf16[2,2,136,512]{3,2,1,0:T(8,128)(2,1)} %collective-permute-done.9.refs_2_.c_ref, bf16[2,2,136,512]{3,2,1,0:T(8,128)(2,1)S(1)} %copy-done.1, ...), custom_call_target="tpu_custom_call" | custom-call | tf_op jit(solution)/shard_map/last/pallas_call | solution.py:247
  106.3 4.6 %fusion.16 = f32[128,4096]{1,0:T(8,128)S(1)} fusion(bf16[128,1024]{1,0:T(8,128)(2,1)S(1)} %last.1, bf16[1024,4096]{1,0:T(8,128)(2,1)} %param.16), kind=kOutput, calls=%fused_computation.54 | convolution fusion | flops 1073741824 | bytes 10747904 | tf_op jit(solution)/shard_map/dot_general | solution.py:252
  112.2 1.7 %collective-permute-done.12 = bf16[2,32,4096]{2,1,0:T(8,128)(2,1)} collective-permute-done((bf16[2,32,4096]{2,1,0:T(8,128)(2,1)S(1)}, bf16[2,32,4096]{2,1,0:T(8,128)(2,1)}, u32[]{:S(2)}, u32[]{:S(2)}) %collective-permute-start.12) | collective-permute-done | bytes 524320 | tf_op jit(solution)/shard_map/ppermute | solution.py:62
  115.1 1.5 %collective-permute-start.13 = (bf16[32,4096]{1,0:T(8,128)(2,1)S(1)}, bf16[32,4096]{1,0:T(8,128)(2,1)S(1)}, u32[]{:S(2)}, u32[]{:S(2)}) collective-permute-start(bf16[32,4096]{1,0:T(8,128)(2,1)S(1)} %fusion.4), channel_id=1, source_target_pairs={{0,2},{1,3},{2,0},{3,1},{4,6},{5,7},{6,4},{7,5},{8,10},{9,11},{10,... | collective-permute-start | bytes 786440 | tf_op jit(solution)/shard_map/ppermute | solution.py:62
  116.6 7.1 %collective-permute-done.13 = bf16[32,4096]{1,0:T(8,128)(2,1)S(1)} collective-permute-done((bf16[32,4096]{1,0:T(8,128)(2,1)S(1)}, bf16[32,4096]{1,0:T(8,128)(2,1)S(1)}, u32[]{:S(2)}, u32[]{:S(2)}) %collective-permute-start.13) | collective-permute-done | bytes 262176 | tf_op jit(solution)/shard_map/ppermute | solution.py:62
  (60 shorter events, 18.5 us)
Async XLA Ops:
  3.8 10.0 %collective-permute-start = (bf16[136,1024]{1,0:T(8,128)(2,1)S(1)}, bf16[136,1024]{1,0:T(8,128)(2,1)S(1)}, u32[]{:S(2)}, u32[]{:S(2)}) collective-permute-start(bf16[136,1024]{1,0:T(8,128)(2,1)S(1)} %get-tuple-element.14), channel_id=1, source_target_pairs={{0,16},{1,17},{2,18},{3,19},{4,20},{5,21},{6,22},{7,23},{8,24},{9,... | collective-permute-start | bytes 835592 | tf_op jit(solution)/shard_map/ppermute | solution.py:62
  13.8 3.7 %copy-start.7 = (bf16[136,1024]{1,0:T(8,128)(2,1)}, bf16[136,1024]{1,0:T(8,128)(2,1)S(1)}, u32[]{:S(2)}) copy-start(bf16[136,1024]{1,0:T(8,128)(2,1)S(1)} %collective-permute-done) | copy-start | bytes 835588
  14.7 12.9 %collective-permute-start.1 = (bf16[2,136,1024]{2,1,0:T(8,128)(2,1)}, bf16[2,136,1024]{2,1,0:T(8,128)(2,1)}, u32[]{:S(2)}, u32[]{:S(2)}) collective-permute-start(bf16[2,136,1024]{2,1,0:T(8,128)(2,1)} %pad_maximum_fusion.q_ref), channel_id=1, source_target_pairs={{0,96},{1,13},{2,98},{3,15},{4,100},{5,1},{6,102},{7,3},{8,104},{9... | collective-permute-start | bytes 1671176 | tf_op jit(solution)/shard_map/ppermute | solution.py:62
  17.5 15.4 %collective-permute-start.2 = (bf16[2,136,1024]{2,1,0:T(8,128)(2,1)}, bf16[2,136,1024]{2,1,0:T(8,128)(2,1)}, u32[]{:S(2)}, u32[]{:S(2)}) collective-permute-start(bf16[2,136,1024]{2,1,0:T(8,128)(2,1)} %pad_maximum_fusion.q_ref), channel_id=1, source_target_pairs={{0,32},{1,5},{2,34},{3,7},{4,36},{5,9},{6,38},{7,11},{8,40},{9,13}... | collective-permute-start | bytes 1671176 | tf_op jit(solution)/shard_map/ppermute | solution.py:62
  17.5 23.0 %collective-permute-start.3 = (bf16[2,136,1024]{2,1,0:T(8,128)(2,1)}, bf16[2,136,1024]{2,1,0:T(8,128)(2,1)}, u32[]{:S(2)}, u32[]{:S(2)}) collective-permute-start(bf16[2,136,1024]{2,1,0:T(8,128)(2,1)} %pad_maximum_fusion.q_ref), channel_id=1, source_target_pairs={{0,64},{1,9},{2,66},{3,11},{4,68},{5,13},{6,70},{7,15},{8,72},{9,1... | collective-permute-start | bytes 1671176 | tf_op jit(solution)/shard_map/ppermute | solution.py:62
  19.7 1.0 copy-start.3
  20.8 1.0 copy-start.4
  22.1 30.4 %collective-permute-start.4 = (bf16[2,8,2,128,128]{4,3,2,1,0:T(8,128)(2,1)S(1)}, bf16[2,8,2,128,128]{4,3,2,1,0:T(8,128)(2,1)S(1)}, u32[]{:S(2)}, u32[]{:S(2)}) collective-permute-start(bf16[2,8,2,128,128]{4,3,2,1,0:T(8,128)(2,1)S(1)} %pack.1.refs_0_), channel_id=1, source_target_pairs={{0,12},{1,97},{2,14},{3,99},{4,0},{5,101},{6,2},{7,103},{8,4},{9,1... | collective-permute-start | bytes 3145736 | tf_op jit(solution)/shard_map/ppermute | solution.py:62
  26.2 29.7 %collective-permute-start.5 = (bf16[2,8,2,128,128]{4,3,2,1,0:T(8,128)(2,1)S(1)}, bf16[2,8,2,128,128]{4,3,2,1,0:T(8,128)(2,1)S(1)}, u32[]{:S(2)}, u32[]{:S(2)}) collective-permute-start(bf16[2,8,2,128,128]{4,3,2,1,0:T(8,128)(2,1)S(1)} %pack.1.refs_0_), channel_id=1, source_target_pairs={{0,4},{1,33},{2,6},{3,35},{4,8},{5,37},{6,10},{7,39},{8,12},{9,41}... | collective-permute-start | bytes 3145736 | tf_op jit(solution)/shard_map/ppermute | solution.py:62
  27.6 28.2 %collective-permute-start.6 = (bf16[2,8,2,128,128]{4,3,2,1,0:T(8,128)(2,1)S(1)}, bf16[2,8,2,128,128]{4,3,2,1,0:T(8,128)(2,1)}, u32[]{:S(2)}, u32[]{:S(2)}) collective-permute-start(bf16[2,8,2,128,128]{4,3,2,1,0:T(8,128)(2,1)S(1)} %pack.1.refs_0_), channel_id=1, source_target_pairs={{0,8},{1,65},{2,10},{3,67},{4,12},{5,69},{6,14},{7,71},{8,0},{9,73... | collective-permute-start | bytes 3145736 | tf_op jit(solution)/shard_map/ppermute | solution.py:62
  61.7 28.8 %copy-start.5 = (bf16[128,256]{1,0:T(8,128)(2,1)S(1)}, bf16[128,256]{1,0:T(8,128)(2,1)}, u32[]{:S(2)}) copy-start(bf16[128,256]{1,0:T(8,128)(2,1)} %k_ref.3) | copy-start | bytes 196612
  61.7 28.8 %copy-start.6 = (bf16[128,256]{1,0:T(8,128)(2,1)S(1)}, bf16[128,256]{1,0:T(8,128)(2,1)}, u32[]{:S(2)}) copy-start(bf16[128,256]{1,0:T(8,128)(2,1)} %v_ref.3) | copy-start | bytes 196612
  61.7 40.8 %copy-start.2 = (bf16[128,1024]{1,0:T(8,128)(2,1)S(1)}, bf16[128,1024]{1,0:T(8,128)(2,1)}, u32[]{:S(2)}) copy-start(bf16[128,1024]{1,0:T(8,128)(2,1)} %q_ref.1) | copy-start | bytes 786436
  61.7 22.8 %collective-permute-start.9 = (bf16[2,2,136,512]{3,2,1,0:T(8,128)(2,1)}, bf16[2,2,136,512]{3,2,1,0:T(8,128)(2,1)}, u32[]{:S(2)}, u32[]{:S(2)}) collective-permute-start(bf16[2,2,136,512]{3,2,1,0:T(8,128)(2,1)} %attend.6), channel_id=1, source_target_pairs={{0,96},{1,13},{2,98},{3,15},{4,100},{5,1},{6,102},{7,3},{8,104},{9... | collective-permute-start | bytes 1671176 | tf_op jit(solution)/shard_map/ppermute | solution.py:62
  70.5 14.1 %collective-permute-start.8 = (bf16[2,2,136,512]{3,2,1,0:T(8,128)(2,1)}, bf16[2,2,136,512]{3,2,1,0:T(8,128)(2,1)}, u32[]{:S(2)}, u32[]{:S(2)}) collective-permute-start(bf16[2,2,136,512]{3,2,1,0:T(8,128)(2,1)} %attend.5), channel_id=1, source_target_pairs={{0,32},{1,5},{2,34},{3,7},{4,36},{5,9},{6,38},{7,11},{8,40},{9,13}... | collective-permute-start | bytes 1671176 | tf_op jit(solution)/shard_map/ppermute | solution.py:62
  76.4 11.4 %collective-permute-start.7 = (bf16[2,2,136,512]{3,2,1,0:T(8,128)(2,1)}, bf16[2,2,136,512]{3,2,1,0:T(8,128)(2,1)}, u32[]{:S(2)}, u32[]{:S(2)}) collective-permute-start(bf16[2,2,136,512]{3,2,1,0:T(8,128)(2,1)} %attend.4), channel_id=1, source_target_pairs={{0,64},{1,9},{2,66},{3,11},{4,68},{5,13},{6,70},{7,15},{8,72},{9,1... | collective-permute-start | bytes 1671176 | tf_op jit(solution)/shard_map/ppermute | solution.py:62
  89.4 0.8 copy-start
  90.2 13.2 %collective-permute-start.10 = (bf16[2,136,512]{2,1,0:T(8,128)(2,1)S(1)}, bf16[2,136,512]{2,1,0:T(8,128)(2,1)S(1)}, u32[]{:S(2)}, u32[]{:S(2)}) collective-permute-start(bf16[2,136,512]{2,1,0:T(8,128)(2,1)S(1)} %join.1), channel_id=1, source_target_pairs={{0,16},{1,17},{2,18},{3,19},{4,20},{5,21},{6,22},{7,23},{8,24},{9,... | collective-permute-start | bytes 835592 | tf_op jit(solution)/shard_map/ppermute | solution.py:62
  90.6 12.0 %collective-permute-start.11 = (bf16[128,512]{1,0:T(8,128)(2,1)S(1)}, bf16[128,512]{1,0:T(8,128)(2,1)S(1)}, u32[]{:S(2)}, u32[]{:S(2)}) collective-permute-start(bf16[128,512]{1,0:T(8,128)(2,1)S(1)} %pad_maximum_fusion.1), channel_id=1, source_target_pairs={{0,4},{1,5},{2,6},{3,7},{4,8},{5,9},{6,10},{7,11},{8,12},{9,13},{1... | collective-permute-start | bytes 393224 | tf_op jit(solution)/shard_map/ppermute | solution.py:62
  103.5 1.1 copy-start.1
  111.1 2.8 %collective-permute-start.12 = (bf16[2,32,4096]{2,1,0:T(8,128)(2,1)S(1)}, bf16[2,32,4096]{2,1,0:T(8,128)(2,1)}, u32[]{:S(2)}, u32[]{:S(2)}) collective-permute-start(bf16[2,32,4096]{2,1,0:T(8,128)(2,1)S(1)} %fusion.1), channel_id=1, source_target_pairs={{0,1},{1,0},{2,3},{3,2},{4,5},{5,4},{6,7},{7,6},{8,9},{9,8},{10,11... | collective-permute-start | bytes 1572872 | tf_op jit(solution)/shard_map/ppermute | solution.py:62
  115.1 8.7 %collective-permute-start.13 = (bf16[32,4096]{1,0:T(8,128)(2,1)S(1)}, bf16[32,4096]{1,0:T(8,128)(2,1)S(1)}, u32[]{:S(2)}, u32[]{:S(2)}) collective-permute-start(bf16[32,4096]{1,0:T(8,128)(2,1)S(1)} %fusion.4), channel_id=1, source_target_pairs={{0,2},{1,3},{2,0},{3,1},{4,6},{5,7},{6,4},{7,5},{8,10},{9,11},{10,... | collective-permute-start | bytes 786440 | tf_op jit(solution)/shard_map/ppermute | solution.py:62

commit v2 on v1

v2 whole, which is shorter than its diff:
```python
import functools

import jax
import jax.numpy as jnp
from jax import lax
from jax.experimental import pallas as pl
from jax.experimental.pallas import tpu as pltpu
from jax.sharding import PartitionSpec as P

HD = 128
BLOCK = 128
CB_DEV = 8
KVL = 2
GROUP = 4
NX, NY, NZ = 4, 2, 4
HALVES, CORES = 2, 2
COLS = GROUP * BLOCK
ROWS = HD + 8
STEPS = (1, -1, 2)
SCALE = HD**-0.5
NEG = -1e30
AXES = ("ctx", "head")
COST = pl.CostEstimate(flops=1 << 31, transcendentals=1 << 20, bytes_accessed=12 << 20)
BF = jnp.bfloat16
F32 = jnp.float32


def flat(x, y, z, yl, c):
    return ((x * NY + y) * NZ + z) * (HALVES * CORES) + yl * CORES + c


def everyone():
    for x in range(NX):
        for y in range(NY):
            for z in range(NZ):
                for yl in range(HALVES):
                    for c in range(CORES):
                        yield x, y, z, yl, c


def moved(x, y, z, yl, c, by, keys):
    if (c == 0) == keys:
        return flat(x, y, (z + by) % NZ, yl, c)
    return flat((x + by) % NX, y, z, yl, c)


def pairs_along(by, keys):
    return [(flat(*d), moved(*d, by, keys)) for d in everyone()]


PAIRS_Y = [(flat(x, y, z, l, c), flat(x, 1 - y, z, l, c)) for x, y, z, l, c in everyone()]
PAIRS_CORE = [(flat(x, y, z, l, c), flat(x, y, z, l, 1 - c)) for x, y, z, l, c in everyone()]
PAIRS_LO = [(flat(x, y, z, l, c), flat(x, y, z, 1 - l, c)) for x, y, z, l, c in everyone()]
PAIRS_PREV = [
    (i * HALVES * CORES + h, (i + 1) * HALVES * CORES + h)
    for i in range(NX * NY * NZ - 1)
    for h in range(HALVES * CORES)
]


def send(array, pairs):
    return lax.ppermute(array, AXES, pairs)


def nt(a, b):
    return lax.dot_general(a, b, (((1,), (1,)), ((), ())), preferred_element_type=F32)


def nn(a, b):
    return lax.dot_general(a, b, (((1,), (0,)), ((), ())), preferred_element_type=F32)


def turned(block):
    return block.astype(F32).T.astype(BF)


def packed_sum(level):
    hi = level.astype(BF)
    rest = level - hi.astype(F32)
    mid = rest.astype(BF)
    low = (rest - mid.astype(F32)).astype(BF)
    return jnp.concatenate([hi.astype(F32), mid.astype(F32), low.astype(F32), jnp.zeros((5, COLS), F32)], axis=0).astype(BF)


def pack_kernel(list_ref, q_ref, k_ref, v_ref, asked_ref, kv_ref, v_buf, sems):
    rows = k_ref.shape[0]
    copies = [
        pltpu.make_async_copy(q_ref, asked_ref.at[0:BLOCK], sems.at[0]),
        pltpu.make_async_copy(v_ref, v_buf, sems.at[1]),
        pltpu.make_async_copy(k_ref, kv_ref.at[0:rows], sems.at[2]),
    ]
    for copy in copies:
        copy.start()
    asked_ref[BLOCK : BLOCK + 8, :] = jnp.zeros((8, asked_ref.shape[1]), BF)
    asked_ref[BLOCK : BLOCK + KVL, 0 : list_ref.shape[1]] = list_ref[...].astype(F32).astype(BF)
    copies[1].wait()
    for b in range(CB_DEV):
        for h in range(KVL):
            cols = slice(h * HD, (h + 1) * HD)
            kv_ref[rows + b * BLOCK : rows + (b + 1) * BLOCK, cols] = turned(v_buf[b * BLOCK : (b + 1) * BLOCK, cols])
    copies[0].wait()
    copies[2].wait()


def query_rows(q):
    return jnp.concatenate([q[:, m * HD : (m + 1) * HD] for m in range(GROUP)], axis=0)


def attend(tab_ref, q_ref, kvs, shard, y, h):
    q = query_rows(q_ref[y, 0:BLOCK, h * COLS : (h + 1) * COLS])
    cols = slice(h * HD, (h + 1) * HD)
    scores, offs, values = [], [], []
    for s, (keys, turned_values, base) in enumerate(kvs):
        first, second = tab_ref[y, h, shard + s, 0], tab_ref[y, h, shard + s, 1]
        for j, b in enumerate((first, second)):
            row = pl.multiple_of(b * BLOCK, BLOCK)
            scores.append(nt(keys[pl.ds(row, BLOCK), cols], q))
            values.append(turned_values[pl.ds(row + base, BLOCK), cols])
            offs.append(None if j == 0 else jnp.where(second == first, NEG, 0.0).astype(F32))
    tops = [
        jnp.max(t, axis=0, keepdims=True) if o is None else jnp.max(t, axis=0, keepdims=True) + o
        for t, o in zip(scores, offs)
    ]
    top = functools.reduce(jnp.maximum, tops) * SCALE
    weights = [jnp.exp(t * SCALE - (top if o is None else top - o)).astype(BF) for t, o in zip(scores, offs)]
    weights = jnp.concatenate(weights, axis=0)
    ones = jnp.ones((8, weights.shape[0]), BF)
    mixture = nn(jnp.concatenate([jnp.concatenate(values, axis=1), ones], axis=0), weights)
    return top, mixture[HD : HD + 1], mixture[0:HD]


def early_kernel(tab_ref, q0_ref, q1_ref, q2_ref, q3_ref, kv0_ref, kv1_ref, *out_refs):
    kvs = [(r, r, CB_DEV * BLOCK) for r in (kv0_ref, kv1_ref)]
    for i, q_ref in enumerate((q0_ref, q1_ref, q2_ref, q3_ref)):
        o_ref, s_ref = out_refs[2 * i : 2 * i + 2]
        for y in range(NY):
            for h in range(KVL):
                top, total, mixture = attend(tab_ref.at[i], q_ref, kvs, 0, y, h)
                o_ref[y, h] = mixture
                s_ref[y, h, 0:1, :] = top
                s_ref[y, h, 1:2, :] = total


def late_kernel(tab_ref, q_ref, kv2_ref, k3_ref, v3_ref, m_ref, s_ref, o_ref):
    kvs = [(kv2_ref, kv2_ref, CB_DEV * BLOCK), (k3_ref, v3_ref, 0)]
    for y in range(NY):
        for h in range(KVL):
            top, total, mixture = attend(tab_ref, q_ref, kvs, 2, y, h)
            top0, total0 = s_ref[y, h, 0:1, :], s_ref[y, h, 1:2, :]
            peak = jnp.maximum(top, top0)
            share, share0 = jnp.exp(top - peak), jnp.exp(top0 - peak)
            total = total * share + total0 * share0
            inverse = 1.0 / total
            o_ref[y, h, 0:HD, :] = (mixture * (share * inverse) + m_ref[y, h] * (share0 * inverse)).astype(BF)
            o_ref[y, h, HD:ROWS, :] = packed_sum(peak + jnp.log(total))


def stretch_kernel(first_ref, q_ref, k_ref, v_ref, prev_ref, o_ref, l_ref):
    off = jnp.where(first_ref[0] == 0, NEG, 0.0).astype(F32)
    key = lax.broadcasted_iota(jnp.int32, (BLOCK, COLS), 0)
    row = lax.broadcasted_iota(jnp.int32, (BLOCK, COLS), 1) % BLOCK
    for h in range(KVL):
        q = query_rows(q_ref[:, h * COLS : (h + 1) * COLS])
        cols = slice(h * HD, (h + 1) * HD)
        vcols = slice((KVL + h) * HD, (KVL + h + 1) * HD)
        own = jnp.where(key <= row, nt(k_ref[:, cols], q), NEG)
        before = nt(prev_ref[:, cols], q)
        top = jnp.maximum(
            jnp.max(own, axis=0, keepdims=True), jnp.max(before, axis=0, keepdims=True) + off
        ) * SCALE
        w_own = jnp.exp(own * SCALE - top)
        w_before = jnp.exp(before * SCALE - (top - off))
        total = jnp.sum(w_own, axis=0, keepdims=True) + jnp.sum(w_before, axis=0, keepdims=True)
        mixture = nn(turned(v_ref[:, cols]), w_own.astype(BF)) + nn(
            turned(prev_ref[:, vcols]), w_before.astype(BF)
        )
        o_ref[h] = mixture * (1.0 / total)
        l_ref[h] = jnp.broadcast_to(top + jnp.log(total), (8, COLS))


def level_of(rows):
    r = rows.astype(F32)
    return r[0:1] + r[1:2] + r[2:3]


def joined(mixtures, levels):
    top = functools.reduce(jnp.maximum, levels)
    shares = [jnp.exp(v - top) for v in levels]
    total = functools.reduce(jnp.add, shares)
    inverse = 1.0 / total
    mixture = functools.reduce(jnp.add, [m * (s * inverse) for m, s in zip(mixtures, shares)])
    return mixture, top + jnp.log(total)


def join_kernel(which, *refs):
    parts, o_ref = refs[:-1], refs[-1]
    for h in range(KVL):
        mixture, level = joined(
            [p[which, h, 0:HD, :].astype(F32) for p in parts], [level_of(p[which, h, HD:ROWS, :]) for p in parts]
        )
        o_ref[h, 0:HD, :] = mixture.astype(BF)
        o_ref[h, HD:ROWS, :] = packed_sum(level)


def last_kernel(
    place_ref, a_ref, b_ref, c_ref, d_ref, e_ref, s_ref, l_ref, w_ref, theirs_ref, mine_ref, att_ref, w_buf, sems
):
    chunks = sems.shape[0]
    width = w_buf.shape[1] // chunks
    copies = [
        pltpu.make_async_copy(
            w_ref.at[:, i * width : (i + 1) * width], w_buf.at[:, i * width : (i + 1) * width], sems.at[i]
        )
        for i in range(chunks)
    ]
    for copy in copies:
        copy.start()
    parts = (a_ref, b_ref, c_ref, d_ref)
    for h in range(KVL):
        mixtures = [p[0, h, 0:HD, :].astype(F32) for p in parts] + [e_ref[h, 0:HD, :].astype(F32), s_ref[h]]
        levels = [level_of(p[0, h, HD:ROWS, :]) for p in parts] + [level_of(e_ref[h, HD:ROWS, :]), l_ref[h, 0:1, :]]
        mixture, _ = joined(mixtures, levels)
        for m in range(GROUP):
            c = (h * GROUP + m) * HD
            att_ref[:, c : c + HD] = mixture[:, m * BLOCK : (m + 1) * BLOCK].T.astype(BF)
    half, core = place_ref[0], place_ref[1]
    share = BLOCK // (HALVES * CORES)
    order = [(1 - half, 1 - core), (half, 1 - core), (1 - half, core), (half, core)]
    rows = [att_ref[pl.ds(pl.multiple_of((a * CORES + b) * share, share), share), :] for a, b in order]
    rows = jnp.concatenate(rows, axis=0)
    for n in range(chunks):
        cols = slice(n * width, (n + 1) * width)
        copies[n].wait()
        product = nn(rows, w_buf[:, cols])
        for i in range(HALVES):
            theirs_ref[i, :, cols] = product[i * share : (i + 1) * share].astype(BF)
            mine_ref[i, :, cols] = product[(HALVES + i) * share : (HALVES + i + 1) * share]


def call(kernel, out_shape, smem=0, n=0, hbm=0, name=None, memory=24, scratch=(), cost=None):
    spaces = [pltpu.SMEM] * smem + [pltpu.VMEM] * n + [pltpu.HBM] * hbm
    vm = pl.BlockSpec(memory_space=pltpu.VMEM)
    return pl.pallas_call(
        kernel,
        out_shape=out_shape,
        in_specs=[pl.BlockSpec(memory_space=space) for space in spaces],
        out_specs=jax.tree.map(lambda _: vm, out_shape),
        scratch_shapes=scratch,
        compiler_params=pltpu.CompilerParams(vmem_limit_bytes=memory << 20),
        cost_estimate=cost,
        name=name,
    )


def shape(dims, dtype):
    return jax.ShapeDtypeStruct(dims, dtype)


def shards(queries, keys_new, values_new, cache_keys, cache_values, block_list, block_count, out_weight):
    ctx, head = lax.axis_index("ctx"), lax.axis_index("head")
    x, z = ctx // (NY * NZ), ctx % NZ
    core, half = head % CORES, head // CORES
    sel = block_list.shape[2]

    rows = cache_keys.shape[0]
    asked, kv = call(
        pack_kernel,
        (shape((queries.shape[0] + 8, queries.shape[1]), BF), shape((2 * rows, cache_keys.shape[1]), BF)),
        n=1,
        hbm=3,
        name="pack",
        scratch=[pltpu.VMEM(cache_values.shape, BF), pltpu.SemaphoreType.DMA((3,))],
    )(block_list.reshape(KVL, sel), *(pltpu.with_memory_space_constraint(a, pltpu.HBM) for a in (queries, cache_keys, cache_values)))
    asked_pair = jnp.stack([asked, send(asked, PAIRS_Y)])
    after, before = send(kv, pairs_along(-1, True)), send(kv, pairs_along(1, True))
    asked_all = [asked_pair] + [send(asked_pair, pairs_along(-d, False)) for d in STEPS]
    half_keys, half_values = after[:rows], before[rows:]
    asked_all, half_keys, half_values = lax.optimization_barrier((asked_all, half_keys, half_values))
    far_keys = send(half_keys, pairs_along(-1, True))
    far_values = send(half_values, pairs_along(1, True))

    steps = jnp.array((0,) + STEPS, jnp.int32)
    owners = jnp.where(core == 0, ctx - z + (z + steps) % NZ, ctx + ((x + steps) % NX - x) * NY * NZ)
    lists = jnp.stack([a[:, BLOCK : BLOCK + KVL, None, :sel] for a in asked_all]).astype(jnp.int32)
    inside = lists // CB_DEV == owners[:, None]
    slot = lists % CB_DEV
    table = jnp.stack(
        [jnp.min(jnp.where(inside, slot, CB_DEV), axis=-1), jnp.max(jnp.where(inside, slot, -1), axis=-1)], axis=-1
    )
    table = jnp.clip(table, 0, CB_DEV - 1)
    begun = call(
        early_kernel,
        (shape((NY, KVL, HD, COLS), F32), shape((NY, KVL, 8, COLS), F32)) * 4,
        smem=1,
        n=6,
        name="early",
        cost=COST,
    )(table, *asked_all, kv, after)
    begun, keys_new, values_new = lax.optimization_barrier((begun, keys_new, values_new))

    prev = send(jnp.concatenate([keys_new, values_new], axis=1), PAIRS_PREV)
    local = call(
        stretch_kernel, (shape((KVL, HD, COLS), F32), shape((KVL, 8, COLS), F32)), smem=1, n=4, name="stretch"
    )(jnp.minimum(ctx, 1).reshape(1), queries, keys_new, values_new, prev)

    parts = []
    for i in (3, 1, 2, 0):
        part = call(late_kernel, shape((NY, KVL, ROWS, COLS), BF), smem=1, n=6, name="late", cost=COST)(
            table[i], asked_all[i], before, far_keys, far_values, begun[2 * i], begun[2 * i + 1]
        )
        parts.append(part if i == 0 else send(part, pairs_along(((0,) + STEPS)[i], False)))
    other = call(functools.partial(join_kernel, 1), shape((KVL, ROWS, COLS), BF), n=4, name="join")(*parts)
    other = send(other, PAIRS_Y)

    share, width = BLOCK // (HALVES * CORES), out_weight.shape[1]
    theirs, mine = call(
        last_kernel,
        (shape((HALVES, share, width), BF), shape((HALVES, share, width), F32)),
        smem=1,
        n=7,
        hbm=1,
        name="last",
        scratch=[
            pltpu.VMEM((BLOCK, KVL * COLS), BF),
            pltpu.VMEM(out_weight.shape, BF),
            pltpu.SemaphoreType.DMA((4,)),
        ],
    )(jnp.stack([half, core]), *parts, other, *local, pltpu.with_memory_space_constraint(out_weight, pltpu.HBM))
    chip = mine + send(theirs, PAIRS_CORE).astype(F32)
    return (chip[1] + send(chip[0].astype(BF), PAIRS_LO).astype(F32)).astype(BF)


def solution(mesh):
    return jax.shard_map(
        shards,
        mesh=mesh,
        in_specs=(
            P("ctx", "head"),
            P("ctx", "head"),
            P("ctx", "head"),
            P("ctx", "head"),
            P("ctx", "head"),
            P("head", "ctx", None),
            P("head", "ctx"),
            P("head", None),
        ),
        out_specs=P(("ctx", "head"), None),
        check_vma=False,
    )
```

time: 127 us -> 107 us (0.84); the launches traced: 124 us -> 106 us
  waiting for transfers between devices: 51.3 us -> 45.2 us
  other arithmetic: 8.04 us -> 2.51 us
  matrix products: 4.64 us -> 0 us
  Pallas kernels: 27.4 us -> 31.9 us
  starting transfers between devices: 24 us -> 20.4 us
  local copies, waits for them, and re-layouts: 8.87 us -> 5.48 us
    ppermute x14 -> x15, waiting for transfers between devices: 51.3 us -> 45.2 us  [send(): return lax.ppermute(array, AXES, pairs)]
    dot_general x1 -> x0, matrix products: 4.64 us -> none  [shards(): product = jnp.dot(attention, out_weight, preferred_element_type=F32)]
    pallas_call x8 -> x9, Pallas kernels: 27.4 us -> 31.9 us  [the longest x4 13 us: shards(): call(late_kernel, shape((NY, KVL, ROWS, COLS), BF), smem=1, n=6, name='la...]
    ppermute x14 -> x15, starting transfers between devices: 24 us -> 20.4 us  [send(): return lax.ppermute(array, AXES, pairs)]
    unnamed x17 -> x12, local copies, waits for them, and re-layouts: 4.46 us -> 1.92 us
    another operation x2 -> x1, other arithmetic: 1.94 us -> 0.05 us  [shards(): asked_pair = jnp.stack([asked, send(asked, PAIRS_Y)])]
    squeeze x6 -> x1, local copies, waits for them, and re-layouts: 1.8 us -> 0.01 us  [shards(): table[i]]
    another operation x4, local copies, waits for them, and re-layouts: 0.35 us -> 1.8 us  [the longest x2 1.39 us: shards(): jnp.stack([a[:, BLOCK:BLOCK + KVL, None, :sel] for a in asked_all])]
  transfers between devices with their start and end apart: 14 -> 15, of which waited for: 8 -> 8; matrix products, arithmetic and copies ran while one was open for 5% -> 2% of each run, Pallas kernels for 14% -> 20%
where the time goes in v2:
time: 107 us; the launch traced here: 106 us
  waiting for transfers between devices  45.2 us (42%)
  Pallas kernels  31.9 us (30%)
  starting transfers between devices  20.4 us (19%)
  local copies, waits for them, and re-layouts  5.48 us (5%)
  other arithmetic  2.51 us (2%)
    ppermute x15, waiting for transfers between devices, send(): return lax.ppermute(array, AXES, pairs)  45.2 us
    ppermute x15, starting transfers between devices, send(): return lax.ppermute(array, AXES, pairs)  20.4 us
    pallas_call x4, Pallas kernels, shards(): call(late_kernel, shape((NY, KVL, ROWS, COLS), BF), smem=1, n=6, name='la...  13 us
    pallas_call x1, Pallas kernels, shards(): call(early_kernel, (shape((NY, KVL, HD, COLS), F32), shape((NY, KVL, 8, C...  10.4 us
    pallas_call x1, Pallas kernels, shards(): call(last_kernel, (shape((HALVES, share, width), BF), shape((HALVES, shar...  4.89 us
    pallas_call x1, Pallas kernels, shards(): call(pack_kernel, (shape((queries.shape[0] + 8, queries.shape[1]), BF), s...  2.33 us
  transfers between devices with their start and end apart: 15, of which 8 were waited for; matrix products, arithmetic and copies ran while one was open for 2% of the time, Pallas kernels for 20%

profile of v2, /device:TPU:16, one launch (start us, length us, event | category | flops | bytes accessed | tf_op | source)
XLA Modules:
  0.0 105.7 jit_solution(5286731127404647350)
XLA Ops:
  0.7 2.3 %pack.1 = (bf16[136,1024]{1,0:T(8,128)(2,1)S(1)}, bf16[2048,256]{1,0:T(8,128)(2,1)}) custom-call(s32[2,64]{1,0:T(2,128)S(1)} %bitcast.33, bf16[128,1024]{1,0:T(8,128)(2,1)} %q_ref.3, bf16[1024,256]{1,0:T(8,128)(2,1)} %k_ref.1, bf16[1024,256]{1,0:T(8,128)(2,1)} %v_ref.1), custom_call_target="tpu_custom_call" | custom-call | tf_op jit(solution)/shard_map/pack/pallas_call | solution.py:266
  3.0 2.0 %collective-permute-start.5 = (bf16[2048,256]{1,0:T(8,128)(2,1)}, bf16[2048,256]{1,0:T(8,128)(2,1)S(1)}, u32[]{:S(2)}, u32[]{:S(2)}) collective-permute-start(bf16[2048,256]{1,0:T(8,128)(2,1)} %get-tuple-element.36.kv0_ref), channel_id=1, source_target_pairs={{0,4},{1,33},{2,6},{3,35},{4,8},{5,37},{6,10},{7,39},{8,12},{9,41}... | collective-permute-start | bytes 3145736 | tf_op jit(solution)/shard_map/ppermute | solution.py:62
  5.0 2.2 %collective-permute-start.4 = (bf16[2048,256]{1,0:T(8,128)(2,1)}, bf16[2048,256]{1,0:T(8,128)(2,1)S(1)}, u32[]{:S(2)}, u32[]{:S(2)}) collective-permute-start(bf16[2048,256]{1,0:T(8,128)(2,1)} %get-tuple-element.36.kv0_ref), channel_id=1, source_target_pairs={{0,12},{1,97},{2,14},{3,99},{4,0},{5,101},{6,2},{7,103},{8,4},{9,1... | collective-permute-start | bytes 3145736 | tf_op jit(solution)/shard_map/ppermute | solution.py:62
  7.5 8.1 %collective-permute-done = bf16[136,1024]{1,0:T(8,128)(2,1)S(1)} collective-permute-done((bf16[136,1024]{1,0:T(8,128)(2,1)S(1)}, bf16[136,1024]{1,0:T(8,128)(2,1)S(1)}, u32[]{:S(2)}, u32[]{:S(2)}) %collective-permute-start) | collective-permute-done | bytes 278560 | tf_op jit(solution)/shard_map/ppermute | solution.py:62
  15.7 2.4 %collective-permute-start.1 = (bf16[2,136,1024]{2,1,0:T(8,128)(2,1)S(1)}, bf16[2,136,1024]{2,1,0:T(8,128)(2,1)}, u32[]{:S(2)}, u32[]{:S(2)}) collective-permute-start(bf16[2,136,1024]{2,1,0:T(8,128)(2,1)S(1)} %pad_maximum_fusion.q0_ref.q_ref), channel_id=1, source_target_pairs={{0,96},{1,13},{2,98},{3,15},{4,100},{5,1},{6,102},{7,3},{8,104},{9... | collective-permute-start | bytes 1671176 | tf_op jit(solution)/shard_map/ppermute | solution.py:62
  18.1 2.3 %collective-permute-start.3 = (bf16[2,136,1024]{2,1,0:T(8,128)(2,1)S(1)}, bf16[2,136,1024]{2,1,0:T(8,128)(2,1)}, u32[]{:S(2)}, u32[]{:S(2)}) collective-permute-start(bf16[2,136,1024]{2,1,0:T(8,128)(2,1)S(1)} %pad_maximum_fusion.q0_ref.q_ref), channel_id=1, source_target_pairs={{0,64},{1,9},{2,66},{3,11},{4,68},{5,13},{6,70},{7,15},{8,72},{9,1... | collective-permute-start | bytes 1671176 | tf_op jit(solution)/shard_map/ppermute | solution.py:62
  22.9 8.3 %collective-permute-done.1.q1_ref.q_ref = bf16[2,136,1024]{2,1,0:T(8,128)(2,1)} collective-permute-done((bf16[2,136,1024]{2,1,0:T(8,128)(2,1)S(1)}, bf16[2,136,1024]{2,1,0:T(8,128)(2,1)}, u32[]{:S(2)}, u32[]{:S(2)}) %collective-permute-start.1) | collective-permute-done | bytes 557088 | tf_op jit(solution)/shard_map/ppermute | solution.py:62
  31.2 3.8 %collective-permute-done.2.q2_ref.q_ref = bf16[2,136,1024]{2,1,0:T(8,128)(2,1)} collective-permute-done((bf16[2,136,1024]{2,1,0:T(8,128)(2,1)S(1)}, bf16[2,136,1024]{2,1,0:T(8,128)(2,1)}, u32[]{:S(2)}, u32[]{:S(2)}) %collective-permute-start.2) | collective-permute-done | bytes 557088 | tf_op jit(solution)/shard_map/ppermute | solution.py:62
  37.5 3.3 %collective-permute-start.6 = (bf16[1024,256]{1,0:T(8,128)(2,1)}, bf16[1024,256]{1,0:T(8,128)(2,1)S(1)}, u32[]{:S(2)}, u32[]{:S(2)}) collective-permute-start(bf16[1024,256]{1,0:T(8,128)(2,1)} %slice.49), channel_id=1, source_target_pairs={{0,12},{1,97},{2,14},{3,99},{4,0},{5,101},{6,2},{7,103},{8,4},{9,1... | collective-permute-start | bytes 1572872 | tf_op jit(solution)/shard_map/ppermute | solution.py:62
  40.9 10.4 %early.1 = (f32[2,2,128,512]{3,2,1,0:T(8,128)S(1)}, f32[2,2,8,512]{3,2,1,0:T(8,128)S(1)}, f32[2,2,128,512]{3,2,1,0:T(8,128)S(1)}, f32[2,2,8,512]{3,2,1,0:T(8,128...) custom-call(s32[4,2,2,4,2]{4,3,2,1,0:T(4,128)S(1)} %add_clamp_fusion, ...), custom_call_target="tpu_custom_call" | custom-call | flops 2147483648 | bytes 12582912 | tf_op jit(solution)/shard_map/early/pallas_call | solution.py:291
  51.4 3.3 %late.6 = bf16[2,2,136,512]{3,2,1,0:T(8,128)(2,1)S(1)} custom-call(s32[2,2,4,2]{3,2,1,0:T(4,128)S(1)} %get-tuple-element.70.tab_ref, bf16[2,136,1024]{2,1,0:T(8,128)(2,1)} %collective-permute-done.2.q2_ref.q_ref, bf16[2048,256]{1,0:T(8,128)(2,1)S(1)} %collective-permute-done.5.kv2_ref, bf16[1024,256]{1,0:T(8,128)(2,1)S(1)} %collective-permute-done.6.k3_ref, ...), custom_call_target="tpu_custom_call" | custom-call | flops 2147483648 | bytes 12582912 | tf_op jit(solution)/shard_map/late/pallas_call | solution.py:308
  54.9 3.3 %late.5 = bf16[2,2,136,512]{3,2,1,0:T(8,128)(2,1)S(1)} custom-call(s32[2,2,4,2]{3,2,1,0:T(4,128)S(1)} %get-tuple-element.71.tab_ref, bf16[2,136,1024]{2,1,0:T(8,128)(2,1)} %collective-permute-done.1.q1_ref.q_ref, bf16[2048,256]{1,0:T(8,128)(2,1)S(1)} %collective-permute-done.5.kv2_ref, bf16[1024,256]{1,0:T(8,128)(2,1)S(1)} %collective-permute-done.6.k3_ref, ...), custom_call_target="tpu_custom_call" | custom-call | flops 2147483648 | bytes 12582912 | tf_op jit(solution)/shard_map/late/pallas_call | solution.py:308
  58.2 2.3 %collective-permute-start.9 = (bf16[2,2,136,512]{3,2,1,0:T(8,128)(2,1)S(1)}, bf16[2,2,136,512]{3,2,1,0:T(8,128)(2,1)S(1)}, u32[]{:S(2)}, u32[]{:S(2)}) collective-permute-start(bf16[2,2,136,512]{3,2,1,0:T(8,128)(2,1)S(1)} %late.5), channel_id=1, source_target_pairs={{0,32},{1,5},{2,34},{3,7},{4,36},{5,9},{6,38},{7,11},{8,40},{9,13}... | collective-permute-start | bytes 1671176 | tf_op jit(solution)/shard_map/ppermute | solution.py:62
  60.5 3.4 %late.4 = bf16[2,2,136,512]{3,2,1,0:T(8,128)(2,1)S(1)} custom-call(s32[2,2,4,2]{3,2,1,0:T(4,128)S(1)} %get-tuple-element.72.tab_ref, bf16[2,136,1024]{2,1,0:T(8,128)(2,1)} %collective-permute-done.3.q3_ref.q_ref, bf16[2048,256]{1,0:T(8,128)(2,1)S(1)} %collective-permute-done.5.kv2_ref, bf16[1024,256]{1,0:T(8,128)(2,1)S(1)} %collective-permute-done.6.k3_ref, ...), custom_call_target="tpu_custom_call" | custom-call | flops 2147483648 | bytes 12582912 | tf_op jit(solution)/shard_map/late/pallas_call | solution.py:308
  64.8 1.2 %copy-done.2 = bf16[2048,256]{1,0:T(8,128)(2,1)S(1)} copy-done((bf16[2048,256]{1,0:T(8,128)(2,1)S(1)}, bf16[2048,256]{1,0:T(8,128)(2,1)}, u32[]{:S(2)}) %copy-start.2) | copy-done | bytes 1048600
  66.0 2.9 %late.7.refs_3_.d_ref = bf16[2,2,136,512]{3,2,1,0:T(8,128)(2,1)S(1)} custom-call(s32[2,2,4,2]{3,2,1,0:T(4,128)S(1)} %get-tuple-element.69.tab_ref, bf16[2,136,1024]{2,1,0:T(8,128)(2,1)S(1)} %pad_maximum_fusion.q0_ref.q_ref, bf16[2048,256]{1,0:T(8,128)(2,1)S(1)} %copy-done.2, bf16[1024,256]{1,0:T(8,128)(2,1)S(1)} %collective-permute-done.6.k3_ref, ...), custom_call_target="tpu_custom_call" | custom-call | flops 2147483648 | bytes 12582912 | tf_op jit(solution)/shard_map/late/pallas_call | solution.py:308
  69.0 6.3 %collective-permute-done.9.refs_1_.b_ref = bf16[2,2,136,512]{3,2,1,0:T(8,128)(2,1)S(1)} collective-permute-done((bf16[2,2,136,512]{3,2,1,0:T(8,128)(2,1)S(1)}, bf16[2,2,136,512]{3,2,1,0:T(8,128)(2,1)S(1)}, u32[]{:S(2)}, u32[]{:S(2)}) %collective-permute-start.9) | collective-permute-done | bytes 557088 | tf_op jit(solution)/shard_map/ppermute | solution.py:62
  75.9 1.9 %collective-permute-start.12 = (bf16[128,512]{1,0:T(8,128)(2,1)S(1)}, bf16[128,512]{1,0:T(8,128)(2,1)S(1)}, u32[]{:S(2)}, u32[]{:S(2)}) collective-permute-start(bf16[128,512]{1,0:T(8,128)(2,1)S(1)} %pad_maximum_fusion.1), channel_id=1, source_target_pairs={{0,4},{1,5},{2,6},{3,7},{4,8},{5,9},{6,10},{7,11},{8,12},{9,13},{1... | collective-permute-start | bytes 393224 | tf_op jit(solution)/shard_map/ppermute | solution.py:62
  78.0 10.2 %collective-permute-done.12.prev_ref = bf16[128,512]{1,0:T(8,128)(2,1)S(1)} collective-permute-done((bf16[128,512]{1,0:T(8,128)(2,1)S(1)}, bf16[128,512]{1,0:T(8,128)(2,1)S(1)}, u32[]{:S(2)}, u32[]{:S(2)}) %collective-permute-start.12) | collective-permute-done | bytes 131104 | tf_op jit(solution)/shard_map/ppermute | solution.py:62
  88.1 0.9 stretch.1
  89.1 4.9 %last.1 = (bf16[2,32,4096]{2,1,0:T(8,128)(2,1)S(1)}, f32[2,32,4096]{2,1,0:T(8,128)S(1)}) custom-call(s32[2]{0:T(128)S(1)} %pad_add_fusion.place_ref, bf16[2,2,136,512]{3,2,1,0:T(8,128)(2,1)S(1)} %collective-permute-done.8.refs_0_.a_ref, bf16[2,2,136,512]{3,2,1,0:T(8,128)(2,1)S(1)} %collective-permute-done.9.refs_1_.b_ref, ...), custom_call_target="tpu_custom_call" | custom-call | tf_op jit(solution)/shard_map/last/pallas_call | solution.py:316
  94.1 1.9 %collective-permute-done.13 = bf16[2,32,4096]{2,1,0:T(8,128)(2,1)S(1)} collective-permute-done((bf16[2,32,4096]{2,1,0:T(8,128)(2,1)S(1)}, bf16[2,32,4096]{2,1,0:T(8,128)(2,1)S(1)}, u32[]{:S(2)}, u32[]{:S(2)}) %collective-permute-start.13) | collective-permute-done | bytes 524320 | tf_op jit(solution)/shard_map/ppermute | solution.py:62
  96.1 2.3 %collective-permute-start.14 = (bf16[32,4096]{1,0:T(8,128)(2,1)S(1)}, bf16[32,4096]{1,0:T(8,128)(2,1)S(1)}, u32[]{:S(2)}, u32[]{:S(2)}) collective-permute-start(bf16[32,4096]{1,0:T(8,128)(2,1)S(1)} %fusion.2), channel_id=1, source_target_pairs={{0,2},{1,3},{2,0},{3,1},{4,6},{5,7},{6,4},{7,5},{8,10},{9,11},{10,... | collective-permute-start | bytes 786440 | tf_op jit(solution)/shard_map/ppermute | solution.py:62
  98.4 6.6 %collective-permute-done.14 = bf16[32,4096]{1,0:T(8,128)(2,1)S(1)} collective-permute-done((bf16[32,4096]{1,0:T(8,128)(2,1)S(1)}, bf16[32,4096]{1,0:T(8,128)(2,1)S(1)}, u32[]{:S(2)}, u32[]{:S(2)}) %collective-permute-start.14) | collective-permute-done | bytes 262176 | tf_op jit(solution)/shard_map/ppermute | solution.py:62
  (45 shorter events, 8.9 us)
Async XLA Ops:
  0.0 0.7 copy-start.5
  3.0 18.1 %collective-permute-start.5 = (bf16[2048,256]{1,0:T(8,128)(2,1)}, bf16[2048,256]{1,0:T(8,128)(2,1)S(1)}, u32[]{:S(2)}, u32[]{:S(2)}) collective-permute-start(bf16[2048,256]{1,0:T(8,128)(2,1)} %get-tuple-element.36.kv0_ref), channel_id=1, source_target_pairs={{0,4},{1,33},{2,6},{3,35},{4,8},{5,37},{6,10},{7,39},{8,12},{9,41}... | collective-permute-start | bytes 3145736 | tf_op jit(solution)/shard_map/ppermute | solution.py:62
  5.0 17.0 %collective-permute-start.4 = (bf16[2048,256]{1,0:T(8,128)(2,1)}, bf16[2048,256]{1,0:T(8,128)(2,1)S(1)}, u32[]{:S(2)}, u32[]{:S(2)}) collective-permute-start(bf16[2048,256]{1,0:T(8,128)(2,1)} %get-tuple-element.36.kv0_ref), channel_id=1, source_target_pairs={{0,12},{1,97},{2,14},{3,99},{4,0},{5,101},{6,2},{7,103},{8,4},{9,1... | collective-permute-start | bytes 3145736 | tf_op jit(solution)/shard_map/ppermute | solution.py:62
  7.2 8.5 %collective-permute-start = (bf16[136,1024]{1,0:T(8,128)(2,1)S(1)}, bf16[136,1024]{1,0:T(8,128)(2,1)S(1)}, u32[]{:S(2)}, u32[]{:S(2)}) collective-permute-start(bf16[136,1024]{1,0:T(8,128)(2,1)S(1)} %get-tuple-element.35), channel_id=1, source_target_pairs={{0,16},{1,17},{2,18},{3,19},{4,20},{5,21},{6,22},{7,23},{8,24},{9,... | collective-permute-start | bytes 835592 | tf_op jit(solution)/shard_map/ppermute | solution.py:62
  15.7 15.5 %collective-permute-start.1 = (bf16[2,136,1024]{2,1,0:T(8,128)(2,1)S(1)}, bf16[2,136,1024]{2,1,0:T(8,128)(2,1)}, u32[]{:S(2)}, u32[]{:S(2)}) collective-permute-start(bf16[2,136,1024]{2,1,0:T(8,128)(2,1)S(1)} %pad_maximum_fusion.q0_ref.q_ref), channel_id=1, source_target_pairs={{0,96},{1,13},{2,98},{3,15},{4,100},{5,1},{6,102},{7,3},{8,104},{9... | collective-permute-start | bytes 1671176 | tf_op jit(solution)/shard_map/ppermute | solution.py:62
  18.1 16.8 %collective-permute-start.2 = (bf16[2,136,1024]{2,1,0:T(8,128)(2,1)S(1)}, bf16[2,136,1024]{2,1,0:T(8,128)(2,1)}, u32[]{:S(2)}, u32[]{:S(2)}) collective-permute-start(bf16[2,136,1024]{2,1,0:T(8,128)(2,1)S(1)} %pad_maximum_fusion.q0_ref.q_ref), channel_id=1, source_target_pairs={{0,32},{1,5},{2,34},{3,7},{4,36},{5,9},{6,38},{7,11},{8,40},{9,13}... | collective-permute-start | bytes 1671176 | tf_op jit(solution)/shard_map/ppermute | solution.py:62
  18.1 16.8 %collective-permute-start.3 = (bf16[2,136,1024]{2,1,0:T(8,128)(2,1)S(1)}, bf16[2,136,1024]{2,1,0:T(8,128)(2,1)}, u32[]{:S(2)}, u32[]{:S(2)}) collective-permute-start(bf16[2,136,1024]{2,1,0:T(8,128)(2,1)S(1)} %pad_maximum_fusion.q0_ref.q_ref), channel_id=1, source_target_pairs={{0,64},{1,9},{2,66},{3,11},{4,68},{5,13},{6,70},{7,15},{8,72},{9,1... | collective-permute-start | bytes 1671176 | tf_op jit(solution)/shard_map/ppermute | solution.py:62
  21.1 39.4 %copy-start.1 = (bf16[2048,256]{1,0:T(8,128)(2,1)}, bf16[2048,256]{1,0:T(8,128)(2,1)S(1)}, u32[]{:S(2)}) copy-start(bf16[2048,256]{1,0:T(8,128)(2,1)S(1)} %collective-permute-done.5.kv2_ref) | copy-start | bytes 3145732
  37.5 13.8 %collective-permute-start.6 = (bf16[1024,256]{1,0:T(8,128)(2,1)}, bf16[1024,256]{1,0:T(8,128)(2,1)S(1)}, u32[]{:S(2)}, u32[]{:S(2)}) collective-permute-start(bf16[1024,256]{1,0:T(8,128)(2,1)} %slice.49), channel_id=1, source_target_pairs={{0,12},{1,97},{2,14},{3,99},{4,0},{5,101},{6,2},{7,103},{8,4},{9,1... | collective-permute-start | bytes 1572872 | tf_op jit(solution)/shard_map/ppermute | solution.py:62
  40.8 10.6 %collective-permute-start.7 = (bf16[1024,256]{1,0:T(8,128)(2,1)}, bf16[1024,256]{1,0:T(8,128)(2,1)S(1)}, u32[]{:S(2)}, u32[]{:S(2)}) collective-permute-start(bf16[1024,256]{1,0:T(8,128)(2,1)} %slice.50), channel_id=1, source_target_pairs={{0,4},{1,33},{2,6},{3,35},{4,8},{5,37},{6,10},{7,39},{8,12},{9,41}... | collective-permute-start | bytes 1572872 | tf_op jit(solution)/shard_map/ppermute | solution.py:62
  54.8 14.2 %collective-permute-start.10 = (bf16[2,2,136,512]{3,2,1,0:T(8,128)(2,1)S(1)}, bf16[2,2,136,512]{3,2,1,0:T(8,128)(2,1)S(1)}, u32[]{:S(2)}, u32[]{:S(2)}) collective-permute-start(bf16[2,2,136,512]{3,2,1,0:T(8,128)(2,1)S(1)} %late.6), channel_id=1, source_target_pairs={{0,96},{1,13},{2,98},{3,15},{4,100},{5,1},{6,102},{7,3},{8,104},{9... | collective-permute-start | bytes 1671176 | tf_op jit(solution)/shard_map/ppermute | solution.py:62
  58.2 17.0 %collective-permute-start.9 = (bf16[2,2,136,512]{3,2,1,0:T(8,128)(2,1)S(1)}, bf16[2,2,136,512]{3,2,1,0:T(8,128)(2,1)S(1)}, u32[]{:S(2)}, u32[]{:S(2)}) collective-permute-start(bf16[2,2,136,512]{3,2,1,0:T(8,128)(2,1)S(1)} %late.5), channel_id=1, source_target_pairs={{0,32},{1,5},{2,34},{3,7},{4,36},{5,9},{6,38},{7,11},{8,40},{9,13}... | collective-permute-start | bytes 1671176 | tf_op jit(solution)/shard_map/ppermute | solution.py:62
  60.5 15.4 %copy-start.3 = (bf16[128,256]{1,0:T(8,128)(2,1)S(1)}, bf16[128,256]{1,0:T(8,128)(2,1)}, u32[]{:S(2)}) copy-start(bf16[128,256]{1,0:T(8,128)(2,1)} %k_ref.2) | copy-start | bytes 196612
  60.5 15.4 %copy-start.4 = (bf16[128,256]{1,0:T(8,128)(2,1)S(1)}, bf16[128,256]{1,0:T(8,128)(2,1)}, u32[]{:S(2)}) copy-start(bf16[128,256]{1,0:T(8,128)(2,1)} %v_ref.2) | copy-start | bytes 196612
  60.5 27.6 %copy-start = (bf16[128,1024]{1,0:T(8,128)(2,1)S(1)}, bf16[128,1024]{1,0:T(8,128)(2,1)}, u32[]{:S(2)}) copy-start(bf16[128,1024]{1,0:T(8,128)(2,1)} %q_ref.3) | copy-start | bytes 786436
  63.9 11.3 %collective-permute-start.8 = (bf16[2,2,136,512]{3,2,1,0:T(8,128)(2,1)S(1)}, bf16[2,2,136,512]{3,2,1,0:T(8,128)(2,1)S(1)}, u32[]{:S(2)}, u32[]{:S(2)}) collective-permute-start(bf16[2,2,136,512]{3,2,1,0:T(8,128)(2,1)S(1)} %late.4), channel_id=1, source_target_pairs={{0,64},{1,9},{2,66},{3,11},{4,68},{5,13},{6,70},{7,15},{8,72},{9,1... | collective-permute-start | bytes 1671176 | tf_op jit(solution)/shard_map/ppermute | solution.py:62
  64.8 1.2 %copy-start.2 = (bf16[2048,256]{1,0:T(8,128)(2,1)S(1)}, bf16[2048,256]{1,0:T(8,128)(2,1)}, u32[]{:S(2)}) copy-start(bf16[2048,256]{1,0:T(8,128)(2,1)} %copy-done.1) | copy-start | bytes 3145732
  75.5 13.6 %collective-permute-start.11 = (bf16[2,136,512]{2,1,0:T(8,128)(2,1)S(1)}, bf16[2,136,512]{2,1,0:T(8,128)(2,1)S(1)}, u32[]{:S(2)}, u32[]{:S(2)}) collective-permute-start(bf16[2,136,512]{2,1,0:T(8,128)(2,1)S(1)} %join.1), channel_id=1, source_target_pairs={{0,16},{1,17},{2,18},{3,19},{4,20},{5,21},{6,22},{7,23},{8,24},{9,... | collective-permute-start | bytes 835592 | tf_op jit(solution)/shard_map/ppermute | solution.py:62
  75.9 12.2 %collective-permute-start.12 = (bf16[128,512]{1,0:T(8,128)(2,1)S(1)}, bf16[128,512]{1,0:T(8,128)(2,1)S(1)}, u32[]{:S(2)}, u32[]{:S(2)}) collective-permute-start(bf16[128,512]{1,0:T(8,128)(2,1)S(1)} %pad_maximum_fusion.1), channel_id=1, source_target_pairs={{0,4},{1,5},{2,6},{3,7},{4,8},{5,9},{6,10},{7,11},{8,12},{9,13},{1... | collective-permute-start | bytes 393224 | tf_op jit(solution)/shard_map/ppermute | solution.py:62
  94.0 2.0 %collective-permute-start.13 = (bf16[2,32,4096]{2,1,0:T(8,128)(2,1)S(1)}, bf16[2,32,4096]{2,1,0:T(8,128)(2,1)S(1)}, u32[]{:S(2)}, u32[]{:S(2)}) collective-permute-start(bf16[2,32,4096]{2,1,0:T(8,128)(2,1)S(1)} %get-tuple-element.64), channel_id=1, source_target_pairs={{0,1},{1,0},{2,3},{3,2},{4,5},{5,4},{6,7},{7,6},{8,9},{9,8},{10,11... | collective-permute-start | bytes 1572872 | tf_op jit(solution)/shard_map/ppermute | solution.py:62
  96.1 8.9 %collective-permute-start.14 = (bf16[32,4096]{1,0:T(8,128)(2,1)S(1)}, bf16[32,4096]{1,0:T(8,128)(2,1)S(1)}, u32[]{:S(2)}, u32[]{:S(2)}) collective-permute-start(bf16[32,4096]{1,0:T(8,128)(2,1)S(1)} %fusion.2), channel_id=1, source_target_pairs={{0,2},{1,3},{2,0},{3,1},{4,6},{5,7},{6,4},{7,5},{8,10},{9,11},{10,... | collective-permute-start | bytes 786440 | tf_op jit(solution)/shard_map/ppermute | solution.py:62

commit v3 on v2

--- a/solution.py
+++ b/solution.py
@@ -129,10 +129,11 @@
     return top, mixture[HD : HD + 1], mixture[0:HD]
 
 
-def early_kernel(tab_ref, q0_ref, q1_ref, q2_ref, q3_ref, kv0_ref, kv1_ref, *out_refs):
-    kvs = [(r, r, CB_DEV * BLOCK) for r in (kv0_ref, kv1_ref)]
-    for i, q_ref in enumerate((q0_ref, q1_ref, q2_ref, q3_ref)):
-        o_ref, s_ref = out_refs[2 * i : 2 * i + 2]
+def early_kernel(count, tab_ref, turn_ref, kv0_ref, kv1_ref, kv2_ref, *refs):
+    kvs = [(r, r, CB_DEV * BLOCK) for r in (kv0_ref, kv1_ref, kv2_ref)]
+    refs[-1][...] = turn_ref[...]
+    for i, q_ref in enumerate(refs[:count]):
+        o_ref, s_ref = refs[count + 2 * i : count + 2 * i + 2]
         for y in range(NY):
             for h in range(KVL):
                 top, total, mixture = attend(tab_ref.at[i], q_ref, kvs, 0, y, h)
@@ -141,18 +142,21 @@
                 s_ref[y, h, 1:2, :] = total
 
 
-def late_kernel(tab_ref, q_ref, kv2_ref, k3_ref, v3_ref, m_ref, s_ref, o_ref):
-    kvs = [(kv2_ref, kv2_ref, CB_DEV * BLOCK), (k3_ref, v3_ref, 0)]
-    for y in range(NY):
-        for h in range(KVL):
-            top, total, mixture = attend(tab_ref, q_ref, kvs, 2, y, h)
-            top0, total0 = s_ref[y, h, 0:1, :], s_ref[y, h, 1:2, :]
-            peak = jnp.maximum(top, top0)
-            share, share0 = jnp.exp(top - peak), jnp.exp(top0 - peak)
-            total = total * share + total0 * share0
-            inverse = 1.0 / total
-            o_ref[y, h, 0:HD, :] = (mixture * (share * inverse) + m_ref[y, h] * (share0 * inverse)).astype(BF)
-            o_ref[y, h, HD:ROWS, :] = packed_sum(peak + jnp.log(total))
+def late_kernel(count, tab_ref, k3_ref, v3_ref, *refs):
+    kvs = [(k3_ref, v3_ref, 0)]
+    inputs, outputs = refs[: 3 * count], refs[3 * count :]
+    for i, o_ref in enumerate(outputs):
+        q_ref, m_ref, s_ref = inputs[3 * i : 3 * i + 3]
+        for y in range(NY):
+            for h in range(KVL):
+                top, total, mixture = attend(tab_ref.at[i], q_ref, kvs, 3, y, h)
+                top0, total0 = s_ref[y, h, 0:1, :], s_ref[y, h, 1:2, :]
+                peak = jnp.maximum(top, top0)
+                share, share0 = jnp.exp(top - peak), jnp.exp(top0 - peak)
+                total = total * share + total0 * share0
+                inverse = 1.0 / total
+                o_ref[y, h, 0:HD, :] = (mixture * (share * inverse) + m_ref[y, h] * (share0 * inverse)).astype(BF)
+                o_ref[y, h, HD:ROWS, :] = packed_sum(peak + jnp.log(total))
 
 
 def stretch_kernel(first_ref, q_ref, k_ref, v_ref, prev_ref, o_ref, l_ref):
@@ -202,24 +206,24 @@
         o_ref[h, HD:ROWS, :] = packed_sum(level)
 
 
-def last_kernel(
-    place_ref, a_ref, b_ref, c_ref, d_ref, e_ref, s_ref, l_ref, w_ref, theirs_ref, mine_ref, att_ref, w_buf, sems
-):
-    chunks = sems.shape[0]
-    width = w_buf.shape[1] // chunks
-    copies = [
-        pltpu.make_async_copy(
-            w_ref.at[:, i * width : (i + 1) * width], w_buf.at[:, i * width : (i + 1) * width], sems.at[i]
-        )
-        for i in range(chunks)
-    ]
-    for copy in copies:
-        copy.start()
+def home_kernel(a_ref, b_ref, c_ref, d_ref, s_ref, l_ref, w_ref, o_ref, v_ref, copy_ref, sem):
+    copy = pltpu.make_async_copy(w_ref, copy_ref, sem)
+    copy.start()
     parts = (a_ref, b_ref, c_ref, d_ref)
     for h in range(KVL):
-        mixtures = [p[0, h, 0:HD, :].astype(F32) for p in parts] + [e_ref[h, 0:HD, :].astype(F32), s_ref[h]]
-        levels = [level_of(p[0, h, HD:ROWS, :]) for p in parts] + [level_of(e_ref[h, HD:ROWS, :]), l_ref[h, 0:1, :]]
-        mixture, _ = joined(mixtures, levels)
+        mixtures = [p[0, h, 0:HD, :].astype(F32) for p in parts] + [s_ref[h]]
+        levels = [level_of(p[0, h, HD:ROWS, :]) for p in parts] + [l_ref[h, 0:1, :]]
+        mixture, level = joined(mixtures, levels)
+        o_ref[h] = mixture
+        v_ref[h] = jnp.broadcast_to(level, (8, COLS))
+    copy.wait()
+
+
+def last_kernel(place_ref, m_ref, v_ref, e_ref, w_ref, theirs_ref, mine_ref, att_ref):
+    for h in range(KVL):
+        mixture, _ = joined(
+            [m_ref[h], e_ref[h, 0:HD, :].astype(F32)], [v_ref[h, 0:1, :], level_of(e_ref[h, HD:ROWS, :])]
+        )
         for m in range(GROUP):
             c = (h * GROUP + m) * HD
             att_ref[:, c : c + HD] = mixture[:, m * BLOCK : (m + 1) * BLOCK].T.astype(BF)
@@ -228,10 +232,9 @@
     order = [(1 - half, 1 - core), (half, 1 - core), (1 - half, core), (half, core)]
     rows = [att_ref[pl.ds(pl.multiple_of((a * CORES + b) * share, share), share), :] for a, b in order]
     rows = jnp.concatenate(rows, axis=0)
-    for n in range(chunks):
-        cols = slice(n * width, (n + 1) * width)
-        copies[n].wait()
-        product = nn(rows, w_buf[:, cols])
+    for n in range(4):
+        cols = slice(n * w_ref.shape[1] // 4, (n + 1) * w_ref.shape[1] // 4)
+        product = nn(rows, w_ref[:, cols])
         for i in range(HALVES):
             theirs_ref[i, :, cols] = product[i * share : (i + 1) * share].astype(BF)
             mine_ref[i, :, cols] = product[(HALVES + i) * share : (HALVES + i + 1) * share]
@@ -275,57 +278,82 @@
     after, before = send(kv, pairs_along(-1, True)), send(kv, pairs_along(1, True))
     asked_all = [asked_pair] + [send(asked_pair, pairs_along(-d, False)) for d in STEPS]
     half_keys, half_values = after[:rows], before[rows:]
-    asked_all, half_keys, half_values = lax.optimization_barrier((asked_all, half_keys, half_values))
+    asked_pair, half_keys, half_values = lax.optimization_barrier((asked_pair, half_keys, half_values))
     far_keys = send(half_keys, pairs_along(-1, True))
     far_values = send(half_values, pairs_along(1, True))
 
     steps = jnp.array((0,) + STEPS, jnp.int32)
     owners = jnp.where(core == 0, ctx - z + (z + steps) % NZ, ctx + ((x + steps) % NX - x) * NY * NZ)
-    lists = jnp.stack([a[:, BLOCK : BLOCK + KVL, None, :sel] for a in asked_all]).astype(jnp.int32)
-    inside = lists // CB_DEV == owners[:, None]
-    slot = lists % CB_DEV
-    table = jnp.stack(
-        [jnp.min(jnp.where(inside, slot, CB_DEV), axis=-1), jnp.max(jnp.where(inside, slot, -1), axis=-1)], axis=-1
-    )
-    table = jnp.clip(table, 0, CB_DEV - 1)
-    begun = call(
-        early_kernel,
-        (shape((NY, KVL, HD, COLS), F32), shape((NY, KVL, 8, COLS), F32)) * 4,
-        smem=1,
-        n=6,
-        name="early",
-        cost=COST,
-    )(table, *asked_all, kv, after)
-    begun, keys_new, values_new = lax.optimization_barrier((begun, keys_new, values_new))
-
-    prev = send(jnp.concatenate([keys_new, values_new], axis=1), PAIRS_PREV)
+
+    def begin(asked, turn):
+        lists = jnp.stack([a[:, BLOCK : BLOCK + KVL, None, :sel] for a in asked]).astype(jnp.int32)
+        inside = lists // CB_DEV == owners[:, None]
+        slot = lists % CB_DEV
+        table = jnp.stack(
+            [jnp.min(jnp.where(inside, slot, CB_DEV), axis=-1), jnp.max(jnp.where(inside, slot, -1), axis=-1)], axis=-1
+        )
+        table = jnp.clip(table, 0, CB_DEV - 1)
+        n = len(asked)
+        *begun, turn = call(
+            functools.partial(early_kernel, n),
+            (shape((NY, KVL, HD, COLS), F32), shape((NY, KVL, 8, COLS), F32)) * n + (shape((8, HD), F32),),
+            smem=1,
+            n=4 + n,
+            name="early",
+            cost=pl.CostEstimate(flops=0, transcendentals=0, bytes_accessed=1024),
+        )(table, turn, kv, after, before, *asked)
+        return [(table[i], asked[i], *begun[2 * i : 2 * i + 2]) for i in range(n)], turn
+
+    begun, turn = begin([asked_pair], jnp.zeros((8, HD), F32))
+    rest, turn = lax.optimization_barrier((asked_all[1:], turn))
+    ended, turn = begin(rest, turn)
+    begun = begun + ended
+
+    parts = []
+    for group in ((3,), (1,), (2, 0)):
+        inputs = [a for i in group for a in begun[i][1:]]
+        partials = call(
+            functools.partial(late_kernel, len(group)),
+            (shape((NY, KVL, ROWS, COLS), BF),) * len(group),
+            smem=1,
+            n=2 + len(inputs),
+            name="late",
+            cost=COST,
+        )(jnp.stack([begun[i][0] for i in group]), far_keys, far_values, *inputs)
+        parts += [p if i == 0 else send(p, pairs_along(((0,) + STEPS)[i], False)) for i, p in zip(group, partials)]
+    stretch_rows = jnp.concatenate([keys_new, values_new], axis=1)
+    prev = send(stretch_rows, PAIRS_PREV)
+    other = call(functools.partial(join_kernel, 1), shape((KVL, ROWS, COLS), BF), n=4, name="join")(*parts)
+    other, prev = lax.optimization_barrier((other, prev))
     local = call(
         stretch_kernel, (shape((KVL, HD, COLS), F32), shape((KVL, 8, COLS), F32)), smem=1, n=4, name="stretch"
     )(jnp.minimum(ctx, 1).reshape(1), queries, keys_new, values_new, prev)
-
-    parts = []
-    for i in (3, 1, 2, 0):
-        part = call(late_kernel, shape((NY, KVL, ROWS, COLS), BF), smem=1, n=6, name="late", cost=COST)(
-            table[i], asked_all[i], before, far_keys, far_values, begun[2 * i], begun[2 * i + 1]
-        )
-        parts.append(part if i == 0 else send(part, pairs_along(((0,) + STEPS)[i], False)))
-    other = call(functools.partial(join_kernel, 1), shape((KVL, ROWS, COLS), BF), n=4, name="join")(*parts)
     other = send(other, PAIRS_Y)
+    *home, weight = call(
+        home_kernel,
+        (
+            shape((KVL, HD, COLS), F32),
+            shape((KVL, 8, COLS), F32),
+            shape(out_weight.shape, BF),
+        ),
+        n=6,
+        hbm=1,
+        name="home",
+        scratch=[pltpu.SemaphoreType.DMA],
+        memory=16,
+        cost=COST,
+    )(*parts, *local, pltpu.with_memory_space_constraint(out_weight, pltpu.HBM))
 
     share, width = BLOCK // (HALVES * CORES), out_weight.shape[1]
     theirs, mine = call(
         last_kernel,
         (shape((HALVES, share, width), BF), shape((HALVES, share, width), F32)),
         smem=1,
-        n=7,
-        hbm=1,
+        n=4,
         name="last",
-        scratch=[
-            pltpu.VMEM((BLOCK, KVL * COLS), BF),
-            pltpu.VMEM(out_weight.shape, BF),
-            pltpu.SemaphoreType.DMA((4,)),
-        ],
-    )(jnp.stack([half, core]), *parts, other, *local, pltpu.with_memory_space_constraint(out_weight, pltpu.HBM))
+        scratch=[pltpu.VMEM((BLOCK, KVL * COLS), BF)],
+        memory=16,
+    )(jnp.stack([half, core]), *home, other, weight)
     chip = mine + send(theirs, PAIRS_CORE).astype(F32)
     return (chip[1] + send(chip[0].astype(BF), PAIRS_LO).astype(F32)).astype(BF)
 

time: 107 us -> 103 us (0.963)
  waiting for transfers between devices: 45.2 us -> 30.7 us
  starting transfers between devices: 20.4 us -> 25.4 us
  Pallas kernels: 31.9 us -> 34.7 us
  other arithmetic: 2.51 us -> 5.19 us
    ppermute x15, waiting for transfers between devices: 45.2 us -> 30.7 us  [send(): return lax.ppermute(array, AXES, pairs)]
    pallas_call x5 -> x6, Pallas kernels: 23.4 us -> 30.1 us  [the longest x2 14.9 us: begin(): call(functools.partial(early_kernel, n), (shape((NY, KVL, HD, COLS), F32)...]
    ppermute x15, starting transfers between devices: 20.4 us -> 25.4 us  [send(): return lax.ppermute(array, AXES, pairs)]
    pallas_call x1, Pallas kernels: 4.89 us -> 2 us  [shards(): call(last_kernel, (shape((HALVES, share, width), BF), shape((HALVES, shar...]
    another operation x1, other arithmetic: 0.05 us -> 1.81 us  [shards(): asked_pair = jnp.stack([asked, send(asked, PAIRS_Y)])]
  transfers between devices with their start and end apart: 15 -> 15, of which waited for: 8 -> 8; matrix products, arithmetic and copies ran while one was open for 2% -> 8% of each run, Pallas kernels for 20% -> 28%
where the time goes in v3:
time: 103 us; the launch traced here: 102 us
  Pallas kernels  34.7 us (34%)
  waiting for transfers between devices  30.7 us (30%)
  starting transfers between devices  25.4 us (25%)
  local copies, waits for them, and re-layouts  5.35 us (5%)
  other arithmetic  5.19 us (5%)
    ppermute x15, waiting for transfers between devices, send(): return lax.ppermute(array, AXES, pairs)  30.7 us
    ppermute x15, starting transfers between devices, send(): return lax.ppermute(array, AXES, pairs)  25.4 us
    pallas_call x2, Pallas kernels, begin(): call(functools.partial(early_kernel, n), (shape((NY, KVL, HD, COLS), F32)...  14.9 us
    pallas_call x3, Pallas kernels, shards(): call(functools.partial(late_kernel, len(group)), (shape((NY, KVL, ROWS, C...  11.9 us
    pallas_call x1, Pallas kernels, shards(): call(home_kernel, (shape((KVL, HD, COLS), F32), shape((KVL, 8, COLS), F32...  3.39 us
  transfers between devices with their start and end apart: 15, of which 8 were waited for; matrix products, arithmetic and copies ran while one was open for 8% of the time, Pallas kernels for 28%

profile of v3, /device:TPU:16, one launch (start us, length us, event | category | flops | bytes accessed | tf_op | source)
XLA Modules:
  0.0 101.6 jit_solution(11404976978028288161)
XLA Ops:
  2.0 2.0 %collective-permute-start.5 = (bf16[2048,256]{1,0:T(8,128)(2,1)S(1)}, bf16[2048,256]{1,0:T(8,128)(2,1)S(1)}, u32[]{:S(2)}, u32[]{:S(2)}) collective-permute-start(bf16[2048,256]{1,0:T(8,128)(2,1)S(1)} %get-tuple-element.35.kv0_ref), channel_id=1, source_target_pairs={{0,4},{1,33},{2,6},{3,35},{4,8},{5,37},{6,10},{7,39},{8,12},{9,41}... | collective-permute-start | bytes 3145736 | tf_op jit(solution)/shard_map/ppermute | solution.py:62
  4.0 2.2 %collective-permute-start.4 = (bf16[2048,256]{1,0:T(8,128)(2,1)S(1)}, bf16[2048,256]{1,0:T(8,128)(2,1)S(1)}, u32[]{:S(2)}, u32[]{:S(2)}) collective-permute-start(bf16[2048,256]{1,0:T(8,128)(2,1)S(1)} %get-tuple-element.35.kv0_ref), channel_id=1, source_target_pairs={{0,12},{1,97},{2,14},{3,99},{4,0},{5,101},{6,2},{7,103},{8,4},{9,1... | collective-permute-start | bytes 3145736 | tf_op jit(solution)/shard_map/ppermute | solution.py:62
  6.6 8.2 %collective-permute-done = bf16[136,1024]{1,0:T(8,128)(2,1)} collective-permute-done((bf16[136,1024]{1,0:T(8,128)(2,1)S(1)}, bf16[136,1024]{1,0:T(8,128)(2,1)}, u32[]{:S(2)}, u32[]{:S(2)}) %collective-permute-start) | collective-permute-done | bytes 278560 | tf_op jit(solution)/shard_map/ppermute | solution.py:62
  14.8 1.8 %pad_maximum_fusion.refs_0_.refs_3_ = bf16[2,136,1024]{2,1,0:T(8,128)(2,1)} fusion(bf16[1,136,1024]{2,1,0:T(8,128)(2,1)} %bitcast.4, bf16[1,136,1024]{2,1,0:T(8,128)(2,1)S(1)} %bitcast.24), kind=kLoop, calls=%fused_computation.1 | loop fusion | flops 278528 | bytes 1114112 | tf_op jit(solution)/shard_map/stack | solution.py:277
  16.6 2.6 %collective-permute-start.3 = (bf16[2,136,1024]{2,1,0:T(8,128)(2,1)}, bf16[2,136,1024]{2,1,0:T(8,128)(2,1)}, u32[]{:S(2)}, u32[]{:S(2)}) collective-permute-start(bf16[2,136,1024]{2,1,0:T(8,128)(2,1)} %pad_maximum_fusion.refs_0_.refs_3_), channel_id=1, source_target_pairs={{0,64},{1,9},{2,66},{3,11},{4,68},{5,13},{6,70},{7,15},{8,72},{9,1... | collective-permute-start | bytes 1671176 | tf_op jit(solution)/shard_map/ppermute | solution.py:62
  19.8 2.6 %collective-permute-start.1 = (bf16[2,136,1024]{2,1,0:T(8,128)(2,1)}, bf16[2,136,1024]{2,1,0:T(8,128)(2,1)}, u32[]{:S(2)}, u32[]{:S(2)}) collective-permute-start(bf16[2,136,1024]{2,1,0:T(8,128)(2,1)} %pad_maximum_fusion.refs_0_.refs_3_), channel_id=1, source_target_pairs={{0,96},{1,13},{2,98},{3,15},{4,100},{5,1},{6,102},{7,3},{8,104},{9... | collective-permute-start | bytes 1671176 | tf_op jit(solution)/shard_map/ppermute | solution.py:62
  26.1 3.2 %collective-permute-start.6 = (bf16[1024,256]{1,0:T(8,128)(2,1)}, bf16[1024,256]{1,0:T(8,128)(2,1)}, u32[]{:S(2)}, u32[]{:S(2)}) collective-permute-start(bf16[1024,256]{1,0:T(8,128)(2,1)} %slice.45), channel_id=1, source_target_pairs={{0,12},{1,97},{2,14},{3,99},{4,0},{5,101},{6,2},{7,103},{8,4},{9,1... | collective-permute-start | bytes 1572872 | tf_op jit(solution)/shard_map/ppermute | solution.py:62
  29.4 4.1 %early.2 = (f32[2,2,128,512]{3,2,1,0:T(8,128)S(1)}, f32[2,2,8,512]{3,2,1,0:T(8,128)S(1)}, f32[8,128]{1,0:T(8,128)S(1)}) custom-call(s32[1,2,2,4,2]{4,3,2,1,0:T(4,128)S(1)} %add_clamp_fusion.1.tab_ref, f32[8,128]{1,0:T(8,128)S(1)} %broadcast_in_dim.42.turn_ref, bf16[2048,256]{1,0:T(8,128)(2,1)S(1)} %get-tuple-element.35.kv0_ref, ...), custom_call_target="tpu_custom_call" | custom-call | bytes 1024 | tf_op jit(solution)/shard_map/early/pallas_call | solution.py:297
  34.6 2.6 %collective-permute-done.2.refs_1_.refs_0_ = bf16[2,136,1024]{2,1,0:T(8,128)(2,1)} collective-permute-done((bf16[2,136,1024]{2,1,0:T(8,128)(2,1)}, bf16[2,136,1024]{2,1,0:T(8,128)(2,1)}, u32[]{:S(2)}, u32[]{:S(2)}) %collective-permute-start.2) | collective-permute-done | bytes 557088 | tf_op jit(solution)/shard_map/ppermute | solution.py:62
  40.6 10.7 %early.3 = (f32[2,2,128,512]{3,2,1,0:T(8,128)S(1)}, f32[2,2,8,512]{3,2,1,0:T(8,128)S(1)}, f32[2,2,128,512]{3,2,1,0:T(8,128)S(1)}, f32[2,2,8,512]{3,2,1,0:T(8,128...) custom-call(s32[3,2,2,4,2]{4,3,2,1,0:T(4,128)S(1)} %add_clamp_fusion.tab_ref, ...), custom_call_target="tpu_custom_call" | custom-call | bytes 1024 | tf_op jit(solution)/shard_map/early/pallas_call | solution.py:297
  51.4 3.3 %late.3 = bf16[2,2,136,512]{3,2,1,0:T(8,128)(2,1)S(1)} custom-call(s32[1,2,2,4,2]{4,3,2,1,0:T(4,128)S(1)} %get-tuple-element.71.tab_ref, bf16[1024,256]{1,0:T(8,128)(2,1)} %collective-permute-done.6.k3_ref, bf16[1024,256]{1,0:T(8,128)(2,1)} %collective-permute-done.7.v3_ref, bf16[2,136,1024]{2,1,0:T(8,128)(2,1)} %collective-permute-done.3.refs_2_.refs_0_, ...), custom_call_target="tpu_custom_call" | custom-call | flops 2147483648 | bytes 12582912 | tf_op jit(solution)/shard_map/late/pallas_call | solution.py:315
  54.7 3.1 %collective-permute-start.8 = (bf16[2,2,136,512]{3,2,1,0:T(8,128)(2,1)S(1)}, bf16[2,2,136,512]{3,2,1,0:T(8,128)(2,1)S(1)}, u32[]{:S(2)}, u32[]{:S(2)}) collective-permute-start(bf16[2,2,136,512]{3,2,1,0:T(8,128)(2,1)S(1)} %late.3), channel_id=1, source_target_pairs={{0,64},{1,9},{2,66},{3,11},{4,68},{5,13},{6,70},{7,15},{8,72},{9,1... | collective-permute-start | bytes 1671176 | tf_op jit(solution)/shard_map/ppermute | solution.py:62
  57.9 3.9 %late.4 = bf16[2,2,136,512]{3,2,1,0:T(8,128)(2,1)} custom-call(s32[1,2,2,4,2]{4,3,2,1,0:T(4,128)S(1)} %get-tuple-element.70.tab_ref, bf16[1024,256]{1,0:T(8,128)(2,1)} %collective-permute-done.6.k3_ref, bf16[1024,256]{1,0:T(8,128)(2,1)} %collective-permute-done.7.v3_ref, bf16[2,136,1024]{2,1,0:T(8,128)(2,1)} %collective-permute-done.1.refs_0_, ...), custom_call_target="tpu_custom_call" | custom-call | flops 2147483648 | bytes 12582912 | tf_op jit(solution)/shard_map/late/pallas_call | solution.py:315
  61.8 1.5 %collective-permute-start.9 = (bf16[2,2,136,512]{3,2,1,0:T(8,128)(2,1)}, bf16[2,2,136,512]{3,2,1,0:T(8,128)(2,1)S(1)}, u32[]{:S(2)}, u32[]{:S(2)}) collective-permute-start(bf16[2,2,136,512]{3,2,1,0:T(8,128)(2,1)} %late.4), channel_id=1, source_target_pairs={{0,32},{1,5},{2,34},{3,7},{4,36},{5,9},{6,38},{7,11},{8,40},{9,13}... | collective-permute-start | bytes 1671176 | tf_op jit(solution)/shard_map/ppermute | solution.py:62
  63.3 4.7 %late.5 = (bf16[2,2,136,512]{3,2,1,0:T(8,128)(2,1)}, bf16[2,2,136,512]{3,2,1,0:T(8,128)(2,1)S(1)}) custom-call(s32[2,2,2,4,2]{4,3,2,1,0:T(4,128)S(1)} %pad_add_fusion.tab_ref, bf16[1024,256]{1,0:T(8,128)(2,1)} %collective-permute-done.6.k3_ref, bf16[1024,256]{1,0:T(8,128)(2,1)} %collective-permute-done.7.v3_ref, ...), custom_call_target="tpu_custom_call" | custom-call | flops 2147483648 | bytes 12582912 | tf_op jit(solution)/shard_map/late/pallas_call | solution.py:315
  67.9 1.8 %collective-permute-start.10 = (bf16[2,2,136,512]{3,2,1,0:T(8,128)(2,1)}, bf16[2,2,136,512]{3,2,1,0:T(8,128)(2,1)S(1)}, u32[]{:S(2)}, u32[]{:S(2)}) collective-permute-start(bf16[2,2,136,512]{3,2,1,0:T(8,128)(2,1)} %get-tuple-element.52), channel_id=1, source_target_pairs={{0,96},{1,13},{2,98},{3,15},{4,100},{5,1},{6,102},{7,3},{8,104},{9... | collective-permute-start | bytes 1671176 | tf_op jit(solution)/shard_map/ppermute | solution.py:62
  69.8 3.9 %collective-permute-start.11 = (bf16[128,512]{1,0:T(8,128)(2,1)S(1)}, bf16[128,512]{1,0:T(8,128)(2,1)S(1)}, u32[]{:S(2)}, u32[]{:S(2)}) collective-permute-start(bf16[128,512]{1,0:T(8,128)(2,1)S(1)} %pad_maximum_fusion.1), channel_id=1, source_target_pairs={{0,4},{1,5},{2,6},{3,7},{4,8},{5,9},{6,10},{7,11},{8,12},{9,13},{1... | collective-permute-start | bytes 393224 | tf_op jit(solution)/shard_map/ppermute | solution.py:62
  73.8 4.0 %collective-permute-done.10.refs_2_.c_ref = bf16[2,2,136,512]{3,2,1,0:T(8,128)(2,1)S(1)} collective-permute-done((bf16[2,2,136,512]{3,2,1,0:T(8,128)(2,1)}, bf16[2,2,136,512]{3,2,1,0:T(8,128)(2,1)S(1)}, u32[]{:S(2)}, u32[]{:S(2)}) %collective-permute-start.10) | collective-permute-done | bytes 557088 | tf_op jit(solution)/shard_map/ppermute | solution.py:62
  78.0 2.2 %collective-permute-done.11.prev_ref = bf16[128,512]{1,0:T(8,128)(2,1)S(1)} collective-permute-done((bf16[128,512]{1,0:T(8,128)(2,1)S(1)}, bf16[128,512]{1,0:T(8,128)(2,1)S(1)}, u32[]{:S(2)}, u32[]{:S(2)}) %collective-permute-start.11) | collective-permute-done | bytes 131104 | tf_op jit(solution)/shard_map/ppermute | solution.py:62
  81.3 3.4 %home.1 = (f32[2,128,512]{2,1,0:T(8,128)S(1)}, f32[2,8,512]{2,1,0:T(8,128)S(1)}, bf16[1024,4096]{1,0:T(8,128)(2,1)S(1)}) custom-call(bf16[2,2,136,512]{3,2,1,0:T(8,128)(2,1)S(1)} %collective-permute-done.8.refs_0_.a_ref, bf16[2,2,136,512]{3,2,1,0:T(8,128)(2,1)S(1)} %collective-permute-done.9.refs_1_.b_ref, ...), custom_call_target="tpu_custom_call" | custom-call | flops 2147483648 | bytes 12582912 | tf_op jit(solution)/shard_map/home/pallas_call | solution.py:332
  84.7 3.6 %collective-permute-done.12.e_ref = bf16[2,136,512]{2,1,0:T(8,128)(2,1)S(1)} collective-permute-done((bf16[2,136,512]{2,1,0:T(8,128)(2,1)S(1)}, bf16[2,136,512]{2,1,0:T(8,128)(2,1)S(1)}, u32[]{:S(2)}, u32[]{:S(2)}) %collective-permute-start.12) | collective-permute-done | bytes 278560 | tf_op jit(solution)/shard_map/ppermute | solution.py:62
  88.3 2.0 %last.1 = (bf16[2,32,4096]{2,1,0:T(8,128)(2,1)S(1)}, f32[2,32,4096]{2,1,0:T(8,128)S(1)}) custom-call(s32[2]{0:T(128)S(1)} %pad_add_fusion.1.place_ref, f32[2,128,512]{2,1,0:T(8,128)S(1)} %get-tuple-element.57.m_ref, f32[2,8,512]{2,1,0:T(8,128)S(1)} %get-tuple-element.58.v_ref, bf16[2,136,512]{2,1,0:T(8,128)(2,1)S(1)} %collective-permute-done.12.e_ref, ...), custom_call_target="tpu_custom_call" | custom-call | tf_op jit(solution)/shard_map/last/pallas_call | solution.py:348
  90.4 1.9 %collective-permute-done.13 = bf16[2,32,4096]{2,1,0:T(8,128)(2,1)S(1)} collective-permute-done((bf16[2,32,4096]{2,1,0:T(8,128)(2,1)S(1)}, bf16[2,32,4096]{2,1,0:T(8,128)(2,1)S(1)}, u32[]{:S(2)}, u32[]{:S(2)}) %collective-permute-start.13) | collective-permute-done | bytes 524320 | tf_op jit(solution)/shard_map/ppermute | solution.py:62
  93.8 7.1 %collective-permute-done.14 = bf16[32,4096]{1,0:T(8,128)(2,1)S(1)} collective-permute-done((bf16[32,4096]{1,0:T(8,128)(2,1)S(1)}, bf16[32,4096]{1,0:T(8,128)(2,1)S(1)}, u32[]{:S(2)}, u32[]{:S(2)}) %collective-permute-start.14) | collective-permute-done | bytes 262176 | tf_op jit(solution)/shard_map/ppermute | solution.py:62
  (52 shorter events, 14.7 us)
Async XLA Ops:
  0.0 0.7 copy-start.3
  2.0 21.1 %collective-permute-start.5 = (bf16[2048,256]{1,0:T(8,128)(2,1)S(1)}, bf16[2048,256]{1,0:T(8,128)(2,1)S(1)}, u32[]{:S(2)}, u32[]{:S(2)}) collective-permute-start(bf16[2048,256]{1,0:T(8,128)(2,1)S(1)} %get-tuple-element.35.kv0_ref), channel_id=1, source_target_pairs={{0,4},{1,33},{2,6},{3,35},{4,8},{5,37},{6,10},{7,39},{8,12},{9,41}... | collective-permute-start | bytes 3145736 | tf_op jit(solution)/shard_map/ppermute | solution.py:62
  4.0 20.0 %collective-permute-start.4 = (bf16[2048,256]{1,0:T(8,128)(2,1)S(1)}, bf16[2048,256]{1,0:T(8,128)(2,1)S(1)}, u32[]{:S(2)}, u32[]{:S(2)}) collective-permute-start(bf16[2048,256]{1,0:T(8,128)(2,1)S(1)} %get-tuple-element.35.kv0_ref), channel_id=1, source_target_pairs={{0,12},{1,97},{2,14},{3,99},{4,0},{5,101},{6,2},{7,103},{8,4},{9,1... | collective-permute-start | bytes 3145736 | tf_op jit(solution)/shard_map/ppermute | solution.py:62
  6.2 8.6 %collective-permute-start = (bf16[136,1024]{1,0:T(8,128)(2,1)S(1)}, bf16[136,1024]{1,0:T(8,128)(2,1)}, u32[]{:S(2)}, u32[]{:S(2)}) collective-permute-start(bf16[136,1024]{1,0:T(8,128)(2,1)S(1)} %get-tuple-element.34), channel_id=1, source_target_pairs={{0,16},{1,17},{2,18},{3,19},{4,20},{5,21},{6,22},{7,23},{8,24},{9,... | collective-permute-start | bytes 835592 | tf_op jit(solution)/shard_map/ppermute | solution.py:62
  16.6 17.9 %collective-permute-start.3 = (bf16[2,136,1024]{2,1,0:T(8,128)(2,1)}, bf16[2,136,1024]{2,1,0:T(8,128)(2,1)}, u32[]{:S(2)}, u32[]{:S(2)}) collective-permute-start(bf16[2,136,1024]{2,1,0:T(8,128)(2,1)} %pad_maximum_fusion.refs_0_.refs_3_), channel_id=1, source_target_pairs={{0,64},{1,9},{2,66},{3,11},{4,68},{5,13},{6,70},{7,15},{8,72},{9,1... | collective-permute-start | bytes 1671176 | tf_op jit(solution)/shard_map/ppermute | solution.py:62
  19.2 18.0 %collective-permute-start.2 = (bf16[2,136,1024]{2,1,0:T(8,128)(2,1)}, bf16[2,136,1024]{2,1,0:T(8,128)(2,1)}, u32[]{:S(2)}, u32[]{:S(2)}) collective-permute-start(bf16[2,136,1024]{2,1,0:T(8,128)(2,1)} %pad_maximum_fusion.refs_0_.refs_3_), channel_id=1, source_target_pairs={{0,32},{1,5},{2,34},{3,7},{4,36},{5,9},{6,38},{7,11},{8,40},{9,13}... | collective-permute-start | bytes 1671176 | tf_op jit(solution)/shard_map/ppermute | solution.py:62
  19.8 18.4 %collective-permute-start.1 = (bf16[2,136,1024]{2,1,0:T(8,128)(2,1)}, bf16[2,136,1024]{2,1,0:T(8,128)(2,1)}, u32[]{:S(2)}, u32[]{:S(2)}) collective-permute-start(bf16[2,136,1024]{2,1,0:T(8,128)(2,1)} %pad_maximum_fusion.refs_0_.refs_3_), channel_id=1, source_target_pairs={{0,96},{1,13},{2,98},{3,15},{4,100},{5,1},{6,102},{7,3},{8,104},{9... | collective-permute-start | bytes 1671176 | tf_op jit(solution)/shard_map/ppermute | solution.py:62
  26.1 25.3 %collective-permute-start.6 = (bf16[1024,256]{1,0:T(8,128)(2,1)}, bf16[1024,256]{1,0:T(8,128)(2,1)}, u32[]{:S(2)}, u32[]{:S(2)}) collective-permute-start(bf16[1024,256]{1,0:T(8,128)(2,1)} %slice.45), channel_id=1, source_target_pairs={{0,12},{1,97},{2,14},{3,99},{4,0},{5,101},{6,2},{7,103},{8,4},{9,1... | collective-permute-start | bytes 1572872 | tf_op jit(solution)/shard_map/ppermute | solution.py:62
  29.3 22.0 %collective-permute-start.7 = (bf16[1024,256]{1,0:T(8,128)(2,1)}, bf16[1024,256]{1,0:T(8,128)(2,1)}, u32[]{:S(2)}, u32[]{:S(2)}) collective-permute-start(bf16[1024,256]{1,0:T(8,128)(2,1)} %slice.46), channel_id=1, source_target_pairs={{0,4},{1,33},{2,6},{3,35},{4,8},{5,37},{6,10},{7,39},{8,12},{9,41}... | collective-permute-start | bytes 1572872 | tf_op jit(solution)/shard_map/ppermute | solution.py:62
  33.5 1.0 copy-start.4
  51.3 11.9 %copy-start.5 = (f32[2,2,128,512]{3,2,1,0:T(8,128)S(1)}, f32[2,2,128,512]{3,2,1,0:T(8,128)}, u32[]{:S(2)}) copy-start(f32[2,2,128,512]{3,2,1,0:T(8,128)} %copy-done.4) | copy-start | bytes 3145732
  54.7 15.0 %copy-start.1 = (bf16[128,256]{1,0:T(8,128)(2,1)S(1)}, bf16[128,256]{1,0:T(8,128)(2,1)}, u32[]{:S(2)}) copy-start(bf16[128,256]{1,0:T(8,128)(2,1)} %k_ref.3) | copy-start | bytes 196612
  54.7 15.0 %copy-start.2 = (bf16[128,256]{1,0:T(8,128)(2,1)S(1)}, bf16[128,256]{1,0:T(8,128)(2,1)}, u32[]{:S(2)}) copy-start(bf16[128,256]{1,0:T(8,128)(2,1)} %v_ref.3) | copy-start | bytes 196612
  54.7 19.0 %collective-permute-start.8 = (bf16[2,2,136,512]{3,2,1,0:T(8,128)(2,1)S(1)}, bf16[2,2,136,512]{3,2,1,0:T(8,128)(2,1)S(1)}, u32[]{:S(2)}, u32[]{:S(2)}) collective-permute-start(bf16[2,2,136,512]{3,2,1,0:T(8,128)(2,1)S(1)} %late.3), channel_id=1, source_target_pairs={{0,64},{1,9},{2,66},{3,11},{4,68},{5,13},{6,70},{7,15},{8,72},{9,1... | collective-permute-start | bytes 1671176 | tf_op jit(solution)/shard_map/ppermute | solution.py:62
  57.9 22.4 %copy-start = (bf16[128,1024]{1,0:T(8,128)(2,1)S(1)}, bf16[128,1024]{1,0:T(8,128)(2,1)}, u32[]{:S(2)}) copy-start(bf16[128,1024]{1,0:T(8,128)(2,1)} %q_ref.3) | copy-start | bytes 786436
  61.8 12.0 %collective-permute-start.9 = (bf16[2,2,136,512]{3,2,1,0:T(8,128)(2,1)}, bf16[2,2,136,512]{3,2,1,0:T(8,128)(2,1)S(1)}, u32[]{:S(2)}, u32[]{:S(2)}) collective-permute-start(bf16[2,2,136,512]{3,2,1,0:T(8,128)(2,1)} %late.4), channel_id=1, source_target_pairs={{0,32},{1,5},{2,34},{3,7},{4,36},{5,9},{6,38},{7,11},{8,40},{9,13}... | collective-permute-start | bytes 1671176 | tf_op jit(solution)/shard_map/ppermute | solution.py:62
  67.9 9.8 %collective-permute-start.10 = (bf16[2,2,136,512]{3,2,1,0:T(8,128)(2,1)}, bf16[2,2,136,512]{3,2,1,0:T(8,128)(2,1)S(1)}, u32[]{:S(2)}, u32[]{:S(2)}) collective-permute-start(bf16[2,2,136,512]{3,2,1,0:T(8,128)(2,1)} %get-tuple-element.52), channel_id=1, source_target_pairs={{0,96},{1,13},{2,98},{3,15},{4,100},{5,1},{6,102},{7,3},{8,104},{9... | collective-permute-start | bytes 1671176 | tf_op jit(solution)/shard_map/ppermute | solution.py:62
  69.8 10.5 %collective-permute-start.11 = (bf16[128,512]{1,0:T(8,128)(2,1)S(1)}, bf16[128,512]{1,0:T(8,128)(2,1)S(1)}, u32[]{:S(2)}, u32[]{:S(2)}) collective-permute-start(bf16[128,512]{1,0:T(8,128)(2,1)S(1)} %pad_maximum_fusion.1), channel_id=1, source_target_pairs={{0,4},{1,5},{2,6},{3,7},{4,8},{5,9},{6,10},{7,11},{8,12},{9,13},{1... | collective-permute-start | bytes 393224 | tf_op jit(solution)/shard_map/ppermute | solution.py:62
  80.3 8.1 %collective-permute-start.12 = (bf16[2,136,512]{2,1,0:T(8,128)(2,1)S(1)}, bf16[2,136,512]{2,1,0:T(8,128)(2,1)S(1)}, u32[]{:S(2)}, u32[]{:S(2)}) collective-permute-start(bf16[2,136,512]{2,1,0:T(8,128)(2,1)S(1)} %join.1), channel_id=1, source_target_pairs={{0,16},{1,17},{2,18},{3,19},{4,20},{5,21},{6,22},{7,23},{8,24},{9,... | collective-permute-start | bytes 835592 | tf_op jit(solution)/shard_map/ppermute | solution.py:62
  90.3 2.0 %collective-permute-start.13 = (bf16[2,32,4096]{2,1,0:T(8,128)(2,1)S(1)}, bf16[2,32,4096]{2,1,0:T(8,128)(2,1)S(1)}, u32[]{:S(2)}, u32[]{:S(2)}) collective-permute-start(bf16[2,32,4096]{2,1,0:T(8,128)(2,1)S(1)} %get-tuple-element.62), channel_id=1, source_target_pairs={{0,1},{1,0},{2,3},{3,2},{4,5},{5,4},{6,7},{7,6},{8,9},{9,8},{10,11... | collective-permute-start | bytes 1572872 | tf_op jit(solution)/shard_map/ppermute | solution.py:62
  92.4 8.4 %collective-permute-start.14 = (bf16[32,4096]{1,0:T(8,128)(2,1)S(1)}, bf16[32,4096]{1,0:T(8,128)(2,1)S(1)}, u32[]{:S(2)}, u32[]{:S(2)}) collective-permute-start(bf16[32,4096]{1,0:T(8,128)(2,1)S(1)} %fusion.2), channel_id=1, source_target_pairs={{0,2},{1,3},{2,0},{3,1},{4,6},{5,7},{6,4},{7,5},{8,10},{9,11},{10,... | collective-permute-start | bytes 786440 | tf_op jit(solution)/shard_map/ppermute | solution.py:62

commit v4 on v3

--- a/solution.py
+++ b/solution.py
@@ -82,17 +82,20 @@
     return jnp.concatenate([hi.astype(F32), mid.astype(F32), low.astype(F32), jnp.zeros((5, COLS), F32)], axis=0).astype(BF)
 
 
-def pack_kernel(list_ref, q_ref, k_ref, v_ref, asked_ref, kv_ref, v_buf, sems):
+def pack_kernel(list_ref, q_ref, k_ref, v_ref, asked_ref, kv_ref, v_buf, list_buf, sems):
     rows = k_ref.shape[0]
     copies = [
         pltpu.make_async_copy(q_ref, asked_ref.at[0:BLOCK], sems.at[0]),
         pltpu.make_async_copy(v_ref, v_buf, sems.at[1]),
         pltpu.make_async_copy(k_ref, kv_ref.at[0:rows], sems.at[2]),
+        pltpu.make_async_copy(list_ref, list_buf, sems.at[3]),
     ]
     for copy in copies:
         copy.start()
     asked_ref[BLOCK : BLOCK + 8, :] = jnp.zeros((8, asked_ref.shape[1]), BF)
-    asked_ref[BLOCK : BLOCK + KVL, 0 : list_ref.shape[1]] = list_ref[...].astype(F32).astype(BF)
+    copies[3].wait()
+    for h in range(KVL):
+        asked_ref[BLOCK + h : BLOCK + h + 1, 0 : list_ref.shape[2]] = list_buf[h].astype(F32).astype(BF)
     copies[1].wait()
     for b in range(CB_DEV):
         for h in range(KVL):
@@ -269,16 +272,20 @@
     asked, kv = call(
         pack_kernel,
         (shape((queries.shape[0] + 8, queries.shape[1]), BF), shape((2 * rows, cache_keys.shape[1]), BF)),
-        n=1,
-        hbm=3,
+        hbm=4,
         name="pack",
-        scratch=[pltpu.VMEM(cache_values.shape, BF), pltpu.SemaphoreType.DMA((3,))],
-    )(block_list.reshape(KVL, sel), *(pltpu.with_memory_space_constraint(a, pltpu.HBM) for a in (queries, cache_keys, cache_values)))
+        scratch=[
+            pltpu.VMEM(cache_values.shape, BF),
+            pltpu.VMEM(block_list.shape, jnp.int32),
+            pltpu.SemaphoreType.DMA((4,)),
+        ],
+    )(*(pltpu.with_memory_space_constraint(a, pltpu.HBM) for a in (block_list, queries, cache_keys, cache_values)))
     asked_pair = jnp.stack([asked, send(asked, PAIRS_Y)])
     after, before = send(kv, pairs_along(-1, True)), send(kv, pairs_along(1, True))
     asked_all = [asked_pair] + [send(asked_pair, pairs_along(-d, False)) for d in STEPS]
     half_keys, half_values = after[:rows], before[rows:]
-    asked_pair, half_keys, half_values = lax.optimization_barrier((asked_pair, half_keys, half_values))
+    prev = send(jnp.concatenate([keys_new, values_new], axis=1), PAIRS_PREV)
+    asked_pair, half_keys, half_values, prev = lax.optimization_barrier((asked_pair, half_keys, half_values, prev))
     far_keys = send(half_keys, pairs_along(-1, True))
     far_values = send(half_values, pairs_along(1, True))
 
@@ -310,7 +317,7 @@
     begun = begun + ended
 
     parts = []
-    for group in ((3,), (1,), (2, 0)):
+    for group in ((3, 1), (2, 0)):
         inputs = [a for i in group for a in begun[i][1:]]
         partials = call(
             functools.partial(late_kernel, len(group)),
@@ -321,10 +328,7 @@
             cost=COST,
         )(jnp.stack([begun[i][0] for i in group]), far_keys, far_values, *inputs)
         parts += [p if i == 0 else send(p, pairs_along(((0,) + STEPS)[i], False)) for i, p in zip(group, partials)]
-    stretch_rows = jnp.concatenate([keys_new, values_new], axis=1)
-    prev = send(stretch_rows, PAIRS_PREV)
     other = call(functools.partial(join_kernel, 1), shape((KVL, ROWS, COLS), BF), n=4, name="join")(*parts)
-    other, prev = lax.optimization_barrier((other, prev))
     local = call(
         stretch_kernel, (shape((KVL, HD, COLS), F32), shape((KVL, 8, COLS), F32)), smem=1, n=4, name="stretch"
     )(jnp.minimum(ctx, 1).reshape(1), queries, keys_new, values_new, prev)

time: 103 us -> 99 us (0.961)
  Pallas kernels: 34.7 us -> 32.7 us
  starting transfers between devices: 25.4 us -> 23.5 us
  other arithmetic: 5.19 us -> 6.71 us
    pallas_call x3 -> x2, Pallas kernels: 11.9 us -> 9.83 us  [shards(): call(functools.partial(late_kernel, len(group)), (shape((NY, KVL, ROWS, C...]
    ppermute x15, starting transfers between devices: 25.4 us -> 23.5 us  [send(): return lax.ppermute(array, AXES, pairs)]
    concatenate x1, other arithmetic: 0.01 us -> 1.53 us  [shards(): prev = send(jnp.concatenate([keys_new, values_new], axis=1), PAIRS_PREV)]
  transfers between devices with their start and end apart: 15 -> 15, of which waited for: 8 -> 8; matrix products, arithmetic and copies ran while one was open for 8% -> 7% of each run, Pallas kernels for 28% -> 24%
where the time goes in v4:
time: 99 us; the launch traced here: 98.6 us
  Pallas kernels  32.7 us (33%)
  waiting for transfers between devices  30.8 us (31%)
  starting transfers between devices  23.5 us (24%)
  other arithmetic  6.71 us (7%)
  local copies, waits for them, and re-layouts  4.64 us (5%)
    ppermute x15, waiting for transfers between devices, send(): return lax.ppermute(array, AXES, pairs)  30.8 us
    ppermute x15, starting transfers between devices, send(): return lax.ppermute(array, AXES, pairs)  23.5 us
    pallas_call x2, Pallas kernels, begin(): call(functools.partial(early_kernel, n), (shape((NY, KVL, HD, COLS), F32)...  14.9 us
    pallas_call x2, Pallas kernels, shards(): call(functools.partial(late_kernel, len(group)), (shape((NY, KVL, ROWS, C...  9.83 us
    pallas_call x1, Pallas kernels, shards(): call(home_kernel, (shape((KVL, HD, COLS), F32), shape((KVL, 8, COLS), F32...  3.39 us
  transfers between devices with their start and end apart: 15, of which 8 were waited for; matrix products, arithmetic and copies ran while one was open for 7% of the time, Pallas kernels for 24%

profile of v4, /device:TPU:16, one launch (start us, length us, event | category | flops | bytes accessed | tf_op | source)
XLA Modules:
  0.0 98.6 jit_solution(4372371165860086408)
XLA Ops:
  0.0 1.4 %pack.1 = (bf16[136,1024]{1,0:T(8,128)(2,1)S(1)}, bf16[2048,256]{1,0:T(8,128)(2,1)S(1)}) custom-call(s32[2,1,64]{2,1,0:T(1,128)} %list_ref.1, bf16[128,1024]{1,0:T(8,128)(2,1)} %q_ref.3, bf16[1024,256]{1,0:T(8,128)(2,1)} %k_ref.2, bf16[1024,256]{1,0:T(8,128)(2,1)} %v_ref.2), custom_call_target="tpu_custom_call" | custom-call | tf_op jit(solution)/shard_map/pack/pallas_call | solution.py:272
  1.4 4.1 %collective-permute-start.4 = (bf16[2048,256]{1,0:T(8,128)(2,1)S(1)}, bf16[2048,256]{1,0:T(8,128)(2,1)S(1)}, u32[]{:S(2)}, u32[]{:S(2)}) collective-permute-start(bf16[2048,256]{1,0:T(8,128)(2,1)S(1)} %get-tuple-element.36.kv0_ref), channel_id=1, source_target_pairs={{0,12},{1,97},{2,14},{3,99},{4,0},{5,101},{6,2},{7,103},{8,4},{9,1... | collective-permute-start | bytes 3145736 | tf_op jit(solution)/shard_map/ppermute | solution.py:62
  5.8 1.5 %pad_maximum_fusion.1 = bf16[128,512]{1,0:T(8,128)(2,1)} fusion(bf16[128,256]{1,0:T(8,128)(2,1)} %v_ref.3, bf16[128,256]{1,0:T(8,128)(2,1)} %k_ref.3), kind=kLoop, calls=%fused_computation.7 | loop fusion | flops 262144 | bytes 262144 | tf_op jit(solution)/shard_map/concatenate | solution.py:287
  7.4 1.9 %collective-permute-start.6 = (bf16[128,512]{1,0:T(8,128)(2,1)}, bf16[128,512]{1,0:T(8,128)(2,1)S(1)}, u32[]{:S(2)}, u32[]{:S(2)}) collective-permute-start(bf16[128,512]{1,0:T(8,128)(2,1)} %pad_maximum_fusion.1), channel_id=1, source_target_pairs={{0,4},{1,5},{2,6},{3,7},{4,8},{5,9},{6,10},{7,11},{8,12},{9,13},{1... | collective-permute-start | bytes 393224 | tf_op jit(solution)/shard_map/ppermute | solution.py:62
  9.3 4.6 %collective-permute-done = bf16[136,1024]{1,0:T(8,128)(2,1)} collective-permute-done((bf16[136,1024]{1,0:T(8,128)(2,1)S(1)}, bf16[136,1024]{1,0:T(8,128)(2,1)}, u32[]{:S(2)}, u32[]{:S(2)}) %collective-permute-start) | collective-permute-done | bytes 278560 | tf_op jit(solution)/shard_map/ppermute | solution.py:62
  13.9 1.8 %pad_maximum_fusion.refs_0_.refs_3_ = bf16[2,136,1024]{2,1,0:T(8,128)(2,1)} fusion(bf16[1,136,1024]{2,1,0:T(8,128)(2,1)} %bitcast.3, bf16[1,136,1024]{2,1,0:T(8,128)(2,1)S(1)} %bitcast.23), kind=kLoop, calls=%fused_computation.1 | loop fusion | flops 278528 | bytes 1114112 | tf_op jit(solution)/shard_map/stack | solution.py:283
  15.7 3.0 %collective-permute-start.1 = (bf16[2,136,1024]{2,1,0:T(8,128)(2,1)}, bf16[2,136,1024]{2,1,0:T(8,128)(2,1)}, u32[]{:S(2)}, u32[]{:S(2)}) collective-permute-start(bf16[2,136,1024]{2,1,0:T(8,128)(2,1)} %pad_maximum_fusion.refs_0_.refs_3_), channel_id=1, source_target_pairs={{0,96},{1,13},{2,98},{3,15},{4,100},{5,1},{6,102},{7,3},{8,104},{9... | collective-permute-start | bytes 1671176 | tf_op jit(solution)/shard_map/ppermute | solution.py:62
  18.7 3.6 %collective-permute-start.3 = (bf16[2,136,1024]{2,1,0:T(8,128)(2,1)}, bf16[2,136,1024]{2,1,0:T(8,128)(2,1)}, u32[]{:S(2)}, u32[]{:S(2)}) collective-permute-start(bf16[2,136,1024]{2,1,0:T(8,128)(2,1)} %pad_maximum_fusion.refs_0_.refs_3_), channel_id=1, source_target_pairs={{0,64},{1,9},{2,66},{3,11},{4,68},{5,13},{6,70},{7,15},{8,72},{9,1... | collective-permute-start | bytes 1671176 | tf_op jit(solution)/shard_map/ppermute | solution.py:62
  23.8 3.0 %collective-permute-done.5.kv2_ref = bf16[2048,256]{1,0:T(8,128)(2,1)S(1)} collective-permute-done((bf16[2048,256]{1,0:T(8,128)(2,1)S(1)}, bf16[2048,256]{1,0:T(8,128)(2,1)S(1)}, u32[]{:S(2)}, u32[]{:S(2)}) %collective-permute-start.5) | collective-permute-done | bytes 1048608 | tf_op jit(solution)/shard_map/ppermute | solution.py:62
  29.0 4.1 %early.2 = (f32[2,2,128,512]{3,2,1,0:T(8,128)S(1)}, f32[2,2,8,512]{3,2,1,0:T(8,128)S(1)}, f32[8,128]{1,0:T(8,128)S(1)}) custom-call(s32[1,2,2,4,2]{4,3,2,1,0:T(4,128)S(1)} %add_clamp_fusion.1.tab_ref, f32[8,128]{1,0:T(8,128)S(1)} %broadcast_in_dim.42.turn_ref, bf16[2048,256]{1,0:T(8,128)(2,1)S(1)} %get-tuple-element.36.kv0_ref, ...), custom_call_target="tpu_custom_call" | custom-call | bytes 1024 | tf_op jit(solution)/shard_map/early/pallas_call | solution.py:304
  34.2 1.6 %collective-permute-done.2.refs_1_.refs_0_ = bf16[2,136,1024]{2,1,0:T(8,128)(2,1)} collective-permute-done((bf16[2,136,1024]{2,1,0:T(8,128)(2,1)}, bf16[2,136,1024]{2,1,0:T(8,128)(2,1)}, u32[]{:S(2)}, u32[]{:S(2)}) %collective-permute-start.2) | collective-permute-done | bytes 557088 | tf_op jit(solution)/shard_map/ppermute | solution.py:62
  38.0 5.5 %collective-permute-start.7 = (bf16[1024,256]{1,0:T(8,128)(2,1)}, bf16[1024,256]{1,0:T(8,128)(2,1)S(1)}, u32[]{:S(2)}, u32[]{:S(2)}) collective-permute-start(bf16[1024,256]{1,0:T(8,128)(2,1)} %slice.45), channel_id=1, source_target_pairs={{0,12},{1,97},{2,14},{3,99},{4,0},{5,101},{6,2},{7,103},{8,4},{9,1... | collective-permute-start | bytes 1572872 | tf_op jit(solution)/shard_map/ppermute | solution.py:62
  43.6 10.7 %early.3 = (f32[2,2,128,512]{3,2,1,0:T(8,128)S(1)}, f32[2,2,8,512]{3,2,1,0:T(8,128)S(1)}, f32[2,2,128,512]{3,2,1,0:T(8,128)S(1)}, f32[2,2,8,512]{3,2,1,0:T(8,128...) custom-call(s32[3,2,2,4,2]{4,3,2,1,0:T(4,128)S(1)} %add_clamp_fusion.tab_ref, ...), custom_call_target="tpu_custom_call" | custom-call | bytes 1024 | tf_op jit(solution)/shard_map/early/pallas_call | solution.py:304
  54.5 5.2 %late.2 = (bf16[2,2,136,512]{3,2,1,0:T(8,128)(2,1)}, bf16[2,2,136,512]{3,2,1,0:T(8,128)(2,1)}) custom-call(s32[2,2,2,4,2]{4,3,2,1,0:T(4,128)S(1)} %pad_add_fusion.tab_ref, bf16[1024,256]{1,0:T(8,128)(2,1)S(1)} %collective-permute-done.7.k3_ref, bf16[1024,256]{1,0:T(8,128)(2,1)S(1)} %collective-permute-done.8.v3_ref, ...), custom_call_target="tpu_custom_call" | custom-call | flops 2147483648 | bytes 12582912 | tf_op jit(solution)/shard_map/late/pallas_call | solution.py:322
  60.5 4.6 %late.3 = (bf16[2,2,136,512]{3,2,1,0:T(8,128)(2,1)}, bf16[2,2,136,512]{3,2,1,0:T(8,128)(2,1)S(1)}) custom-call(s32[2,2,2,4,2]{4,3,2,1,0:T(4,128)S(1)} %pad_add_fusion.1.tab_ref, bf16[1024,256]{1,0:T(8,128)(2,1)S(1)} %collective-permute-done.7.k3_ref, bf16[1024,256]{1,0:T(8,128)(2,1)S(1)} %collective-permute-done.8.v3_ref, ...), custom_call_target="tpu_custom_call" | custom-call | flops 2147483648 | bytes 12582912 | tf_op jit(solution)/shard_map/late/pallas_call | solution.py:322
  65.1 2.7 %collective-permute-start.11 = (bf16[2,2,136,512]{3,2,1,0:T(8,128)(2,1)}, bf16[2,2,136,512]{3,2,1,0:T(8,128)(2,1)S(1)}, u32[]{:S(2)}, u32[]{:S(2)}) collective-permute-start(bf16[2,2,136,512]{3,2,1,0:T(8,128)(2,1)} %get-tuple-element.55), channel_id=1, source_target_pairs={{0,96},{1,13},{2,98},{3,15},{4,100},{5,1},{6,102},{7,3},{8,104},{9... | collective-permute-start | bytes 1671176 | tf_op jit(solution)/shard_map/ppermute | solution.py:62
  67.8 3.2 %collective-permute-done.9.a_ref.refs_0_ = bf16[2,2,136,512]{3,2,1,0:T(8,128)(2,1)S(1)} collective-permute-done((bf16[2,2,136,512]{3,2,1,0:T(8,128)(2,1)}, bf16[2,2,136,512]{3,2,1,0:T(8,128)(2,1)S(1)}, u32[]{:S(2)}, u32[]{:S(2)}) %collective-permute-start.9) | collective-permute-done | bytes 557088 | tf_op jit(solution)/shard_map/ppermute | solution.py:62
  71.0 5.9 %collective-permute-done.10.b_ref.refs_1_ = bf16[2,2,136,512]{3,2,1,0:T(8,128)(2,1)S(1)} collective-permute-done((bf16[2,2,136,512]{3,2,1,0:T(8,128)(2,1)}, bf16[2,2,136,512]{3,2,1,0:T(8,128)(2,1)S(1)}, u32[]{:S(2)}, u32[]{:S(2)}) %collective-permute-start.10) | collective-permute-done | bytes 557088 | tf_op jit(solution)/shard_map/ppermute | solution.py:62
  78.3 3.4 %home.1 = (f32[2,128,512]{2,1,0:T(8,128)S(1)}, f32[2,8,512]{2,1,0:T(8,128)S(1)}, bf16[1024,4096]{1,0:T(8,128)(2,1)S(1)}) custom-call(bf16[2,2,136,512]{3,2,1,0:T(8,128)(2,1)S(1)} %collective-permute-done.9.a_ref.refs_0_, bf16[2,2,136,512]{3,2,1,0:T(8,128)(2,1)S(1)} %collective-permute-done.10.b_ref.refs_1_, ...), custom_call_target="tpu_custom_call" | custom-call | flops 2147483648 | bytes 12582912 | tf_op jit(solution)/shard_map/home/pallas_call | solution.py:336
  81.7 3.6 %collective-permute-done.12.e_ref = bf16[2,136,512]{2,1,0:T(8,128)(2,1)S(1)} collective-permute-done((bf16[2,136,512]{2,1,0:T(8,128)(2,1)S(1)}, bf16[2,136,512]{2,1,0:T(8,128)(2,1)S(1)}, u32[]{:S(2)}, u32[]{:S(2)}) %collective-permute-start.12) | collective-permute-done | bytes 278560 | tf_op jit(solution)/shard_map/ppermute | solution.py:62
  85.3 2.0 %last.1 = (bf16[2,32,4096]{2,1,0:T(8,128)(2,1)S(1)}, f32[2,32,4096]{2,1,0:T(8,128)S(1)}) custom-call(s32[2]{0:T(128)S(1)} %pad_add_fusion.2.place_ref, f32[2,128,512]{2,1,0:T(8,128)S(1)} %get-tuple-element.60.m_ref, f32[2,8,512]{2,1,0:T(8,128)S(1)} %get-tuple-element.61.v_ref, bf16[2,136,512]{2,1,0:T(8,128)(2,1)S(1)} %collective-permute-done.12.e_ref, ...), custom_call_target="tpu_custom_call" | custom-call | tf_op jit(solution)/shard_map/last/pallas_call | solution.py:352
  87.4 1.9 %collective-permute-done.13 = bf16[2,32,4096]{2,1,0:T(8,128)(2,1)S(1)} collective-permute-done((bf16[2,32,4096]{2,1,0:T(8,128)(2,1)S(1)}, bf16[2,32,4096]{2,1,0:T(8,128)(2,1)S(1)}, u32[]{:S(2)}, u32[]{:S(2)}) %collective-permute-start.13) | collective-permute-done | bytes 524320 | tf_op jit(solution)/shard_map/ppermute | solution.py:62
  89.4 1.4 %collective-permute-start.14 = (bf16[32,4096]{1,0:T(8,128)(2,1)S(1)}, bf16[32,4096]{1,0:T(8,128)(2,1)S(1)}, u32[]{:S(2)}, u32[]{:S(2)}) collective-permute-start(bf16[32,4096]{1,0:T(8,128)(2,1)S(1)} %fusion.2), channel_id=1, source_target_pairs={{0,2},{1,3},{2,0},{3,1},{4,6},{5,7},{6,4},{7,5},{8,10},{9,11},{10,... | collective-permute-start | bytes 786440 | tf_op jit(solution)/shard_map/ppermute | solution.py:62
  90.7 7.1 %collective-permute-done.14 = bf16[32,4096]{1,0:T(8,128)(2,1)S(1)} collective-permute-done((bf16[32,4096]{1,0:T(8,128)(2,1)S(1)}, bf16[32,4096]{1,0:T(8,128)(2,1)S(1)}, u32[]{:S(2)}, u32[]{:S(2)}) %collective-permute-start.14) | collective-permute-done | bytes 262176 | tf_op jit(solution)/shard_map/ppermute | solution.py:62
  (50 shorter events, 10.6 us)
Async XLA Ops:
  1.4 17.3 %collective-permute-start.4 = (bf16[2048,256]{1,0:T(8,128)(2,1)S(1)}, bf16[2048,256]{1,0:T(8,128)(2,1)S(1)}, u32[]{:S(2)}, u32[]{:S(2)}) collective-permute-start(bf16[2048,256]{1,0:T(8,128)(2,1)S(1)} %get-tuple-element.36.kv0_ref), channel_id=1, source_target_pairs={{0,12},{1,97},{2,14},{3,99},{4,0},{5,101},{6,2},{7,103},{8,4},{9,1... | collective-permute-start | bytes 3145736 | tf_op jit(solution)/shard_map/ppermute | solution.py:62
  5.5 21.4 %collective-permute-start.5 = (bf16[2048,256]{1,0:T(8,128)(2,1)S(1)}, bf16[2048,256]{1,0:T(8,128)(2,1)S(1)}, u32[]{:S(2)}, u32[]{:S(2)}) collective-permute-start(bf16[2048,256]{1,0:T(8,128)(2,1)S(1)} %get-tuple-element.36.kv0_ref), channel_id=1, source_target_pairs={{0,4},{1,33},{2,6},{3,35},{4,8},{5,37},{6,10},{7,39},{8,12},{9,41}... | collective-permute-start | bytes 3145736 | tf_op jit(solution)/shard_map/ppermute | solution.py:62
  5.5 8.4 %collective-permute-start = (bf16[136,1024]{1,0:T(8,128)(2,1)S(1)}, bf16[136,1024]{1,0:T(8,128)(2,1)}, u32[]{:S(2)}, u32[]{:S(2)}) collective-permute-start(bf16[136,1024]{1,0:T(8,128)(2,1)S(1)} %get-tuple-element.35), channel_id=1, source_target_pairs={{0,16},{1,17},{2,18},{3,19},{4,20},{5,21},{6,22},{7,23},{8,24},{9,... | collective-permute-start | bytes 835592 | tf_op jit(solution)/shard_map/ppermute | solution.py:62
  7.4 20.3 %collective-permute-start.6 = (bf16[128,512]{1,0:T(8,128)(2,1)}, bf16[128,512]{1,0:T(8,128)(2,1)S(1)}, u32[]{:S(2)}, u32[]{:S(2)}) collective-permute-start(bf16[128,512]{1,0:T(8,128)(2,1)} %pad_maximum_fusion.1), channel_id=1, source_target_pairs={{0,4},{1,5},{2,6},{3,7},{4,8},{5,9},{6,10},{7,11},{8,12},{9,13},{1... | collective-permute-start | bytes 393224 | tf_op jit(solution)/shard_map/ppermute | solution.py:62
  15.7 18.4 %collective-permute-start.1 = (bf16[2,136,1024]{2,1,0:T(8,128)(2,1)}, bf16[2,136,1024]{2,1,0:T(8,128)(2,1)}, u32[]{:S(2)}, u32[]{:S(2)}) collective-permute-start(bf16[2,136,1024]{2,1,0:T(8,128)(2,1)} %pad_maximum_fusion.refs_0_.refs_3_), channel_id=1, source_target_pairs={{0,96},{1,13},{2,98},{3,15},{4,100},{5,1},{6,102},{7,3},{8,104},{9... | collective-permute-start | bytes 1671176 | tf_op jit(solution)/shard_map/ppermute | solution.py:62
  18.7 17.0 %collective-permute-start.2 = (bf16[2,136,1024]{2,1,0:T(8,128)(2,1)}, bf16[2,136,1024]{2,1,0:T(8,128)(2,1)}, u32[]{:S(2)}, u32[]{:S(2)}) collective-permute-start(bf16[2,136,1024]{2,1,0:T(8,128)(2,1)} %pad_maximum_fusion.refs_0_.refs_3_), channel_id=1, source_target_pairs={{0,32},{1,5},{2,34},{3,7},{4,36},{5,9},{6,38},{7,11},{8,40},{9,13}... | collective-permute-start | bytes 1671176 | tf_op jit(solution)/shard_map/ppermute | solution.py:62
  18.7 17.0 %collective-permute-start.3 = (bf16[2,136,1024]{2,1,0:T(8,128)(2,1)}, bf16[2,136,1024]{2,1,0:T(8,128)(2,1)}, u32[]{:S(2)}, u32[]{:S(2)}) collective-permute-start(bf16[2,136,1024]{2,1,0:T(8,128)(2,1)} %pad_maximum_fusion.refs_0_.refs_3_), channel_id=1, source_target_pairs={{0,64},{1,9},{2,66},{3,11},{4,68},{5,13},{6,70},{7,15},{8,72},{9,1... | collective-permute-start | bytes 1671176 | tf_op jit(solution)/shard_map/ppermute | solution.py:62
  33.2 1.0 %copy-start.3 = (f32[2,2,128,512]{3,2,1,0:T(8,128)}, f32[2,2,128,512]{3,2,1,0:T(8,128)S(1)}, u32[]{:S(2)}) copy-start(f32[2,2,128,512]{3,2,1,0:T(8,128)S(1)} %get-tuple-element.53.refs_4_) | copy-start | bytes 3145732
  38.0 22.5 %copy-start.4 = (f32[2,2,128,512]{3,2,1,0:T(8,128)S(1)}, f32[2,2,128,512]{3,2,1,0:T(8,128)}, u32[]{:S(2)}) copy-start(f32[2,2,128,512]{3,2,1,0:T(8,128)} %copy-done.3) | copy-start | bytes 3145732
  38.0 16.4 %collective-permute-start.7 = (bf16[1024,256]{1,0:T(8,128)(2,1)}, bf16[1024,256]{1,0:T(8,128)(2,1)S(1)}, u32[]{:S(2)}, u32[]{:S(2)}) collective-permute-start(bf16[1024,256]{1,0:T(8,128)(2,1)} %slice.45), channel_id=1, source_target_pairs={{0,12},{1,97},{2,14},{3,99},{4,0},{5,101},{6,2},{7,103},{8,4},{9,1... | collective-permute-start | bytes 1572872 | tf_op jit(solution)/shard_map/ppermute | solution.py:62
  43.5 10.9 %collective-permute-start.8 = (bf16[1024,256]{1,0:T(8,128)(2,1)}, bf16[1024,256]{1,0:T(8,128)(2,1)S(1)}, u32[]{:S(2)}, u32[]{:S(2)}) collective-permute-start(bf16[1024,256]{1,0:T(8,128)(2,1)} %slice.46), channel_id=1, source_target_pairs={{0,4},{1,33},{2,6},{3,35},{4,8},{5,37},{6,10},{7,39},{8,12},{9,41}... | collective-permute-start | bytes 1572872 | tf_op jit(solution)/shard_map/ppermute | solution.py:62
  54.4 22.9 %copy-start = (bf16[128,1024]{1,0:T(8,128)(2,1)S(1)}, bf16[128,1024]{1,0:T(8,128)(2,1)}, u32[]{:S(2)}) copy-start(bf16[128,1024]{1,0:T(8,128)(2,1)} %q_ref.3) | copy-start | bytes 786436
  54.4 22.9 %copy-start.1 = (bf16[128,256]{1,0:T(8,128)(2,1)S(1)}, bf16[128,256]{1,0:T(8,128)(2,1)}, u32[]{:S(2)}) copy-start(bf16[128,256]{1,0:T(8,128)(2,1)} %k_ref.3) | copy-start | bytes 196612
  54.4 22.9 %copy-start.2 = (bf16[128,256]{1,0:T(8,128)(2,1)S(1)}, bf16[128,256]{1,0:T(8,128)(2,1)}, u32[]{:S(2)}) copy-start(bf16[128,256]{1,0:T(8,128)(2,1)} %v_ref.3) | copy-start | bytes 196612
  59.6 11.4 %collective-permute-start.9 = (bf16[2,2,136,512]{3,2,1,0:T(8,128)(2,1)}, bf16[2,2,136,512]{3,2,1,0:T(8,128)(2,1)S(1)}, u32[]{:S(2)}, u32[]{:S(2)}) collective-permute-start(bf16[2,2,136,512]{3,2,1,0:T(8,128)(2,1)} %get-tuple-element.49), channel_id=1, source_target_pairs={{0,64},{1,9},{2,66},{3,11},{4,68},{5,13},{6,70},{7,15},{8,72},{9,1... | collective-permute-start | bytes 1671176 | tf_op jit(solution)/shard_map/ppermute | solution.py:62
  60.0 16.9 %collective-permute-start.10 = (bf16[2,2,136,512]{3,2,1,0:T(8,128)(2,1)}, bf16[2,2,136,512]{3,2,1,0:T(8,128)(2,1)S(1)}, u32[]{:S(2)}, u32[]{:S(2)}) collective-permute-start(bf16[2,2,136,512]{3,2,1,0:T(8,128)(2,1)} %get-tuple-element.50), channel_id=1, source_target_pairs={{0,32},{1,5},{2,34},{3,7},{4,36},{5,9},{6,38},{7,11},{8,40},{9,13}... | collective-permute-start | bytes 1671176 | tf_op jit(solution)/shard_map/ppermute | solution.py:62
  65.1 11.7 %collective-permute-start.11 = (bf16[2,2,136,512]{3,2,1,0:T(8,128)(2,1)}, bf16[2,2,136,512]{3,2,1,0:T(8,128)(2,1)S(1)}, u32[]{:S(2)}, u32[]{:S(2)}) collective-permute-start(bf16[2,2,136,512]{3,2,1,0:T(8,128)(2,1)} %get-tuple-element.55), channel_id=1, source_target_pairs={{0,96},{1,13},{2,98},{3,15},{4,100},{5,1},{6,102},{7,3},{8,104},{9... | collective-permute-start | bytes 1671176 | tf_op jit(solution)/shard_map/ppermute | solution.py:62
  77.1 8.1 %collective-permute-start.12 = (bf16[2,136,512]{2,1,0:T(8,128)(2,1)S(1)}, bf16[2,136,512]{2,1,0:T(8,128)(2,1)S(1)}, u32[]{:S(2)}, u32[]{:S(2)}) collective-permute-start(bf16[2,136,512]{2,1,0:T(8,128)(2,1)S(1)} %join.1), channel_id=1, source_target_pairs={{0,16},{1,17},{2,18},{3,19},{4,20},{5,21},{6,22},{7,23},{8,24},{9,... | collective-permute-start | bytes 835592 | tf_op jit(solution)/shard_map/ppermute | solution.py:62
  87.3 2.0 %collective-permute-start.13 = (bf16[2,32,4096]{2,1,0:T(8,128)(2,1)S(1)}, bf16[2,32,4096]{2,1,0:T(8,128)(2,1)S(1)}, u32[]{:S(2)}, u32[]{:S(2)}) collective-permute-start(bf16[2,32,4096]{2,1,0:T(8,128)(2,1)S(1)} %get-tuple-element.64), channel_id=1, source_target_pairs={{0,1},{1,0},{2,3},{3,2},{4,5},{5,4},{6,7},{7,6},{8,9},{9,8},{10,11... | collective-permute-start | bytes 1572872 | tf_op jit(solution)/shard_map/ppermute | solution.py:62
  89.4 8.4 %collective-permute-start.14 = (bf16[32,4096]{1,0:T(8,128)(2,1)S(1)}, bf16[32,4096]{1,0:T(8,128)(2,1)S(1)}, u32[]{:S(2)}, u32[]{:S(2)}) collective-permute-start(bf16[32,4096]{1,0:T(8,128)(2,1)S(1)} %fusion.2), channel_id=1, source_target_pairs={{0,2},{1,3},{2,0},{3,1},{4,6},{5,7},{6,4},{7,5},{8,10},{9,11},{10,... | collective-permute-start | bytes 786440 | tf_op jit(solution)/shard_map/ppermute | solution.py:62

commit v5 on v4

--- a/solution.py
+++ b/solution.py
@@ -117,9 +117,11 @@
         first, second = tab_ref[y, h, shard + s, 0], tab_ref[y, h, shard + s, 1]
         for j, b in enumerate((first, second)):
             row = pl.multiple_of(b * BLOCK, BLOCK)
-            scores.append(nt(keys[pl.ds(row, BLOCK), cols], q))
+            scores.append(keys[pl.ds(row, BLOCK), cols])
             values.append(turned_values[pl.ds(row + base, BLOCK), cols])
             offs.append(None if j == 0 else jnp.where(second == first, NEG, 0.0).astype(F32))
+    scores = nt(jnp.concatenate(scores, axis=0), q)
+    scores = [scores[i * BLOCK : (i + 1) * BLOCK] for i in range(len(offs))]
     tops = [
         jnp.max(t, axis=0, keepdims=True) if o is None else jnp.max(t, axis=0, keepdims=True) + o
         for t, o in zip(scores, offs)

time: 99 us -> 99 us (level)
  no operation moved by 1% of the time
where the time goes in v5:
time: 99 us; the launch traced here: 98.6 us
  Pallas kernels  32.6 us (33%)
  waiting for transfers between devices  30.9 us (31%)
  starting transfers between devices  23.5 us (24%)
  other arithmetic  6.71 us (7%)
  local copies, waits for them, and re-layouts  4.64 us (5%)
    ppermute x15, waiting for transfers between devices, send(): return lax.ppermute(array, AXES, pairs)  30.9 us
    ppermute x15, starting transfers between devices, send(): return lax.ppermute(array, AXES, pairs)  23.5 us
    pallas_call x2, Pallas kernels, begin(): call(functools.partial(early_kernel, n), (shape((NY, KVL, HD, COLS), F32)...  14.9 us
    pallas_call x2, Pallas kernels, shards(): call(functools.partial(late_kernel, len(group)), (shape((NY, KVL, ROWS, C...  9.78 us
    pallas_call x1, Pallas kernels, shards(): call(home_kernel, (shape((KVL, HD, COLS), F32), shape((KVL, 8, COLS), F32...  3.39 us
  transfers between devices with their start and end apart: 15, of which 8 were waited for; matrix products, arithmetic and copies ran while one was open for 7% of the time, Pallas kernels for 24%

profile of v5, /device:TPU:16, one launch (start us, length us, event | category | flops | bytes accessed | tf_op | source)
XLA Modules:
  0.0 98.6 jit_solution(17151896606192059409)
XLA Ops:
  0.0 1.4 %pack.1 = (bf16[136,1024]{1,0:T(8,128)(2,1)S(1)}, bf16[2048,256]{1,0:T(8,128)(2,1)S(1)}) custom-call(s32[2,1,64]{2,1,0:T(1,128)} %list_ref.1, bf16[128,1024]{1,0:T(8,128)(2,1)} %q_ref.3, bf16[1024,256]{1,0:T(8,128)(2,1)} %k_ref.2, bf16[1024,256]{1,0:T(8,128)(2,1)} %v_ref.2), custom_call_target="tpu_custom_call" | custom-call | tf_op jit(solution)/shard_map/pack/pallas_call | solution.py:274
  1.4 4.1 %collective-permute-start.4 = (bf16[2048,256]{1,0:T(8,128)(2,1)S(1)}, bf16[2048,256]{1,0:T(8,128)(2,1)S(1)}, u32[]{:S(2)}, u32[]{:S(2)}) collective-permute-start(bf16[2048,256]{1,0:T(8,128)(2,1)S(1)} %get-tuple-element.36.kv0_ref), channel_id=1, source_target_pairs={{0,12},{1,97},{2,14},{3,99},{4,0},{5,101},{6,2},{7,103},{8,4},{9,1... | collective-permute-start | bytes 3145736 | tf_op jit(solution)/shard_map/ppermute | solution.py:62
  5.8 1.5 %pad_maximum_fusion.1 = bf16[128,512]{1,0:T(8,128)(2,1)} fusion(bf16[128,256]{1,0:T(8,128)(2,1)} %v_ref.3, bf16[128,256]{1,0:T(8,128)(2,1)} %k_ref.3), kind=kLoop, calls=%fused_computation.7 | loop fusion | flops 262144 | bytes 262144 | tf_op jit(solution)/shard_map/concatenate | solution.py:289
  7.4 1.9 %collective-permute-start.6 = (bf16[128,512]{1,0:T(8,128)(2,1)}, bf16[128,512]{1,0:T(8,128)(2,1)S(1)}, u32[]{:S(2)}, u32[]{:S(2)}) collective-permute-start(bf16[128,512]{1,0:T(8,128)(2,1)} %pad_maximum_fusion.1), channel_id=1, source_target_pairs={{0,4},{1,5},{2,6},{3,7},{4,8},{5,9},{6,10},{7,11},{8,12},{9,13},{1... | collective-permute-start | bytes 393224 | tf_op jit(solution)/shard_map/ppermute | solution.py:62
  9.3 4.6 %collective-permute-done = bf16[136,1024]{1,0:T(8,128)(2,1)} collective-permute-done((bf16[136,1024]{1,0:T(8,128)(2,1)S(1)}, bf16[136,1024]{1,0:T(8,128)(2,1)}, u32[]{:S(2)}, u32[]{:S(2)}) %collective-permute-start) | collective-permute-done | bytes 278560 | tf_op jit(solution)/shard_map/ppermute | solution.py:62
  13.9 1.8 %pad_maximum_fusion.refs_0_.refs_3_ = bf16[2,136,1024]{2,1,0:T(8,128)(2,1)} fusion(bf16[1,136,1024]{2,1,0:T(8,128)(2,1)} %bitcast.3, bf16[1,136,1024]{2,1,0:T(8,128)(2,1)S(1)} %bitcast.23), kind=kLoop, calls=%fused_computation.1 | loop fusion | flops 278528 | bytes 1114112 | tf_op jit(solution)/shard_map/stack | solution.py:285
  15.7 3.0 %collective-permute-start.1 = (bf16[2,136,1024]{2,1,0:T(8,128)(2,1)}, bf16[2,136,1024]{2,1,0:T(8,128)(2,1)}, u32[]{:S(2)}, u32[]{:S(2)}) collective-permute-start(bf16[2,136,1024]{2,1,0:T(8,128)(2,1)} %pad_maximum_fusion.refs_0_.refs_3_), channel_id=1, source_target_pairs={{0,96},{1,13},{2,98},{3,15},{4,100},{5,1},{6,102},{7,3},{8,104},{9... | collective-permute-start | bytes 1671176 | tf_op jit(solution)/shard_map/ppermute | solution.py:62
  18.7 3.6 %collective-permute-start.3 = (bf16[2,136,1024]{2,1,0:T(8,128)(2,1)}, bf16[2,136,1024]{2,1,0:T(8,128)(2,1)}, u32[]{:S(2)}, u32[]{:S(2)}) collective-permute-start(bf16[2,136,1024]{2,1,0:T(8,128)(2,1)} %pad_maximum_fusion.refs_0_.refs_3_), channel_id=1, source_target_pairs={{0,64},{1,9},{2,66},{3,11},{4,68},{5,13},{6,70},{7,15},{8,72},{9,1... | collective-permute-start | bytes 1671176 | tf_op jit(solution)/shard_map/ppermute | solution.py:62
  23.8 3.0 %collective-permute-done.5.kv2_ref = bf16[2048,256]{1,0:T(8,128)(2,1)S(1)} collective-permute-done((bf16[2048,256]{1,0:T(8,128)(2,1)S(1)}, bf16[2048,256]{1,0:T(8,128)(2,1)S(1)}, u32[]{:S(2)}, u32[]{:S(2)}) %collective-permute-start.5) | collective-permute-done | bytes 1048608 | tf_op jit(solution)/shard_map/ppermute | solution.py:62
  29.0 4.1 %early.2 = (f32[2,2,128,512]{3,2,1,0:T(8,128)S(1)}, f32[2,2,8,512]{3,2,1,0:T(8,128)S(1)}, f32[8,128]{1,0:T(8,128)S(1)}) custom-call(s32[1,2,2,4,2]{4,3,2,1,0:T(4,128)S(1)} %add_clamp_fusion.1.tab_ref, f32[8,128]{1,0:T(8,128)S(1)} %broadcast_in_dim.42.turn_ref, bf16[2048,256]{1,0:T(8,128)(2,1)S(1)} %get-tuple-element.36.kv0_ref, ...), custom_call_target="tpu_custom_call" | custom-call | bytes 1024 | tf_op jit(solution)/shard_map/early/pallas_call | solution.py:306
  34.2 1.6 %collective-permute-done.2.refs_1_.refs_0_ = bf16[2,136,1024]{2,1,0:T(8,128)(2,1)} collective-permute-done((bf16[2,136,1024]{2,1,0:T(8,128)(2,1)}, bf16[2,136,1024]{2,1,0:T(8,128)(2,1)}, u32[]{:S(2)}, u32[]{:S(2)}) %collective-permute-start.2) | collective-permute-done | bytes 557088 | tf_op jit(solution)/shard_map/ppermute | solution.py:62
  38.0 5.5 %collective-permute-start.7 = (bf16[1024,256]{1,0:T(8,128)(2,1)}, bf16[1024,256]{1,0:T(8,128)(2,1)S(1)}, u32[]{:S(2)}, u32[]{:S(2)}) collective-permute-start(bf16[1024,256]{1,0:T(8,128)(2,1)} %slice.45), channel_id=1, source_target_pairs={{0,12},{1,97},{2,14},{3,99},{4,0},{5,101},{6,2},{7,103},{8,4},{9,1... | collective-permute-start | bytes 1572872 | tf_op jit(solution)/shard_map/ppermute | solution.py:62
  43.6 10.7 %early.3 = (f32[2,2,128,512]{3,2,1,0:T(8,128)S(1)}, f32[2,2,8,512]{3,2,1,0:T(8,128)S(1)}, f32[2,2,128,512]{3,2,1,0:T(8,128)S(1)}, f32[2,2,8,512]{3,2,1,0:T(8,128...) custom-call(s32[3,2,2,4,2]{4,3,2,1,0:T(4,128)S(1)} %add_clamp_fusion.tab_ref, ...), custom_call_target="tpu_custom_call" | custom-call | bytes 1024 | tf_op jit(solution)/shard_map/early/pallas_call | solution.py:306
  54.4 5.2 %late.2 = (bf16[2,2,136,512]{3,2,1,0:T(8,128)(2,1)}, bf16[2,2,136,512]{3,2,1,0:T(8,128)(2,1)}) custom-call(s32[2,2,2,4,2]{4,3,2,1,0:T(4,128)S(1)} %pad_add_fusion.tab_ref, bf16[1024,256]{1,0:T(8,128)(2,1)S(1)} %collective-permute-done.7.k3_ref, bf16[1024,256]{1,0:T(8,128)(2,1)S(1)} %collective-permute-done.8.v3_ref, ...), custom_call_target="tpu_custom_call" | custom-call | flops 2147483648 | bytes 12582912 | tf_op jit(solution)/shard_map/late/pallas_call | solution.py:324
  60.5 4.6 %late.3 = (bf16[2,2,136,512]{3,2,1,0:T(8,128)(2,1)}, bf16[2,2,136,512]{3,2,1,0:T(8,128)(2,1)S(1)}) custom-call(s32[2,2,2,4,2]{4,3,2,1,0:T(4,128)S(1)} %pad_add_fusion.1.tab_ref, bf16[1024,256]{1,0:T(8,128)(2,1)S(1)} %collective-permute-done.7.k3_ref, bf16[1024,256]{1,0:T(8,128)(2,1)S(1)} %collective-permute-done.8.v3_ref, ...), custom_call_target="tpu_custom_call" | custom-call | flops 2147483648 | bytes 12582912 | tf_op jit(solution)/shard_map/late/pallas_call | solution.py:324
  65.1 2.7 %collective-permute-start.11 = (bf16[2,2,136,512]{3,2,1,0:T(8,128)(2,1)}, bf16[2,2,136,512]{3,2,1,0:T(8,128)(2,1)S(1)}, u32[]{:S(2)}, u32[]{:S(2)}) collective-permute-start(bf16[2,2,136,512]{3,2,1,0:T(8,128)(2,1)} %get-tuple-element.55), channel_id=1, source_target_pairs={{0,96},{1,13},{2,98},{3,15},{4,100},{5,1},{6,102},{7,3},{8,104},{9... | collective-permute-start | bytes 1671176 | tf_op jit(solution)/shard_map/ppermute | solution.py:62
  67.8 3.2 %collective-permute-done.9.a_ref.refs_0_ = bf16[2,2,136,512]{3,2,1,0:T(8,128)(2,1)S(1)} collective-permute-done((bf16[2,2,136,512]{3,2,1,0:T(8,128)(2,1)}, bf16[2,2,136,512]{3,2,1,0:T(8,128)(2,1)S(1)}, u32[]{:S(2)}, u32[]{:S(2)}) %collective-permute-start.9) | collective-permute-done | bytes 557088 | tf_op jit(solution)/shard_map/ppermute | solution.py:62
  71.0 5.9 %collective-permute-done.10.b_ref.refs_1_ = bf16[2,2,136,512]{3,2,1,0:T(8,128)(2,1)S(1)} collective-permute-done((bf16[2,2,136,512]{3,2,1,0:T(8,128)(2,1)}, bf16[2,2,136,512]{3,2,1,0:T(8,128)(2,1)S(1)}, u32[]{:S(2)}, u32[]{:S(2)}) %collective-permute-start.10) | collective-permute-done | bytes 557088 | tf_op jit(solution)/shard_map/ppermute | solution.py:62
  78.3 3.4 %home.1 = (f32[2,128,512]{2,1,0:T(8,128)S(1)}, f32[2,8,512]{2,1,0:T(8,128)S(1)}, bf16[1024,4096]{1,0:T(8,128)(2,1)S(1)}) custom-call(bf16[2,2,136,512]{3,2,1,0:T(8,128)(2,1)S(1)} %collective-permute-done.9.a_ref.refs_0_, bf16[2,2,136,512]{3,2,1,0:T(8,128)(2,1)S(1)} %collective-permute-done.10.b_ref.refs_1_, ...), custom_call_target="tpu_custom_call" | custom-call | flops 2147483648 | bytes 12582912 | tf_op jit(solution)/shard_map/home/pallas_call | solution.py:338
  81.7 3.6 %collective-permute-done.12.e_ref = bf16[2,136,512]{2,1,0:T(8,128)(2,1)S(1)} collective-permute-done((bf16[2,136,512]{2,1,0:T(8,128)(2,1)S(1)}, bf16[2,136,512]{2,1,0:T(8,128)(2,1)S(1)}, u32[]{:S(2)}, u32[]{:S(2)}) %collective-permute-start.12) | collective-permute-done | bytes 278560 | tf_op jit(solution)/shard_map/ppermute | solution.py:62
  85.3 2.0 %last.1 = (bf16[2,32,4096]{2,1,0:T(8,128)(2,1)S(1)}, f32[2,32,4096]{2,1,0:T(8,128)S(1)}) custom-call(s32[2]{0:T(128)S(1)} %pad_add_fusion.2.place_ref, f32[2,128,512]{2,1,0:T(8,128)S(1)} %get-tuple-element.60.m_ref, f32[2,8,512]{2,1,0:T(8,128)S(1)} %get-tuple-element.61.v_ref, bf16[2,136,512]{2,1,0:T(8,128)(2,1)S(1)} %collective-permute-done.12.e_ref, ...), custom_call_target="tpu_custom_call" | custom-call | tf_op jit(solution)/shard_map/last/pallas_call | solution.py:354
  87.3 1.9 %collective-permute-done.13 = bf16[2,32,4096]{2,1,0:T(8,128)(2,1)S(1)} collective-permute-done((bf16[2,32,4096]{2,1,0:T(8,128)(2,1)S(1)}, bf16[2,32,4096]{2,1,0:T(8,128)(2,1)S(1)}, u32[]{:S(2)}, u32[]{:S(2)}) %collective-permute-start.13) | collective-permute-done | bytes 524320 | tf_op jit(solution)/shard_map/ppermute | solution.py:62
  89.4 1.4 %collective-permute-start.14 = (bf16[32,4096]{1,0:T(8,128)(2,1)S(1)}, bf16[32,4096]{1,0:T(8,128)(2,1)S(1)}, u32[]{:S(2)}, u32[]{:S(2)}) collective-permute-start(bf16[32,4096]{1,0:T(8,128)(2,1)S(1)} %fusion.2), channel_id=1, source_target_pairs={{0,2},{1,3},{2,0},{3,1},{4,6},{5,7},{6,4},{7,5},{8,10},{9,11},{10,... | collective-permute-start | bytes 786440 | tf_op jit(solution)/shard_map/ppermute | solution.py:62
  90.7 7.1 %collective-permute-done.14 = bf16[32,4096]{1,0:T(8,128)(2,1)S(1)} collective-permute-done((bf16[32,4096]{1,0:T(8,128)(2,1)S(1)}, bf16[32,4096]{1,0:T(8,128)(2,1)S(1)}, u32[]{:S(2)}, u32[]{:S(2)}) %collective-permute-start.14) | collective-permute-done | bytes 262176 | tf_op jit(solution)/shard_map/ppermute | solution.py:62
  (50 shorter events, 10.6 us)
Async XLA Ops:
  1.4 17.3 %collective-permute-start.4 = (bf16[2048,256]{1,0:T(8,128)(2,1)S(1)}, bf16[2048,256]{1,0:T(8,128)(2,1)S(1)}, u32[]{:S(2)}, u32[]{:S(2)}) collective-permute-start(bf16[2048,256]{1,0:T(8,128)(2,1)S(1)} %get-tuple-element.36.kv0_ref), channel_id=1, source_target_pairs={{0,12},{1,97},{2,14},{3,99},{4,0},{5,101},{6,2},{7,103},{8,4},{9,1... | collective-permute-start | bytes 3145736 | tf_op jit(solution)/shard_map/ppermute | solution.py:62
  5.5 21.4 %collective-permute-start.5 = (bf16[2048,256]{1,0:T(8,128)(2,1)S(1)}, bf16[2048,256]{1,0:T(8,128)(2,1)S(1)}, u32[]{:S(2)}, u32[]{:S(2)}) collective-permute-start(bf16[2048,256]{1,0:T(8,128)(2,1)S(1)} %get-tuple-element.36.kv0_ref), channel_id=1, source_target_pairs={{0,4},{1,33},{2,6},{3,35},{4,8},{5,37},{6,10},{7,39},{8,12},{9,41}... | collective-permute-start | bytes 3145736 | tf_op jit(solution)/shard_map/ppermute | solution.py:62
  5.5 8.4 %collective-permute-start = (bf16[136,1024]{1,0:T(8,128)(2,1)S(1)}, bf16[136,1024]{1,0:T(8,128)(2,1)}, u32[]{:S(2)}, u32[]{:S(2)}) collective-permute-start(bf16[136,1024]{1,0:T(8,128)(2,1)S(1)} %get-tuple-element.35), channel_id=1, source_target_pairs={{0,16},{1,17},{2,18},{3,19},{4,20},{5,21},{6,22},{7,23},{8,24},{9,... | collective-permute-start | bytes 835592 | tf_op jit(solution)/shard_map/ppermute | solution.py:62
  7.4 20.3 %collective-permute-start.6 = (bf16[128,512]{1,0:T(8,128)(2,1)}, bf16[128,512]{1,0:T(8,128)(2,1)S(1)}, u32[]{:S(2)}, u32[]{:S(2)}) collective-permute-start(bf16[128,512]{1,0:T(8,128)(2,1)} %pad_maximum_fusion.1), channel_id=1, source_target_pairs={{0,4},{1,5},{2,6},{3,7},{4,8},{5,9},{6,10},{7,11},{8,12},{9,13},{1... | collective-permute-start | bytes 393224 | tf_op jit(solution)/shard_map/ppermute | solution.py:62
  15.7 18.4 %collective-permute-start.1 = (bf16[2,136,1024]{2,1,0:T(8,128)(2,1)}, bf16[2,136,1024]{2,1,0:T(8,128)(2,1)}, u32[]{:S(2)}, u32[]{:S(2)}) collective-permute-start(bf16[2,136,1024]{2,1,0:T(8,128)(2,1)} %pad_maximum_fusion.refs_0_.refs_3_), channel_id=1, source_target_pairs={{0,96},{1,13},{2,98},{3,15},{4,100},{5,1},{6,102},{7,3},{8,104},{9... | collective-permute-start | bytes 1671176 | tf_op jit(solution)/shard_map/ppermute | solution.py:62
  18.7 17.0 %collective-permute-start.2 = (bf16[2,136,1024]{2,1,0:T(8,128)(2,1)}, bf16[2,136,1024]{2,1,0:T(8,128)(2,1)}, u32[]{:S(2)}, u32[]{:S(2)}) collective-permute-start(bf16[2,136,1024]{2,1,0:T(8,128)(2,1)} %pad_maximum_fusion.refs_0_.refs_3_), channel_id=1, source_target_pairs={{0,32},{1,5},{2,34},{3,7},{4,36},{5,9},{6,38},{7,11},{8,40},{9,13}... | collective-permute-start | bytes 1671176 | tf_op jit(solution)/shard_map/ppermute | solution.py:62
  18.7 17.0 %collective-permute-start.3 = (bf16[2,136,1024]{2,1,0:T(8,128)(2,1)}, bf16[2,136,1024]{2,1,0:T(8,128)(2,1)}, u32[]{:S(2)}, u32[]{:S(2)}) collective-permute-start(bf16[2,136,1024]{2,1,0:T(8,128)(2,1)} %pad_maximum_fusion.refs_0_.refs_3_), channel_id=1, source_target_pairs={{0,64},{1,9},{2,66},{3,11},{4,68},{5,13},{6,70},{7,15},{8,72},{9,1... | collective-permute-start | bytes 1671176 | tf_op jit(solution)/shard_map/ppermute | solution.py:62
  33.1 1.0 %copy-start.3 = (f32[2,2,128,512]{3,2,1,0:T(8,128)}, f32[2,2,128,512]{3,2,1,0:T(8,128)S(1)}, u32[]{:S(2)}) copy-start(f32[2,2,128,512]{3,2,1,0:T(8,128)S(1)} %get-tuple-element.53.refs_4_) | copy-start | bytes 3145732
  38.0 22.5 %copy-start.4 = (f32[2,2,128,512]{3,2,1,0:T(8,128)S(1)}, f32[2,2,128,512]{3,2,1,0:T(8,128)}, u32[]{:S(2)}) copy-start(f32[2,2,128,512]{3,2,1,0:T(8,128)} %copy-done.3) | copy-start | bytes 3145732
  38.0 16.4 %collective-permute-start.7 = (bf16[1024,256]{1,0:T(8,128)(2,1)}, bf16[1024,256]{1,0:T(8,128)(2,1)S(1)}, u32[]{:S(2)}, u32[]{:S(2)}) collective-permute-start(bf16[1024,256]{1,0:T(8,128)(2,1)} %slice.45), channel_id=1, source_target_pairs={{0,12},{1,97},{2,14},{3,99},{4,0},{5,101},{6,2},{7,103},{8,4},{9,1... | collective-permute-start | bytes 1572872 | tf_op jit(solution)/shard_map/ppermute | solution.py:62
  43.5 10.9 %collective-permute-start.8 = (bf16[1024,256]{1,0:T(8,128)(2,1)}, bf16[1024,256]{1,0:T(8,128)(2,1)S(1)}, u32[]{:S(2)}, u32[]{:S(2)}) collective-permute-start(bf16[1024,256]{1,0:T(8,128)(2,1)} %slice.46), channel_id=1, source_target_pairs={{0,4},{1,33},{2,6},{3,35},{4,8},{5,37},{6,10},{7,39},{8,12},{9,41}... | collective-permute-start | bytes 1572872 | tf_op jit(solution)/shard_map/ppermute | solution.py:62
  54.4 22.9 %copy-start = (bf16[128,1024]{1,0:T(8,128)(2,1)S(1)}, bf16[128,1024]{1,0:T(8,128)(2,1)}, u32[]{:S(2)}) copy-start(bf16[128,1024]{1,0:T(8,128)(2,1)} %q_ref.3) | copy-start | bytes 786436
  54.4 22.9 %copy-start.1 = (bf16[128,256]{1,0:T(8,128)(2,1)S(1)}, bf16[128,256]{1,0:T(8,128)(2,1)}, u32[]{:S(2)}) copy-start(bf16[128,256]{1,0:T(8,128)(2,1)} %k_ref.3) | copy-start | bytes 196612
  54.4 22.9 %copy-start.2 = (bf16[128,256]{1,0:T(8,128)(2,1)S(1)}, bf16[128,256]{1,0:T(8,128)(2,1)}, u32[]{:S(2)}) copy-start(bf16[128,256]{1,0:T(8,128)(2,1)} %v_ref.3) | copy-start | bytes 196612
  59.6 11.4 %collective-permute-start.9 = (bf16[2,2,136,512]{3,2,1,0:T(8,128)(2,1)}, bf16[2,2,136,512]{3,2,1,0:T(8,128)(2,1)S(1)}, u32[]{:S(2)}, u32[]{:S(2)}) collective-permute-start(bf16[2,2,136,512]{3,2,1,0:T(8,128)(2,1)} %get-tuple-element.49), channel_id=1, source_target_pairs={{0,64},{1,9},{2,66},{3,11},{4,68},{5,13},{6,70},{7,15},{8,72},{9,1... | collective-permute-start | bytes 1671176 | tf_op jit(solution)/shard_map/ppermute | solution.py:62
  60.0 16.9 %collective-permute-start.10 = (bf16[2,2,136,512]{3,2,1,0:T(8,128)(2,1)}, bf16[2,2,136,512]{3,2,1,0:T(8,128)(2,1)S(1)}, u32[]{:S(2)}, u32[]{:S(2)}) collective-permute-start(bf16[2,2,136,512]{3,2,1,0:T(8,128)(2,1)} %get-tuple-element.50), channel_id=1, source_target_pairs={{0,32},{1,5},{2,34},{3,7},{4,36},{5,9},{6,38},{7,11},{8,40},{9,13}... | collective-permute-start | bytes 1671176 | tf_op jit(solution)/shard_map/ppermute | solution.py:62
  65.1 11.8 %collective-permute-start.11 = (bf16[2,2,136,512]{3,2,1,0:T(8,128)(2,1)}, bf16[2,2,136,512]{3,2,1,0:T(8,128)(2,1)S(1)}, u32[]{:S(2)}, u32[]{:S(2)}) collective-permute-start(bf16[2,2,136,512]{3,2,1,0:T(8,128)(2,1)} %get-tuple-element.55), channel_id=1, source_target_pairs={{0,96},{1,13},{2,98},{3,15},{4,100},{5,1},{6,102},{7,3},{8,104},{9... | collective-permute-start | bytes 1671176 | tf_op jit(solution)/shard_map/ppermute | solution.py:62
  77.1 8.1 %collective-permute-start.12 = (bf16[2,136,512]{2,1,0:T(8,128)(2,1)S(1)}, bf16[2,136,512]{2,1,0:T(8,128)(2,1)S(1)}, u32[]{:S(2)}, u32[]{:S(2)}) collective-permute-start(bf16[2,136,512]{2,1,0:T(8,128)(2,1)S(1)} %join.1), channel_id=1, source_target_pairs={{0,16},{1,17},{2,18},{3,19},{4,20},{5,21},{6,22},{7,23},{8,24},{9,... | collective-permute-start | bytes 835592 | tf_op jit(solution)/shard_map/ppermute | solution.py:62
  87.3 2.0 %collective-permute-start.13 = (bf16[2,32,4096]{2,1,0:T(8,128)(2,1)S(1)}, bf16[2,32,4096]{2,1,0:T(8,128)(2,1)S(1)}, u32[]{:S(2)}, u32[]{:S(2)}) collective-permute-start(bf16[2,32,4096]{2,1,0:T(8,128)(2,1)S(1)} %get-tuple-element.64), channel_id=1, source_target_pairs={{0,1},{1,0},{2,3},{3,2},{4,5},{5,4},{6,7},{7,6},{8,9},{9,8},{10,11... | collective-permute-start | bytes 1572872 | tf_op jit(solution)/shard_map/ppermute | solution.py:62
  89.4 8.4 %collective-permute-start.14 = (bf16[32,4096]{1,0:T(8,128)(2,1)S(1)}, bf16[32,4096]{1,0:T(8,128)(2,1)S(1)}, u32[]{:S(2)}, u32[]{:S(2)}) collective-permute-start(bf16[32,4096]{1,0:T(8,128)(2,1)S(1)} %fusion.2), channel_id=1, source_target_pairs={{0,2},{1,3},{2,0},{3,1},{4,6},{5,7},{6,4},{7,5},{8,10},{9,11},{10,... | collective-permute-start | bytes 786440 | tf_op jit(solution)/shard_map/ppermute | solution.py:62

commit v6 on v5

--- a/solution.py
+++ b/solution.py
@@ -82,13 +82,15 @@
     return jnp.concatenate([hi.astype(F32), mid.astype(F32), low.astype(F32), jnp.zeros((5, COLS), F32)], axis=0).astype(BF)
 
 
-def pack_kernel(list_ref, q_ref, k_ref, v_ref, asked_ref, kv_ref, v_buf, list_buf, sems):
+def pack_kernel(list_ref, q_ref, k_ref, v_ref, kn_ref, vn_ref, asked_ref, kv_ref, rows_ref, v_buf, list_buf, sems):
     rows = k_ref.shape[0]
     copies = [
         pltpu.make_async_copy(q_ref, asked_ref.at[0:BLOCK], sems.at[0]),
         pltpu.make_async_copy(v_ref, v_buf, sems.at[1]),
         pltpu.make_async_copy(k_ref, kv_ref.at[0:rows], sems.at[2]),
         pltpu.make_async_copy(list_ref, list_buf, sems.at[3]),
+        pltpu.make_async_copy(kn_ref, rows_ref.at[:, 0 : KVL * HD], sems.at[4]),
+        pltpu.make_async_copy(vn_ref, rows_ref.at[:, KVL * HD : 2 * KVL * HD], sems.at[5]),
     ]
     for copy in copies:
         copy.start()
@@ -103,6 +105,8 @@
             kv_ref[rows + b * BLOCK : rows + (b + 1) * BLOCK, cols] = turned(v_buf[b * BLOCK : (b + 1) * BLOCK, cols])
     copies[0].wait()
     copies[2].wait()
+    copies[4].wait()
+    copies[5].wait()
 
 
 def query_rows(q):
@@ -271,22 +275,26 @@
     sel = block_list.shape[2]
 
     rows = cache_keys.shape[0]
-    asked, kv = call(
+    asked, kv, stretch_rows = call(
         pack_kernel,
-        (shape((queries.shape[0] + 8, queries.shape[1]), BF), shape((2 * rows, cache_keys.shape[1]), BF)),
-        hbm=4,
+        (
+            shape((queries.shape[0] + 8, queries.shape[1]), BF),
+            shape((2 * rows, cache_keys.shape[1]), BF),
+            shape((BLOCK, 2 * KVL * HD), BF),
+        ),
+        hbm=6,
         name="pack",
         scratch=[
             pltpu.VMEM(cache_values.shape, BF),
             pltpu.VMEM(block_list.shape, jnp.int32),
-            pltpu.SemaphoreType.DMA((4,)),
+            pltpu.SemaphoreType.DMA((6,)),
         ],
-    )(*(pltpu.with_memory_space_constraint(a, pltpu.HBM) for a in (block_list, queries, cache_keys, cache_values)))
+    )(*(pltpu.with_memory_space_constraint(a, pltpu.HBM) for a in (block_list, queries, cache_keys, cache_values, keys_new, values_new)))
     asked_pair = jnp.stack([asked, send(asked, PAIRS_Y)])
     after, before = send(kv, pairs_along(-1, True)), send(kv, pairs_along(1, True))
     asked_all = [asked_pair] + [send(asked_pair, pairs_along(-d, False)) for d in STEPS]
     half_keys, half_values = after[:rows], before[rows:]
-    prev = send(jnp.concatenate([keys_new, values_new], axis=1), PAIRS_PREV)
+    prev = send(stretch_rows, PAIRS_PREV)
     asked_pair, half_keys, half_values, prev = lax.optimization_barrier((asked_pair, half_keys, half_values, prev))
     far_keys = send(half_keys, pairs_along(-1, True))
     far_values = send(half_values, pairs_along(1, True))

time: 99 us -> 99.7 us (level)
  other arithmetic: 6.71 us -> 5.18 us
  waiting for transfers between devices: 30.9 us -> 32.4 us
    concatenate x1 -> x0, other arithmetic: 1.53 us -> none  [shards(): prev = send(jnp.concatenate([keys_new, values_new], axis=1), PAIRS_PREV)]
    ppermute x15, waiting for transfers between devices: 30.9 us -> 32.4 us  [send(): return lax.ppermute(array, AXES, pairs)]
  transfers between devices with their start and end apart: 15 -> 15, of which waited for: 8 -> 8; matrix products, arithmetic and copies ran while one was open for 7% -> 6% of each run, Pallas kernels for 24% -> 24%
where the time goes in v6:
time: 99.7 us; the launch traced here: 99.2 us
  Pallas kernels  33.3 us (33%)
  waiting for transfers between devices  32.4 us (32%)
  starting transfers between devices  23.5 us (24%)
  other arithmetic  5.18 us (5%)
  local copies, waits for them, and re-layouts  4.64 us (5%)
    ppermute x15, waiting for transfers between devices, send(): return lax.ppermute(array, AXES, pairs)  32.4 us
    ppermute x15, starting transfers between devices, send(): return lax.ppermute(array, AXES, pairs)  23.5 us
    pallas_call x2, Pallas kernels, begin(): call(functools.partial(early_kernel, n), (shape((NY, KVL, HD, COLS), F32)...  14.9 us
    pallas_call x2, Pallas kernels, shards(): call(functools.partial(late_kernel, len(group)), (shape((NY, KVL, ROWS, C...  9.78 us
    pallas_call x1, Pallas kernels, shards(): call(home_kernel, (shape((KVL, HD, COLS), F32), shape((KVL, 8, COLS), F32...  3.39 us
    pallas_call x1, Pallas kernels, shards(): call(pack_kernel, (shape((queries.shape[0] + 8, queries.shape[1]), BF), s...  2.04 us
  transfers between devices with their start and end apart: 15, of which 8 were waited for; matrix products, arithmetic and copies ran while one was open for 6% of the time, Pallas kernels for 24%

profile of v6, /device:TPU:16, one launch (start us, length us, event | category | flops | bytes accessed | tf_op | source)
XLA Modules:
  0.0 99.2 jit_solution(13174700654139486685)
XLA Ops:
  0.0 2.0 %pack.1 = (bf16[136,1024]{1,0:T(8,128)(2,1)S(1)}, bf16[2048,256]{1,0:T(8,128)(2,1)S(1)}, bf16[128,512]{1,0:T(8,128)(2,1)}) custom-call(s32[2,1,64]{2,1,0:T(1,128)} %list_ref.1, bf16[128,1024]{1,0:T(8,128)(2,1)} %q_ref.3, bf16[1024,256]{1,0:T(8,128)(2,1)} %k_ref.2, bf16[1024,256]{1,0:T(8,128)(2,1)} %v_ref.2, bf16[128,256]{1,0:T(8,128)(2,1)} %k_ref.3, ...), custom_call_target="tpu_custom_call" | custom-call | tf_op jit(solution)/shard_map/pack/pallas_call | solution.py:278
  2.0 4.1 %collective-permute-start.4 = (bf16[2048,256]{1,0:T(8,128)(2,1)S(1)}, bf16[2048,256]{1,0:T(8,128)(2,1)S(1)}, u32[]{:S(2)}, u32[]{:S(2)}) collective-permute-start(bf16[2048,256]{1,0:T(8,128)(2,1)S(1)} %get-tuple-element.37.kv0_ref), channel_id=1, source_target_pairs={{0,12},{1,97},{2,14},{3,99},{4,0},{5,101},{6,2},{7,103},{8,4},{9,1... | collective-permute-start | bytes 3145736 | tf_op jit(solution)/shard_map/ppermute | solution.py:62
  6.5 1.9 %collective-permute-start.6 = (bf16[128,512]{1,0:T(8,128)(2,1)}, bf16[128,512]{1,0:T(8,128)(2,1)S(1)}, u32[]{:S(2)}, u32[]{:S(2)}) collective-permute-start(bf16[128,512]{1,0:T(8,128)(2,1)} %get-tuple-element.38), channel_id=1, source_target_pairs={{0,4},{1,5},{2,6},{3,7},{4,8},{5,9},{6,10},{7,11},{8,12},{9,13},{1... | collective-permute-start | bytes 393224 | tf_op jit(solution)/shard_map/ppermute | solution.py:62
  8.4 6.2 %collective-permute-done = bf16[136,1024]{1,0:T(8,128)(2,1)} collective-permute-done((bf16[136,1024]{1,0:T(8,128)(2,1)S(1)}, bf16[136,1024]{1,0:T(8,128)(2,1)}, u32[]{:S(2)}, u32[]{:S(2)}) %collective-permute-start) | collective-permute-done | bytes 278560 | tf_op jit(solution)/shard_map/ppermute | solution.py:62
  14.6 1.8 %pad_maximum_fusion.refs_0_.refs_3_ = bf16[2,136,1024]{2,1,0:T(8,128)(2,1)} fusion(bf16[1,136,1024]{2,1,0:T(8,128)(2,1)} %bitcast.3, bf16[1,136,1024]{2,1,0:T(8,128)(2,1)S(1)} %bitcast.23), kind=kLoop, calls=%fused_computation.1 | loop fusion | flops 278528 | bytes 1114112 | tf_op jit(solution)/shard_map/stack | solution.py:293
  16.4 3.0 %collective-permute-start.1 = (bf16[2,136,1024]{2,1,0:T(8,128)(2,1)}, bf16[2,136,1024]{2,1,0:T(8,128)(2,1)}, u32[]{:S(2)}, u32[]{:S(2)}) collective-permute-start(bf16[2,136,1024]{2,1,0:T(8,128)(2,1)} %pad_maximum_fusion.refs_0_.refs_3_), channel_id=1, source_target_pairs={{0,96},{1,13},{2,98},{3,15},{4,100},{5,1},{6,102},{7,3},{8,104},{9... | collective-permute-start | bytes 1671176 | tf_op jit(solution)/shard_map/ppermute | solution.py:62
  19.4 3.6 %collective-permute-start.3 = (bf16[2,136,1024]{2,1,0:T(8,128)(2,1)}, bf16[2,136,1024]{2,1,0:T(8,128)(2,1)}, u32[]{:S(2)}, u32[]{:S(2)}) collective-permute-start(bf16[2,136,1024]{2,1,0:T(8,128)(2,1)} %pad_maximum_fusion.refs_0_.refs_3_), channel_id=1, source_target_pairs={{0,64},{1,9},{2,66},{3,11},{4,68},{5,13},{6,70},{7,15},{8,72},{9,1... | collective-permute-start | bytes 1671176 | tf_op jit(solution)/shard_map/ppermute | solution.py:62
  24.5 3.0 %collective-permute-done.5.kv2_ref = bf16[2048,256]{1,0:T(8,128)(2,1)S(1)} collective-permute-done((bf16[2048,256]{1,0:T(8,128)(2,1)S(1)}, bf16[2048,256]{1,0:T(8,128)(2,1)S(1)}, u32[]{:S(2)}, u32[]{:S(2)}) %collective-permute-start.5) | collective-permute-done | bytes 1048608 | tf_op jit(solution)/shard_map/ppermute | solution.py:62
  29.7 4.1 %early.2 = (f32[2,2,128,512]{3,2,1,0:T(8,128)S(1)}, f32[2,2,8,512]{3,2,1,0:T(8,128)S(1)}, f32[8,128]{1,0:T(8,128)S(1)}) custom-call(s32[1,2,2,4,2]{4,3,2,1,0:T(4,128)S(1)} %add_clamp_fusion.1.tab_ref, f32[8,128]{1,0:T(8,128)S(1)} %broadcast_in_dim.42.turn_ref, bf16[2048,256]{1,0:T(8,128)(2,1)S(1)} %get-tuple-element.37.kv0_ref, ...), custom_call_target="tpu_custom_call" | custom-call | bytes 1024 | tf_op jit(solution)/shard_map/early/pallas_call | solution.py:314
  33.8 1.0 copy-done.3
  34.8 1.6 %collective-permute-done.2.refs_1_.refs_0_ = bf16[2,136,1024]{2,1,0:T(8,128)(2,1)} collective-permute-done((bf16[2,136,1024]{2,1,0:T(8,128)(2,1)}, bf16[2,136,1024]{2,1,0:T(8,128)(2,1)}, u32[]{:S(2)}, u32[]{:S(2)}) %collective-permute-start.2) | collective-permute-done | bytes 557088 | tf_op jit(solution)/shard_map/ppermute | solution.py:62
  38.7 5.5 %collective-permute-start.7 = (bf16[1024,256]{1,0:T(8,128)(2,1)}, bf16[1024,256]{1,0:T(8,128)(2,1)S(1)}, u32[]{:S(2)}, u32[]{:S(2)}) collective-permute-start(bf16[1024,256]{1,0:T(8,128)(2,1)} %slice.45), channel_id=1, source_target_pairs={{0,12},{1,97},{2,14},{3,99},{4,0},{5,101},{6,2},{7,103},{8,4},{9,1... | collective-permute-start | bytes 1572872 | tf_op jit(solution)/shard_map/ppermute | solution.py:62
  44.3 10.7 %early.3 = (f32[2,2,128,512]{3,2,1,0:T(8,128)S(1)}, f32[2,2,8,512]{3,2,1,0:T(8,128)S(1)}, f32[2,2,128,512]{3,2,1,0:T(8,128)S(1)}, f32[2,2,8,512]{3,2,1,0:T(8,128...) custom-call(s32[3,2,2,4,2]{4,3,2,1,0:T(4,128)S(1)} %add_clamp_fusion.tab_ref, ...), custom_call_target="tpu_custom_call" | custom-call | bytes 1024 | tf_op jit(solution)/shard_map/early/pallas_call | solution.py:314
  55.1 5.2 %late.2 = (bf16[2,2,136,512]{3,2,1,0:T(8,128)(2,1)}, bf16[2,2,136,512]{3,2,1,0:T(8,128)(2,1)}) custom-call(s32[2,2,2,4,2]{4,3,2,1,0:T(4,128)S(1)} %pad_add_fusion.tab_ref, bf16[1024,256]{1,0:T(8,128)(2,1)S(1)} %collective-permute-done.7.k3_ref, bf16[1024,256]{1,0:T(8,128)(2,1)S(1)} %collective-permute-done.8.v3_ref, ...), custom_call_target="tpu_custom_call" | custom-call | flops 2147483648 | bytes 12582912 | tf_op jit(solution)/shard_map/late/pallas_call | solution.py:332
  61.2 4.6 %late.3 = (bf16[2,2,136,512]{3,2,1,0:T(8,128)(2,1)}, bf16[2,2,136,512]{3,2,1,0:T(8,128)(2,1)S(1)}) custom-call(s32[2,2,2,4,2]{4,3,2,1,0:T(4,128)S(1)} %pad_add_fusion.1.tab_ref, bf16[1024,256]{1,0:T(8,128)(2,1)S(1)} %collective-permute-done.7.k3_ref, bf16[1024,256]{1,0:T(8,128)(2,1)S(1)} %collective-permute-done.8.v3_ref, ...), custom_call_target="tpu_custom_call" | custom-call | flops 2147483648 | bytes 12582912 | tf_op jit(solution)/shard_map/late/pallas_call | solution.py:332
  65.8 2.7 %collective-permute-start.11 = (bf16[2,2,136,512]{3,2,1,0:T(8,128)(2,1)}, bf16[2,2,136,512]{3,2,1,0:T(8,128)(2,1)S(1)}, u32[]{:S(2)}, u32[]{:S(2)}) collective-permute-start(bf16[2,2,136,512]{3,2,1,0:T(8,128)(2,1)} %get-tuple-element.57), channel_id=1, source_target_pairs={{0,96},{1,13},{2,98},{3,15},{4,100},{5,1},{6,102},{7,3},{8,104},{9... | collective-permute-start | bytes 1671176 | tf_op jit(solution)/shard_map/ppermute | solution.py:62
  68.5 3.2 %collective-permute-done.9.a_ref.refs_0_ = bf16[2,2,136,512]{3,2,1,0:T(8,128)(2,1)S(1)} collective-permute-done((bf16[2,2,136,512]{3,2,1,0:T(8,128)(2,1)}, bf16[2,2,136,512]{3,2,1,0:T(8,128)(2,1)S(1)}, u32[]{:S(2)}, u32[]{:S(2)}) %collective-permute-start.9) | collective-permute-done | bytes 557088 | tf_op jit(solution)/shard_map/ppermute | solution.py:62
  71.7 5.9 %collective-permute-done.10.b_ref.refs_1_ = bf16[2,2,136,512]{3,2,1,0:T(8,128)(2,1)S(1)} collective-permute-done((bf16[2,2,136,512]{3,2,1,0:T(8,128)(2,1)}, bf16[2,2,136,512]{3,2,1,0:T(8,128)(2,1)S(1)}, u32[]{:S(2)}, u32[]{:S(2)}) %collective-permute-start.10) | collective-permute-done | bytes 557088 | tf_op jit(solution)/shard_map/ppermute | solution.py:62
  79.0 3.4 %home.1 = (f32[2,128,512]{2,1,0:T(8,128)S(1)}, f32[2,8,512]{2,1,0:T(8,128)S(1)}, bf16[1024,4096]{1,0:T(8,128)(2,1)S(1)}) custom-call(bf16[2,2,136,512]{3,2,1,0:T(8,128)(2,1)S(1)} %collective-permute-done.9.a_ref.refs_0_, bf16[2,2,136,512]{3,2,1,0:T(8,128)(2,1)S(1)} %collective-permute-done.10.b_ref.refs_1_, ...), custom_call_target="tpu_custom_call" | custom-call | flops 2147483648 | bytes 12582912 | tf_op jit(solution)/shard_map/home/pallas_call | solution.py:346
  82.4 3.6 %collective-permute-done.12.e_ref = bf16[2,136,512]{2,1,0:T(8,128)(2,1)S(1)} collective-permute-done((bf16[2,136,512]{2,1,0:T(8,128)(2,1)S(1)}, bf16[2,136,512]{2,1,0:T(8,128)(2,1)S(1)}, u32[]{:S(2)}, u32[]{:S(2)}) %collective-permute-start.12) | collective-permute-done | bytes 278560 | tf_op jit(solution)/shard_map/ppermute | solution.py:62
  85.9 2.0 %last.1 = (bf16[2,32,4096]{2,1,0:T(8,128)(2,1)S(1)}, f32[2,32,4096]{2,1,0:T(8,128)S(1)}) custom-call(s32[2]{0:T(128)S(1)} %pad_add_fusion.2.place_ref, f32[2,128,512]{2,1,0:T(8,128)S(1)} %get-tuple-element.62.m_ref, f32[2,8,512]{2,1,0:T(8,128)S(1)} %get-tuple-element.63.v_ref, bf16[2,136,512]{2,1,0:T(8,128)(2,1)S(1)} %collective-permute-done.12.e_ref, ...), custom_call_target="tpu_custom_call" | custom-call | tf_op jit(solution)/shard_map/last/pallas_call | solution.py:362
  88.0 1.9 %collective-permute-done.13 = bf16[2,32,4096]{2,1,0:T(8,128)(2,1)S(1)} collective-permute-done((bf16[2,32,4096]{2,1,0:T(8,128)(2,1)S(1)}, bf16[2,32,4096]{2,1,0:T(8,128)(2,1)S(1)}, u32[]{:S(2)}, u32[]{:S(2)}) %collective-permute-start.13) | collective-permute-done | bytes 524320 | tf_op jit(solution)/shard_map/ppermute | solution.py:62
  90.1 1.4 %collective-permute-start.14 = (bf16[32,4096]{1,0:T(8,128)(2,1)S(1)}, bf16[32,4096]{1,0:T(8,128)(2,1)S(1)}, u32[]{:S(2)}, u32[]{:S(2)}) collective-permute-start(bf16[32,4096]{1,0:T(8,128)(2,1)S(1)} %fusion.2), channel_id=1, source_target_pairs={{0,2},{1,3},{2,0},{3,1},{4,6},{5,7},{6,4},{7,5},{8,10},{9,11},{10,... | collective-permute-start | bytes 786440 | tf_op jit(solution)/shard_map/ppermute | solution.py:62
  91.4 7.1 %collective-permute-done.14 = bf16[32,4096]{1,0:T(8,128)(2,1)S(1)} collective-permute-done((bf16[32,4096]{1,0:T(8,128)(2,1)S(1)}, bf16[32,4096]{1,0:T(8,128)(2,1)S(1)}, u32[]{:S(2)}, u32[]{:S(2)}) %collective-permute-start.14) | collective-permute-done | bytes 262176 | tf_op jit(solution)/shard_map/ppermute | solution.py:62
  (49 shorter events, 9.6 us)
Async XLA Ops:
  2.0 17.3 %collective-permute-start.4 = (bf16[2048,256]{1,0:T(8,128)(2,1)S(1)}, bf16[2048,256]{1,0:T(8,128)(2,1)S(1)}, u32[]{:S(2)}, u32[]{:S(2)}) collective-permute-start(bf16[2048,256]{1,0:T(8,128)(2,1)S(1)} %get-tuple-element.37.kv0_ref), channel_id=1, source_target_pairs={{0,12},{1,97},{2,14},{3,99},{4,0},{5,101},{6,2},{7,103},{8,4},{9,1... | collective-permute-start | bytes 3145736 | tf_op jit(solution)/shard_map/ppermute | solution.py:62
  6.2 21.4 %collective-permute-start.5 = (bf16[2048,256]{1,0:T(8,128)(2,1)S(1)}, bf16[2048,256]{1,0:T(8,128)(2,1)S(1)}, u32[]{:S(2)}, u32[]{:S(2)}) collective-permute-start(bf16[2048,256]{1,0:T(8,128)(2,1)S(1)} %get-tuple-element.37.kv0_ref), channel_id=1, source_target_pairs={{0,4},{1,33},{2,6},{3,35},{4,8},{5,37},{6,10},{7,39},{8,12},{9,41}... | collective-permute-start | bytes 3145736 | tf_op jit(solution)/shard_map/ppermute | solution.py:62
  6.2 8.4 %collective-permute-start = (bf16[136,1024]{1,0:T(8,128)(2,1)S(1)}, bf16[136,1024]{1,0:T(8,128)(2,1)}, u32[]{:S(2)}, u32[]{:S(2)}) collective-permute-start(bf16[136,1024]{1,0:T(8,128)(2,1)S(1)} %get-tuple-element.36), channel_id=1, source_target_pairs={{0,16},{1,17},{2,18},{3,19},{4,20},{5,21},{6,22},{7,23},{8,24},{9,... | collective-permute-start | bytes 835592 | tf_op jit(solution)/shard_map/ppermute | solution.py:62
  6.5 21.9 %collective-permute-start.6 = (bf16[128,512]{1,0:T(8,128)(2,1)}, bf16[128,512]{1,0:T(8,128)(2,1)S(1)}, u32[]{:S(2)}, u32[]{:S(2)}) collective-permute-start(bf16[128,512]{1,0:T(8,128)(2,1)} %get-tuple-element.38), channel_id=1, source_target_pairs={{0,4},{1,5},{2,6},{3,7},{4,8},{5,9},{6,10},{7,11},{8,12},{9,13},{1... | collective-permute-start | bytes 393224 | tf_op jit(solution)/shard_map/ppermute | solution.py:62
  16.4 18.4 %collective-permute-start.1 = (bf16[2,136,1024]{2,1,0:T(8,128)(2,1)}, bf16[2,136,1024]{2,1,0:T(8,128)(2,1)}, u32[]{:S(2)}, u32[]{:S(2)}) collective-permute-start(bf16[2,136,1024]{2,1,0:T(8,128)(2,1)} %pad_maximum_fusion.refs_0_.refs_3_), channel_id=1, source_target_pairs={{0,96},{1,13},{2,98},{3,15},{4,100},{5,1},{6,102},{7,3},{8,104},{9... | collective-permute-start | bytes 1671176 | tf_op jit(solution)/shard_map/ppermute | solution.py:62
  19.4 17.0 %collective-permute-start.2 = (bf16[2,136,1024]{2,1,0:T(8,128)(2,1)}, bf16[2,136,1024]{2,1,0:T(8,128)(2,1)}, u32[]{:S(2)}, u32[]{:S(2)}) collective-permute-start(bf16[2,136,1024]{2,1,0:T(8,128)(2,1)} %pad_maximum_fusion.refs_0_.refs_3_), channel_id=1, source_target_pairs={{0,32},{1,5},{2,34},{3,7},{4,36},{5,9},{6,38},{7,11},{8,40},{9,13}... | collective-permute-start | bytes 1671176 | tf_op jit(solution)/shard_map/ppermute | solution.py:62
  19.4 17.0 %collective-permute-start.3 = (bf16[2,136,1024]{2,1,0:T(8,128)(2,1)}, bf16[2,136,1024]{2,1,0:T(8,128)(2,1)}, u32[]{:S(2)}, u32[]{:S(2)}) collective-permute-start(bf16[2,136,1024]{2,1,0:T(8,128)(2,1)} %pad_maximum_fusion.refs_0_.refs_3_), channel_id=1, source_target_pairs={{0,64},{1,9},{2,66},{3,11},{4,68},{5,13},{6,70},{7,15},{8,72},{9,1... | collective-permute-start | bytes 1671176 | tf_op jit(solution)/shard_map/ppermute | solution.py:62
  33.8 1.0 %copy-start.3 = (f32[2,2,128,512]{3,2,1,0:T(8,128)}, f32[2,2,128,512]{3,2,1,0:T(8,128)S(1)}, u32[]{:S(2)}) copy-start(f32[2,2,128,512]{3,2,1,0:T(8,128)S(1)} %get-tuple-element.55.refs_4_) | copy-start | bytes 3145732
  38.7 22.5 %copy-start.4 = (f32[2,2,128,512]{3,2,1,0:T(8,128)S(1)}, f32[2,2,128,512]{3,2,1,0:T(8,128)}, u32[]{:S(2)}) copy-start(f32[2,2,128,512]{3,2,1,0:T(8,128)} %copy-done.3) | copy-start | bytes 3145732
  38.7 16.4 %collective-permute-start.7 = (bf16[1024,256]{1,0:T(8,128)(2,1)}, bf16[1024,256]{1,0:T(8,128)(2,1)S(1)}, u32[]{:S(2)}, u32[]{:S(2)}) collective-permute-start(bf16[1024,256]{1,0:T(8,128)(2,1)} %slice.45), channel_id=1, source_target_pairs={{0,12},{1,97},{2,14},{3,99},{4,0},{5,101},{6,2},{7,103},{8,4},{9,1... | collective-permute-start | bytes 1572872 | tf_op jit(solution)/shard_map/ppermute | solution.py:62
  44.2 10.9 %collective-permute-start.8 = (bf16[1024,256]{1,0:T(8,128)(2,1)}, bf16[1024,256]{1,0:T(8,128)(2,1)S(1)}, u32[]{:S(2)}, u32[]{:S(2)}) collective-permute-start(bf16[1024,256]{1,0:T(8,128)(2,1)} %slice.46), channel_id=1, source_target_pairs={{0,4},{1,33},{2,6},{3,35},{4,8},{5,37},{6,10},{7,39},{8,12},{9,41}... | collective-permute-start | bytes 1572872 | tf_op jit(solution)/shard_map/ppermute | solution.py:62
  55.1 22.9 %copy-start = (bf16[128,1024]{1,0:T(8,128)(2,1)S(1)}, bf16[128,1024]{1,0:T(8,128)(2,1)}, u32[]{:S(2)}) copy-start(bf16[128,1024]{1,0:T(8,128)(2,1)} %q_ref.3) | copy-start | bytes 786436
  55.1 22.9 %copy-start.1 = (bf16[128,256]{1,0:T(8,128)(2,1)S(1)}, bf16[128,256]{1,0:T(8,128)(2,1)}, u32[]{:S(2)}) copy-start(bf16[128,256]{1,0:T(8,128)(2,1)} %k_ref.3) | copy-start | bytes 196612
  55.1 22.9 %copy-start.2 = (bf16[128,256]{1,0:T(8,128)(2,1)S(1)}, bf16[128,256]{1,0:T(8,128)(2,1)}, u32[]{:S(2)}) copy-start(bf16[128,256]{1,0:T(8,128)(2,1)} %v_ref.3) | copy-start | bytes 196612
  60.3 11.4 %collective-permute-start.9 = (bf16[2,2,136,512]{3,2,1,0:T(8,128)(2,1)}, bf16[2,2,136,512]{3,2,1,0:T(8,128)(2,1)S(1)}, u32[]{:S(2)}, u32[]{:S(2)}) collective-permute-start(bf16[2,2,136,512]{3,2,1,0:T(8,128)(2,1)} %get-tuple-element.51), channel_id=1, source_target_pairs={{0,64},{1,9},{2,66},{3,11},{4,68},{5,13},{6,70},{7,15},{8,72},{9,1... | collective-permute-start | bytes 1671176 | tf_op jit(solution)/shard_map/ppermute | solution.py:62
  60.6 16.9 %collective-permute-start.10 = (bf16[2,2,136,512]{3,2,1,0:T(8,128)(2,1)}, bf16[2,2,136,512]{3,2,1,0:T(8,128)(2,1)S(1)}, u32[]{:S(2)}, u32[]{:S(2)}) collective-permute-start(bf16[2,2,136,512]{3,2,1,0:T(8,128)(2,1)} %get-tuple-element.52), channel_id=1, source_target_pairs={{0,32},{1,5},{2,34},{3,7},{4,36},{5,9},{6,38},{7,11},{8,40},{9,13}... | collective-permute-start | bytes 1671176 | tf_op jit(solution)/shard_map/ppermute | solution.py:62
  65.8 11.8 %collective-permute-start.11 = (bf16[2,2,136,512]{3,2,1,0:T(8,128)(2,1)}, bf16[2,2,136,512]{3,2,1,0:T(8,128)(2,1)S(1)}, u32[]{:S(2)}, u32[]{:S(2)}) collective-permute-start(bf16[2,2,136,512]{3,2,1,0:T(8,128)(2,1)} %get-tuple-element.57), channel_id=1, source_target_pairs={{0,96},{1,13},{2,98},{3,15},{4,100},{5,1},{6,102},{7,3},{8,104},{9... | collective-permute-start | bytes 1671176 | tf_op jit(solution)/shard_map/ppermute | solution.py:62
  77.8 8.1 %collective-permute-start.12 = (bf16[2,136,512]{2,1,0:T(8,128)(2,1)S(1)}, bf16[2,136,512]{2,1,0:T(8,128)(2,1)S(1)}, u32[]{:S(2)}, u32[]{:S(2)}) collective-permute-start(bf16[2,136,512]{2,1,0:T(8,128)(2,1)S(1)} %join.1), channel_id=1, source_target_pairs={{0,16},{1,17},{2,18},{3,19},{4,20},{5,21},{6,22},{7,23},{8,24},{9,... | collective-permute-start | bytes 835592 | tf_op jit(solution)/shard_map/ppermute | solution.py:62
  87.9 2.0 %collective-permute-start.13 = (bf16[2,32,4096]{2,1,0:T(8,128)(2,1)S(1)}, bf16[2,32,4096]{2,1,0:T(8,128)(2,1)S(1)}, u32[]{:S(2)}, u32[]{:S(2)}) collective-permute-start(bf16[2,32,4096]{2,1,0:T(8,128)(2,1)S(1)} %get-tuple-element.66), channel_id=1, source_target_pairs={{0,1},{1,0},{2,3},{3,2},{4,5},{5,4},{6,7},{7,6},{8,9},{9,8},{10,11... | collective-permute-start | bytes 1572872 | tf_op jit(solution)/shard_map/ppermute | solution.py:62
  90.1 8.4 %collective-permute-start.14 = (bf16[32,4096]{1,0:T(8,128)(2,1)S(1)}, bf16[32,4096]{1,0:T(8,128)(2,1)S(1)}, u32[]{:S(2)}, u32[]{:S(2)}) collective-permute-start(bf16[32,4096]{1,0:T(8,128)(2,1)S(1)} %fusion.2), channel_id=1, source_target_pairs={{0,2},{1,3},{2,0},{3,1},{4,6},{5,7},{6,4},{7,5},{8,10},{9,11},{10,... | collective-permute-start | bytes 786440 | tf_op jit(solution)/shard_map/ppermute | solution.py:62
